TPU v7x, 32 devices: a whole 2x2x4 slice. The times are simulated.
32 devices in a mesh: dp: 16 (over z, y, x), tensor: 2 (over core).
Axes of the slice: x: 2, y: 2, z: 4, core: 2. Of those that a mesh axis runs over, the one named last changes fastest.
Arguments:
- block_input: bfloat16 [16384, 1024], P('dp'), may hold values from -6 to 6
- w_query: bfloat16 [1024, 1024], P(None, 'tensor'), may hold values from -0.1875 to 0.1875
- w_key: bfloat16 [1024, 1024], P(None, 'tensor'), may hold values from -0.1875 to 0.1875
- w_value: bfloat16 [1024, 1024], P(None, 'tensor'), may hold values from -0.1875 to 0.1875
- w_out: bfloat16 [1024, 1024], P('tensor'), may hold values from -0.375 to 0.375
- w_gate: bfloat16 [1024, 4096], P(None, 'tensor'), may hold values from -0.1875 to 0.1875
- w_up: bfloat16 [1024, 4096], P(None, 'tensor'), may hold values from -0.1875 to 0.1875
- w_down: bfloat16 [4096, 1024], P('tensor'), may hold values from -0.09375 to 0.09375
- gain_attn: bfloat16 [1024], replicated, may hold values from 0.25 to 1.75
- gain_ffn: bfloat16 [1024], replicated, may hold values from 0.25 to 1.75
- item_lengths: int32 [32], P('dp'), may hold values from 0 to 32, as said below
- cotangent: bfloat16 [16384, 1024], P('dp'), may hold values from -6 to 6
Outputs:
- block_output: bfloat16 [16384, 1024], P('dp')
- grad_input: bfloat16 [16384, 1024], P('dp')
- grad_query: float32 [1024, 1024], P('dp', 'tensor')
- grad_key: float32 [1024, 1024], P('dp', 'tensor')
- grad_value: float32 [1024, 1024], P('dp', 'tensor')
- grad_out: float32 [1024, 1024], P('tensor', 'dp')
- grad_gate: float32 [1024, 4096], P('dp', 'tensor')
- grad_up: float32 [1024, 4096], P('dp', 'tensor')
- grad_down: float32 [4096, 1024], P('tensor', 'dp')
- grad_gain_attn: float32 [1024], P('dp')
- grad_gain_ffn: float32 [1024], P('dp')
Inputs may be any that keep to these rules, and one draw needn't show every extreme that they name: `item_lengths`: frames used in each item slot of 32 frames: slot s of an index of dp holds its frames s * 32 to s * 32 + length - 1, the rest of the slot is padding; a length of 0 is an empty slot. Some slot is full in every draw.
All inputs are finite; a program needn't handle non-finite values.
Results may differ from a plain program's by a relative error of at most 0.02.
Values may be sent and summed in bfloat16 or wider, within the bound.
No kernel may reach another device: no remote copies, remote signals or barrier semaphores. Data moves between devices by JAX's collectives and lax.ppermute only.
A program may use at most 128 MiB of HBM per device.

v0:
```python
import functools
import math

import jax
import jax.numpy as jnp
from jax import lax
from jax.experimental import pallas as pl
from jax.experimental.pallas import tpu as pltpu
from jax.sharding import PartitionSpec as P

HD = 64
POS = 16
SLOT = 32
LANES = 128
TILE = 128
MIB = 1 << 20
HALVES = 2
PARTS = 2
COST = 1e-6

epsilon = 1e-05
f32 = jnp.float32
bf16 = jnp.bfloat16
SCALE = 1.0 / math.sqrt(HD)
ANYWHERE = jax.ShapeDtypeStruct


def nn(left, right):
    return lax.dot_general(left, right, (((1,), (0,)), ((), ())), preferred_element_type=f32)


def nt(left, right):
    return lax.dot_general(left, right, (((1,), (1,)), ((), ())), preferred_element_type=f32)


def tn(left, right):
    return lax.dot_general(left, right, (((0,), (0,)), ((), ())), preferred_element_type=f32)


def call(body, name, grid, ins, outs, scratch=(), vmem=40, scalars=0, aliases=None, cost=None, far=()):
    kernel = pl.pallas_call(
        body,
        grid_spec=pltpu.PrefetchScalarGridSpec(
            num_scalar_prefetch=scalars,
            grid=grid,
            in_specs=ins,
            out_specs=[spec for spec, *_ in outs],
            scratch_shapes=scratch,
        ),
        out_shape=[
            (where[0] if where else pltpu.HBM)(shape, dtype) for _, shape, dtype, *where in outs
        ],
        input_output_aliases=aliases or {},
        compiler_params=pltpu.CompilerParams(vmem_limit_bytes=vmem * MIB),
        cost_estimate=pl.CostEstimate(
            flops=int(cost[0] * COST), bytes_accessed=int(cost[1] * COST), transcendentals=0
        ),
        name=name,
    )

    def run(*args):
        return kernel(
            *(
                pltpu.with_memory_space_constraint(arg, pltpu.HBM) if n - scalars in far else arg
                for n, arg in enumerate(args)
            )
        )

    return run


def rows_of(block, width):
    return pl.BlockSpec((block, width), lambda i, *_: (i, 0))


def whole(*shape):
    return pl.BlockSpec(shape, lambda *_: (0,) * len(shape))


def row_of(gain_ref):
    return gain_ref[...].astype(f32).reshape(1, -1)


def inverse_rms(values):
    return lax.rsqrt(jnp.mean(values * values, axis=1, keepdims=True) + epsilon)


def exchanged(index, size):
    if size < 4:
        return index
    return index // 4 * 4 + index % 2 * 2 + index // 2 % 2


def relative(place_ref, g, size):
    apart = g ^ place_ref[0]
    if size < 4:
        return apart
    other = (apart & ~3) | ((apart & 1) << 1) | ((apart >> 1) & 1)
    return jnp.where(place_ref[1] == 1, other, apart)


def put_transposed(ref, place_ref, values):
    parts, depth, _ = ref.shape
    turned = values.T
    for g in range(parts):
        ref[relative(place_ref, g, parts)] = turned[g * depth : (g + 1) * depth]


def pair_mask():
    rows = lax.broadcasted_iota(jnp.int32, (TILE, 2 * TILE), 0)
    keys = lax.broadcasted_iota(jnp.int32, (TILE, 2 * TILE), 1) & (TILE - 1)
    return (rows // POS == keys // POS) & (keys <= rows)


def two_heads(values):
    first = lax.broadcasted_iota(jnp.int32, values.shape, 1) < HD
    zero = jnp.zeros_like(values)
    return jnp.concatenate(
        [jnp.where(first, values, zero), jnp.where(first, zero, values)], axis=0
    )


def one_pair(values):
    first = lax.broadcasted_iota(jnp.int32, (TILE, LANES), 1) < HD
    return jnp.where(first, values[:TILE], values[TILE:])


def per_head(op, values):
    both = [
        jnp.broadcast_to(op(values[:, s : s + TILE], axis=1, keepdims=True), (TILE, TILE))
        for s in (0, TILE)
    ]
    return jnp.concatenate(both, axis=1)


def probs_of(queries, keys, mask):
    scores = jnp.where(mask, nt(queries, keys) * SCALE, -1e30)
    powers = jnp.exp(scores - per_head(jnp.max, scores))
    return powers / per_head(jnp.sum, powers)


def pairs_of(rows, width):
    return [
        (pl.ds(t * TILE, TILE), pl.ds(p * LANES, LANES))
        for t in range(rows // TILE)
        for p in range(width // LANES)
    ]


def wide(lanes):
    return pl.ds(lanes.start // LANES * 2 * TILE, 2 * TILE)


def attention_body(
    x_ref, gain_ref, wq_ref, wk_ref, wv_ref, wo_ref, q_ref, k_ref, v_ref, m_ref, p_ref, part_ref
):
    normed = normed_of(x_ref, gain_ref)
    q_ref[...] = nn(normed, wq_ref[...]).astype(bf16)
    k_ref[...] = nn(normed, wk_ref[...]).astype(bf16)
    v_ref[...] = nn(normed, wv_ref[...]).astype(bf16)
    mask = pair_mask()
    for at in pairs_of(*q_ref.shape):
        probs = probs_of(q_ref[at], two_heads(k_ref[at]), mask).astype(bf16)
        p_ref[at[0], wide(at[1])] = probs
        m_ref[at] = nn(probs, two_heads(v_ref[at])).astype(bf16)
    part_ref[...] = nn(m_ref[...], wo_ref[...]).astype(bf16)


def attention(x, gain, wq, wk, wv, wo):
    rows, width = x.shape
    heads = wq.shape[1]
    block = 256
    outs = [(rows_of(block, heads), (rows, heads), bf16)] * 4
    spread = 2 * TILE * heads // LANES
    outs += [(rows_of(block, spread), (rows, spread), bf16)]
    outs += [(rows_of(block, width), (rows, width), bf16, ANYWHERE)]
    return call(
        attention_body,
        "attention_forward",
        (rows // block,),
        [rows_of(block, width), whole(width)]
        + [whole(width, heads)] * 3
        + [whole(heads, width)],
        outs,
        vmem=24,
        cost=(8 * rows * width * heads, 12 * MIB),
        far=(0, 2, 3, 4, 5),
    )(x, gain, wq, wk, wv, wo)


def seed_body(lengths_ref, me_ref, cot_ref, x_ref, gain_ref, seed_ref, turned_ref, normed_ref):
    block = cot_ref.shape[0]
    first = pl.program_id(0) * block
    length = lengths_ref[first // (SLOT * POS)]
    row = lax.broadcasted_iota(jnp.int32, cot_ref.shape, 0) + first % (SLOT * POS)
    cot = cot_ref[...].astype(f32)
    seed = jnp.where(row // POS < length, cot, 0.0).astype(bf16)
    seed_ref[...] = seed
    put_transposed(turned_ref, me_ref, seed)
    put_transposed(normed_ref, me_ref, normed_of(x_ref, gain_ref))


def normed_of(x_ref, gain_ref):
    values = x_ref[...].astype(f32)
    return (values * inverse_rms(values) * row_of(gain_ref)).astype(bf16)


def turned_out(parts, depth, rows, block):
    return (
        pl.BlockSpec((parts, depth, block), lambda i, *_: (0, 0, i)),
        (parts, depth, rows),
        bf16,
    )


def seeds(lengths, me, cot, x, gain, parts):
    rows, width = cot.shape
    block = 256
    turned = turned_out(parts, width // parts, rows, block)
    return call(
        seed_body,
        "seed_rows",
        (rows // block,),
        [rows_of(block, width)] * 2 + [whole(width)],
        [(rows_of(block, width), (rows, width), bf16, pltpu.VMEM), (*turned, pltpu.VMEM), turned],
        vmem=16,
        scalars=2,
        far=(0, 1),
        cost=(4 * rows * width, 6 * MIB),
    )(lengths, me, cot, x, gain)


def middle_body(me_ref, x_ref, own_ref, peer_ref, gain_ref, middle_ref, normed_ref, turned_ref):
    middle = x_ref[...].astype(f32) + (own_ref[...].astype(f32) + peer_ref[...].astype(f32))
    middle_ref[...] = middle.astype(bf16)
    normed = (middle * inverse_rms(middle) * row_of(gain_ref)).astype(bf16)
    normed_ref[...] = normed
    put_transposed(turned_ref, me_ref, normed)


def middles(me, x, own, peer, gain, parts):
    rows, width = x.shape
    block = 256
    return call(
        middle_body,
        "middle_rows",
        (rows // block,),
        [rows_of(block, width)] * 3 + [whole(width)],
        [
            (rows_of(block, width), (rows, width), bf16),
            (rows_of(block, width), (rows, width), bf16, pltpu.VMEM),
            (*turned_out(parts, width // parts, rows, block), pltpu.VMEM),
        ],
        vmem=24,
        scalars=1,
        cost=(8 * rows * width, 14 * MIB),
    )(me, x, own, peer, gain)


def places(parts, bits):
    count = len(bits)
    return [
        sum(bit for n, bit in enumerate(bits) if place >> (count - 1 - n) & 1)
        for place in range(parts)
    ]


def put_pieces(keep_ref, send_ref, column, values, order, first):
    half, _, depth, _ = keep_ref.shape
    low = values.astype(bf16)
    for n in range(values.shape[0] // depth):
        place = order.index(first + n)
        ref, at = (keep_ref, place) if place < half else (send_ref, place - half)
        for c in range(values.shape[1] // LANES):
            ref[at, column + c] = low[
                n * depth : (n + 1) * depth, c * LANES : (c + 1) * LANES
            ]


def product_pieces(keep_ref, send_ref, column, turned_ref, right, order):
    parts, depth, rows = turned_ref.shape
    group = max(1, 256 // depth)
    for first in range(0, parts, group):
        left = turned_ref[pl.ds(first, group)].reshape(group * depth, rows)
        put_pieces(keep_ref, send_ref, column, nn(left, right), order, first)


def resident():
    return pl.BlockSpec(memory_space=pltpu.VMEM)


def hidden_body(order, first, block, first_call, *refs):
    (n_ref, nt_ref, s_ref, st_ref, wg_ref, wu_ref, wd_ref) = refs[:7]
    h_ref, gg_ref, gu_ref, keep_ref, send_ref = refs[7 if first_call else 10 :]
    rows = n_ref.shape[0]
    step = min(256, rows)
    here = pl.ds(pl.multiple_of(first + pl.program_id(0) * block, block), block)
    for r in range(0, rows, step):
        at = pl.ds(r, step)
        gate = nn(n_ref[at], wg_ref[:, here])
        up = nn(n_ref[at], wu_ref[:, here])
        back = nt(s_ref[at], wd_ref[...])
        sig = 1.0 / (1.0 + jnp.exp(-gate))
        silu = gate * sig
        h_ref[at, here] = (silu * up).astype(bf16)
        gg_ref[at, here] = (back * up * (sig * (1.0 + gate * (1.0 - sig)))).astype(bf16)
        gu_ref[at, here] = (back * silu).astype(bf16)
    columns = block // LANES
    product_pieces(keep_ref, send_ref, 0, nt_ref, gg_ref[:, here], order)
    product_pieces(keep_ref, send_ref, columns, nt_ref, gu_ref[:, here], order)
    product_pieces(keep_ref, send_ref, 2 * columns, st_ref, h_ref[:, here], order)


def hidden_chunk(first, steps, block, order, normed, normed_t, seed, seed_t, wg, wu, wd, earlier):
    rows, width = normed.shape
    parts, depth, _ = normed_t.shape
    hidden = wg.shape[1]
    groups = 3 * block // LANES
    pieces = (
        pl.BlockSpec((parts // 2, groups, depth, LANES), lambda j: (0, j, 0, 0)),
        (parts // 2, steps * groups, depth, LANES),
        bf16,
    )
    args = [normed, normed_t, seed, seed_t, wg, wu, wd]
    ins = [resident()] * 6
    ins.append(pl.BlockSpec((block, width), lambda j: (first // block + j, 0)))
    aliases = {}
    if earlier is not None:
        aliases = {7: 0, 8: 1, 9: 2}
        args += list(earlier)
        ins += [resident()] * 3
    return call(
        functools.partial(hidden_body, order, first, block, earlier is None),
        "hidden_units",
        (steps,),
        ins,
        [(resident(), (rows, hidden), bf16, pltpu.VMEM)] * 3 + [pieces, (*pieces, ANYWHERE)],
        vmem=13,
        far=(6,),
        aliases=aliases,
        cost=(12 * rows * width * block * steps, 20 * MIB),
    )(*args)


def back_body(first, gg_ref, gu_ref, wg_ref, wu_ref, *part_refs):
    rows = part_refs[0].shape[0]
    here = pl.ds(first, rows * len(part_refs))
    part = nt(gg_ref[here], wg_ref[...]) + nt(gu_ref[here], wu_ref[...])
    for n, ref in enumerate(part_refs):
        ref[...] = part[n * rows : (n + 1) * rows].astype(bf16)


def normed_two_back(half, gg, gu, wg, wu):
    rows, hidden = gg.shape
    rows //= HALVES
    width = wg.shape[0]
    block = 256
    weights = pl.BlockSpec((block, hidden), lambda j: (j, 0))
    piece = rows // PARTS
    out = (pl.BlockSpec((piece, block), lambda j: (0, j)), (piece, width), bf16, ANYWHERE)
    return call(
        functools.partial(back_body, half * rows),
        "normed_two_back",
        (width // block,),
        [resident()] * 2 + [weights] * 2,
        [out] * PARTS,
        vmem=20,
        cost=(4 * rows * width * hidden, 14 * MIB),
    )(gg, gu, wg, wu)


def down_body(h_ref, wd_ref, *part_refs):
    part = nn(h_ref[...], wd_ref[...])
    rows = part_refs[0].shape[0]
    for n, ref in enumerate(part_refs):
        ref[...] = part[n * rows : (n + 1) * rows].astype(bf16)


def hidden_down(hidden, wd):
    rows, units = hidden.shape
    width = wd.shape[1]
    block = 256
    piece = rows // PARTS
    out = (pl.BlockSpec((piece, block), lambda j: (0, j)), (piece, width), bf16, ANYWHERE)
    return call(
        down_body,
        "hidden_down",
        (width // block,),
        [resident(), pl.BlockSpec((units, block), lambda j: (0, j))],
        [out] * PARTS,
        vmem=20,
        cost=(2 * rows * width * units, 10 * MIB),
    )(hidden, wd)


def add_up(ref, part):
    @pl.when(pl.program_id(0) == 0)
    def _():
        ref[...] = part

    @pl.when(pl.program_id(0) > 0)
    def _():
        ref[...] += part


def shares_sum(pairs, scratch_ref):
    for n in range(PARTS):

        @pl.when(pl.program_id(0) == n)
        def _():
            scratch_ref[...] = pairs[n][...].astype(f32) + pairs[PARTS + n][...].astype(f32)

    return scratch_ref[...]


def middle_back_body(me_ref, mid_ref, seed_ref, gain_ref, wo_ref, *refs):
    turned_ref, mixed_ref, grad_ref, sum_ref, scratch_ref = refs[-5:]
    upstream = shares_sum(refs, scratch_ref)
    middle = mid_ref[...].astype(f32)
    inverse = inverse_rms(middle)
    scaled = middle * inverse
    add_up(sum_ref, jnp.sum(upstream * scaled, axis=0, keepdims=True))
    weighted = upstream * row_of(gain_ref)
    grad_middle = seed_ref[...].astype(f32) + inverse * (
        weighted - scaled * jnp.mean(weighted * scaled, axis=1, keepdims=True)
    )
    low = grad_middle.astype(bf16)
    grad_ref[...] = low
    mixed_ref[...] = nt(low, wo_ref[...]).astype(bf16)
    put_transposed(turned_ref, me_ref, low)


def middle_back(half, me, middle, seed, gain, wo, parts, shares, earlier):
    rows, width = middle.shape
    heads = wo.shape[0]
    share = rows // HALVES
    block = share // PARTS
    depth = width // parts
    there = lambda n: pl.BlockSpec((block, n), lambda i, *_: (half * PARTS + i, 0))
    ins = [there(width)] * 2 + [whole(width), whole(heads, width)]
    ins += [whole(block, width)] * (2 * PARTS)
    args = [me, middle, seed, gain, wo, *shares]
    aliases = {}
    if earlier is not None:
        ins += [pl.BlockSpec(memory_space=pl.ANY)] * 2
        aliases = {len(args) + n: n for n in range(2)}
        args += list(earlier)
    return call(
        middle_back_body,
        "middle_backward",
        (PARTS,),
        ins,
        [
            (
                pl.BlockSpec((parts, depth, block), lambda i, *_: (0, 0, half * PARTS + i)),
                (parts, depth, rows),
                bf16,
            ),
            (there(heads), (rows, heads), bf16),
            (rows_of(block, width), (share, width), bf16),
            (whole(1, width), (1, width), f32),
        ],
        scratch=[pltpu.VMEM((block, width), f32)],
        vmem=24,
        scalars=1,
        aliases=aliases,
        cost=(2 * share * width * heads, 9 * MIB),
    )(*args)


def attention_back_body(q_ref, k_ref, v_ref, p_ref, mixed_ref, wq_ref, wk_ref, wv_ref, *refs):
    gqkv_ref, *part_refs = refs[-1 - PARTS :]
    heads = q_ref.shape[1]
    for at in pairs_of(*q_ref.shape):
        rows, lanes = at
        queries, grads = q_ref[at], mixed_ref[at]
        keys, values = two_heads(k_ref[at]), two_heads(v_ref[at])
        low = p_ref[rows, wide(lanes)]
        probs = low.astype(f32)
        grad_probs = nt(grads, values)
        grad_values = one_pair(tn(low, grads))
        inner = per_head(jnp.sum, grad_probs * probs)
        grad_scores = (probs * (grad_probs - inner)).astype(bf16)
        grad_queries = nn(grad_scores, keys) * SCALE
        grad_keys = one_pair(tn(grad_scores, queries)) * SCALE
        for n, grad in enumerate((grad_queries, grad_keys, grad_values)):
            gqkv_ref[rows, pl.ds(n * heads + lanes.start, LANES)] = grad.astype(bf16)
    part = nt(gqkv_ref[:, :heads], wq_ref[...])
    part += nt(gqkv_ref[:, heads : 2 * heads], wk_ref[...])
    part += nt(gqkv_ref[:, 2 * heads :], wv_ref[...])
    for n, ref in enumerate(part_refs):

        @pl.when(pl.program_id(0) == n)
        def _():
            ref[...] = part.astype(bf16)


def attention_back(half, q, k, v, probs, grad_mixed, wq, wk, wv, earlier):
    rows, heads = q.shape
    width = wq.shape[0]
    share = rows // HALVES
    block = share // PARTS
    there = lambda n: pl.BlockSpec((block, n), lambda i: (half * PARTS + i, 0))
    ins = [there(heads)] * 3 + [there(probs.shape[1]), there(heads)] + [whole(width, heads)] * 3
    args = [q, k, v, probs, grad_mixed, wq, wk, wv]
    aliases = {}
    if earlier is not None:
        ins.append(pl.BlockSpec(memory_space=pl.ANY))
        aliases = {len(args): 0}
        args.append(earlier)
    return call(
        attention_back_body,
        "attention_backward",
        (PARTS,),
        ins,
        [
            (there(3 * heads), (rows, 3 * heads), bf16, ANYWHERE),
            *[(whole(block, width), (block, width), bf16, ANYWHERE)] * PARTS,
        ],
        vmem=32,
        far=(4,),
        aliases=aliases,
        cost=(6 * share * width * heads, 9 * MIB),
    )(*args)


def query_key_body(order, turned_ref, right_ref, keep_ref, send_ref):
    product_pieces(keep_ref, send_ref, 0, turned_ref, right_ref[...], order)


def query_key_pieces(order, turned, right, heads):
    parts, depth, rows = turned.shape
    groups = heads // LANES
    pieces = (
        pl.BlockSpec((parts // 2, groups, depth, LANES), lambda j: (0, j, 0, 0)),
        (parts // 2, 2 * groups, depth, LANES),
        bf16,
    )
    return call(
        functools.partial(query_key_body, order),
        "query_key_grads",
        (2,),
        [whole(parts, depth, rows), pl.BlockSpec((rows, heads), lambda j: (0, j))],
        [pieces, (*pieces, ANYWHERE)],
        vmem=24,
        cost=(4 * rows * parts * depth * heads, 6 * MIB),
    )(turned, right)


def value_out_body(order, value_ref, right_ref, out_ref, mixed_ref, me_ref, *refs):
    *gain_refs, keep_ref, send_ref = refs
    groups = right_ref.shape[1] // LANES
    product_pieces(keep_ref, send_ref, 0, value_ref, right_ref[...], order)
    product_pieces(keep_ref, send_ref, groups, out_ref, mixed_ref[...], order)
    first, second = (sum(ref[...] for ref in gain_refs[n::2]) for n in range(2))
    row = lax.broadcasted_iota(jnp.int32, (LANES, first.shape[1]), 0)
    both = jnp.where(row == 0, first, jnp.where(row == 1, second, 0.0))
    turned = both.T.astype(bf16)
    half, _, depth, _ = keep_ref.shape
    bits = [order[1 << n] for n in reversed(range((2 * half).bit_length() - 1))]
    for g in range(2 * half):
        apart = relative(me_ref, g, 2 * half)
        place = 0
        for bit in bits:
            place = 2 * place + (apart & bit != 0).astype(jnp.int32)
        piece = turned[g * depth : (g + 1) * depth]

        @pl.when(place < half)
        def _():
            keep_ref[jnp.minimum(place, half - 1), 2 * groups] = piece

        @pl.when(place >= half)
        def _():
            send_ref[jnp.maximum(place - half, 0), 2 * groups] = piece


def value_out_pieces(order, turned, right, out_turned, mixed, me, *gains):
    parts, depth, rows = turned.shape
    heads = mixed.shape[1]
    shape = (parts // 2, 2 * heads // LANES + 1, depth, LANES)
    return call(
        functools.partial(value_out_body, order),
        "value_out_grads",
        (1,),
        [
            whole(parts, depth, rows),
            pl.BlockSpec((rows, heads), lambda j: (0, 2)),
            whole(parts, depth, rows),
            whole(rows, heads),
            pl.BlockSpec(memory_space=pltpu.SMEM),
            *[whole(1, parts * depth)] * len(gains),
        ],
        [(whole(*shape), shape, bf16), (whole(*shape), shape, bf16, ANYWHERE)],
        vmem=32,
        cost=(4 * rows * parts * depth * heads, 8 * MIB),
    )(turned, right, out_turned, mixed, me, *gains)


def input_grad_body(x_ref, gm_ref, gain_ref, *refs):
    out_ref, sum_ref, scratch_ref = refs[-3:]
    inputs = x_ref[...].astype(f32)
    inverse = inverse_rms(inputs)
    scaled = inputs * inverse
    upstream = shares_sum(refs, scratch_ref)
    add_up(sum_ref, jnp.sum(upstream * scaled, axis=0, keepdims=True))
    weighted = upstream * row_of(gain_ref)
    out_ref[...] = (
        gm_ref[...].astype(f32)
        + inverse * (weighted - scaled * jnp.mean(weighted * scaled, axis=1, keepdims=True))
    ).astype(bf16)


def input_grad(half, x, grad_middle, gain, shares, earlier):
    rows, width = x.shape
    block = rows // HALVES // PARTS
    there = pl.BlockSpec((block, width), lambda i: (half * PARTS + i, 0))
    ins = [there, rows_of(block, width), whole(width)] + [whole(block, width)] * (2 * PARTS)
    args = [x, grad_middle, gain, *shares]
    aliases = {}
    if earlier is not None:
        ins.append(pl.BlockSpec(memory_space=pl.ANY))
        aliases = {len(args): 0}
        args.append(earlier)
    return call(
        input_grad_body,
        "input_grad",
        (PARTS,),
        ins,
        [(there, (rows, width), bf16), (whole(1, width), (1, width), f32)],
        scratch=[pltpu.VMEM((block, width), f32)],
        vmem=24,
        aliases=aliases,
        cost=(10 * rows // HALVES * width, 6 * MIB),
    )(*args)


def total_of(refs):
    total = refs[0][0].astype(f32)
    for ref in refs[1:]:
        total += ref[0].astype(f32)
    return total


def last_hidden_body(count, block, first_call, *refs):
    total = total_of(refs[:count])
    outs = refs[count if first_call else count + 3 :]
    third = block // LANES
    for c in range(total.shape[0]):
        n, at = c // third % 3, (c // (3 * third) * third + c % third) * LANES
        outs[n][:, at : at + LANES] = total[c]


def last_hidden(first, arrays, steps, block, hidden, earlier):
    _, groups, depth, _ = arrays[0].shape
    at_once = math.gcd(first // block, steps)
    steps //= at_once
    ins = [pl.BlockSpec((1, groups // steps, depth, LANES), lambda j: (0, j, 0, 0))] * len(arrays)
    args = list(arrays)
    aliases = {}
    if earlier is not None:
        ins += [pl.BlockSpec(memory_space=pl.ANY)] * 3
        aliases = {len(arrays) + n: n for n in range(3)}
        args += list(earlier)
    wide = block * at_once
    out = (pl.BlockSpec((depth, wide), lambda j: (0, first // wide + j)), (depth, hidden), f32)
    return call(
        functools.partial(last_hidden_body, len(arrays), block, earlier is None),
        "hidden_grads_out",
        (steps,),
        ins,
        [out] * 3,
        vmem=16,
        aliases=aliases,
        cost=(6 * groups * depth * LANES, MIB),
    )(*args)


def last_heads_body(count, *refs):
    total = total_of(refs[:count])
    outs = refs[count:]
    groups = outs[0].shape[1] // LANES
    for n, ref in enumerate(outs[:2]):
        for c in range(groups):
            ref[:, c * LANES : (c + 1) * LANES] = total[n * groups + c]
    if len(outs) > 2:
        turned = total[2 * groups].T
        for n, ref in enumerate(outs[2:]):
            ref[...] = turned[n]


def last_heads(arrays, heads):
    _, groups, depth, _ = arrays[0].shape
    shapes = [(depth, heads)] * 2
    if groups * LANES > 2 * heads:
        shapes += [(depth,)] * 2
    return call(
        functools.partial(last_heads_body, len(arrays)),
        "head_grads_out",
        (1,),
        [pl.BlockSpec((1, groups, depth, LANES), lambda j: (0, 0, 0, 0))] * len(arrays),
        [(whole(*shape), shape, f32) for shape in shapes],
        vmem=16,
        cost=(6 * groups * depth * LANES, MIB),
    )(*arrays)


def block_output_body(mid_ref, *refs):
    out_ref, scratch_ref = refs[-2:]
    out_ref[...] = (mid_ref[...].astype(f32) + shares_sum(refs, scratch_ref)).astype(bf16)


def block_outputs(middle, shares):
    rows, width = middle.shape
    block = rows // PARTS
    return call(
        block_output_body,
        "block_output",
        (PARTS,),
        [rows_of(block, width)] + [whole(block, width)] * (2 * PARTS),
        [(rows_of(block, width), (rows, width), bf16)],
        scratch=[pltpu.VMEM((block, width), f32)],
        vmem=24,
        cost=(3 * rows * width, 10 * MIB),
    )(middle, *shares)[0]


def swap(array, axis, size, bit):
    return lax.ppermute(array, axis, [(i, i ^ bit) for i in range(size)])


def hop_swap(array, dp, tensor, bit):
    bits = [exchanged(bit, dp) if t % 2 else bit for t in range(tensor)]
    pairs = [
        (i * tensor + t, (i ^ bits[t]) * tensor + t) for i in range(dp) for t in range(tensor)
    ]
    return lax.ppermute(array, ("dp", "tensor"), pairs)


def both_shares(partial, size):
    bit = 1
    while 2 * bit < size:
        other = swap(partial, "tensor", size, bit)
        partial = (partial.astype(f32) + other.astype(f32)).astype(bf16)
        bit *= 2
    return partial, swap(partial, "tensor", size, bit)


def after(value, *others):
    return lax.optimization_barrier((value, *others))[0]


def next_send_body(*refs):
    total = refs[0][...].astype(f32)
    for ref in refs[1:-1]:
        total += ref[...].astype(f32)
    refs[-1][...] = total.astype(bf16)


def next_send(half, arrays):
    _, *rest = arrays[0].shape
    block = max(1, half // 2)
    steps = half // block
    return call(
        next_send_body,
        "next_send",
        (steps,),
        [pl.BlockSpec((block, *rest), lambda i: (steps + i, 0, 0, 0))] * len(arrays),
        [(pl.BlockSpec((block, *rest), lambda i: (i, 0, 0, 0)), (half, *rest), bf16, ANYWHERE)],
        vmem=16,
        cost=(half * math.prod(rest), MIB),
    )(*arrays)[0]


class Line:
    def __init__(self):
        self.last = None

    def __call__(self, kernel, waits, *args):
        if self.last is not None:
            waits, _ = lax.optimization_barrier((waits, self.last))
        out = kernel(waits, *args)
        self.last = jax.tree.leaves(out)[-1]
        return out


class Halving:
    def __init__(self, line, pieces, sizes, bits):
        self.line, self.sizes, self.bits = line, sizes, list(bits)
        self.arrays = [pieces[0]]
        self.half = sizes[0] // 2
        self.launch(pieces[1])

    def launch(self, send):
        self.coming = hop_swap(send, *self.sizes, self.bits.pop(0))

    def hop(self):
        self.arrays.append(self.coming)
        self.half //= 2
        self.launch(
            self.line(
                lambda newest: next_send(self.half, [*self.arrays[:-1], newest]), self.arrays[-1]
            )
        )

    def end(self, kernel, *rest):
        return self.line(lambda newest: kernel([*self.arrays, newest], *rest), self.coming)


STEPS = (
    "attn", "seed", "mid", "H0", "H1", "ntA", "ntB", "mbA", "mbB", "abA", "h:0", "abB", "igA",
    "QK", "igB", "VO", "h:1", "h:0", "down", "h:QK", "h:VO", "h:1", "h:QK", "h:VO", "h:0", "h:VO",
    "h:1", "h:QK", "e:QK", "bo", "e:1", "e:0", "e:VO",
)


class Layer:
    def __init__(self, args, dp, tensor, bits_of):
        (
            self.x, self.wq, self.wk, self.wv, self.wo, self.wg, self.wu, self.wd,
            self.gain_one, self.gain_two, self.lengths, self.cot,
        ) = args
        self.dp, self.tensor, self.bits_of = dp, tensor, bits_of
        self.heads, self.units = self.wq.shape[1], self.wg.shape[1]
        self.line, self.sums = Line(), {}
        self.block = 256 if self.units >= 2048 else LANES
        blocks = self.units // self.block
        shares = [blocks * n // 8 for n in (5,)]
        self.shares = [*shares, blocks - sum(shares)]
        self.me = jnp.stack([lax.axis_index("dp"), lax.axis_index("tensor") % 2]).astype(jnp.int32)
        self.acts = self.saved = self.gqkv = self.grads = self.grad_input = None
        self.mid_shares, self.in_shares, self.middle_grads, self.gain_sums = [], [], [], {}

    def order(self, name):
        return places(self.dp, self.bits_of[name])

    def begin(self, name, pieces):
        self.sums[name] = Halving(self.line, pieces, (self.dp, self.tensor), self.bits_of[name])

    def shared(self, parts):
        both = [both_shares(part, self.tensor) for part in parts]
        return [own for own, _ in both] + [peer for _, peer in both]

    def attention(self):
        self.q, self.k, self.v, self.mixed, self.probs, part = attention(
            self.x, self.gain_one, self.wq, self.wk, self.wv, self.wo
        )
        self.line.last = part
        self.own, self.peer = both_shares(part, self.tensor)

    def seeds(self):
        self.seed, self.seed_t, self.normed_t = self.line(
            lambda cot: seeds(self.lengths, self.me, cot, self.x, self.gain_one, self.dp), self.cot
        )

    def middles(self):
        self.middle, self.normed, self.normed_two_t = self.line(
            lambda peer: middles(self.me, self.x, self.own, peer, self.gain_two, self.dp), self.peer
        )

    def hidden(self, c):
        *acts, keep, send = self.line(
            lambda normed: hidden_chunk(
                self.block * sum(self.shares[:c]), self.shares[c], self.block, self.order(c),
                normed, self.normed_two_t, self.seed, self.seed_t, self.wg, self.wu, self.wd, self.acts,
            ),
            self.normed,
        )
        self.acts = acts
        self.begin(c, (keep, send))

    def normed_back(self, half):
        parts = self.line(
            lambda gg: normed_two_back(half, gg, self.acts[2], self.wg, self.wu), self.acts[1]
        )
        self.mid_shares.append(self.shared(parts))

    def down(self):
        self.down_shares = self.shared(
            self.line(lambda hidden: hidden_down(hidden, self.wd), self.acts[0])
        )

    def output(self):
        self.block_output = self.line(
            lambda shares: block_outputs(self.middle, shares), self.down_shares
        )

    def middle_back(self, half):
        *self.saved, grad, self.gain_sums["two", half] = self.line(
            lambda shares: middle_back(
                half, self.me, self.middle, self.seed, self.gain_two, self.wo, self.dp, shares, self.saved
            ),
            self.mid_shares[half],
        )
        self.middle_grads.append(grad)

    def attention_back(self, half):
        self.gqkv, *parts = self.line(
            lambda grad_mixed: attention_back(
                half, self.q, self.k, self.v, self.probs, grad_mixed, self.wq, self.wk, self.wv, self.gqkv
            ),
            self.saved[1],
        )
        self.in_shares.append(self.shared(parts))

    def query_key(self):
        self.begin(
            "qk",
            self.line(
                lambda gqkv: query_key_pieces(self.order("qk"), self.normed_t, gqkv, self.heads),
                self.gqkv,
            ),
        )

    def input_back(self, half):
        self.grad_input, self.gain_sums["one", half] = self.line(
            lambda shares: input_grad(
                half, self.x, self.middle_grads[half], self.gain_one, shares, self.grad_input
            ),
            self.in_shares[half],
        )

    def value_out(self):
        gains = [self.gain_sums[name, half] for half in range(HALVES) for name in ("one", "two")]
        self.begin(
            "vo",
            self.line(
                lambda gqkv: value_out_pieces(
                    self.order("vo"), self.normed_t, gqkv, self.saved[0], self.mixed, self.me, *gains
                ),
                self.gqkv,
            ),
        )

    def hop(self, name):
        if self.sums[name].bits:
            self.sums[name].hop()

    def end(self, name):
        one = self.sums[name]
        while one.bits:
            one.hop()
        if name == "qk":
            self.grad_query, self.grad_key = one.end(last_heads, self.heads)
        elif name == "vo":
            self.grad_value, self.grad_out, *self.gains = one.end(last_heads, self.heads)
        else:
            first = self.block * sum(self.shares[:name])
            self.grads = one.end(
                lambda arrays: last_hidden(
                    first, arrays, self.shares[name], self.block, self.units, self.grads
                )
            )

    def run(self):
        calls = {
            "attn": self.attention, "seed": self.seeds, "mid": self.middles, "down": self.down,
            "bo": self.output, "QK": self.query_key, "VO": self.value_out,
        }
        halves = {
            "nt": self.normed_back, "mb": self.middle_back,
            "ab": self.attention_back, "ig": self.input_back,
        }
        for step in STEPS:
            if step in calls:
                calls[step]()
            elif step[:2] in halves:
                halves[step[:2]]("AB".index(step[2:]))
            elif step[0] == "H":
                self.hidden(int(step[1:]))
            else:
                name = step[2:].lower()
                name = int(name) if name.isdigit() else name
                (self.hop if step[0] == "h" else self.end)(name)
        return (
            self.block_output,
            self.grad_input,
            self.grad_query,
            self.grad_key,
            self.grad_value,
            self.grad_out.T,
            self.grads[0],
            self.grads[1],
            self.grads[2].T,
            *self.gains,
        )


def body_of(dp, tensor):
    n_bits = dp.bit_length() - 1

    def order(*start):
        return [1 << k for k in start if k < n_bits] + [1 << k for k in range(n_bits) if k not in start]

    bits_of = {
        0: order(0, 1, 3, 2),
        1: order(2, 0, 1, 3),
        "qk": order(0, 2, 3, 1),
        "vo": order(0, 1, 2, 3),
    }

    def body(*args):
        return Layer(args, dp, tensor, bits_of).run()

    return body


def solution(mesh):
    placed = (
        P("dp", None),
        P(None, "tensor"),
        P(None, "tensor"),
        P(None, "tensor"),
        P("tensor", None),
        P(None, "tensor"),
        P(None, "tensor"),
        P("tensor", None),
        P(),
        P(),
        P("dp"),
        P("dp", None),
    )
    return jax.shard_map(
        body_of(mesh.shape["dp"], mesh.shape["tensor"]),
        mesh=mesh,
        in_specs=placed,
        out_specs=(
            P("dp", None),
            P("dp", None),
            P("dp", "tensor"),
            P("dp", "tensor"),
            P("dp", "tensor"),
            P("tensor", "dp"),
            P("dp", "tensor"),
            P("dp", "tensor"),
            P("tensor", "dp"),
            P("dp"),
            P("dp"),
        ),
        check_vma=False,
    )
```

profile of v0, /device:TPU:0, one launch (start us, length us, event | category | flops | bytes accessed | tf_op | source)
XLA Modules:
  0.0 217.6 jit_solution(394160059810614545)
XLA Ops:
  0.7 0.7 copy-done.29
  1.3 12.2 %attention_forward.1 = (bf16[1024,512]{1,0:T(8,128)(2,1)}, bf16[1024,512]{1,0:T(8,128)(2,1)}, bf16[1024,512]{1,0:T(8,128)(2,1)}, bf16[1024,512]{1,0:T(8,128)(2,1...) custom-call(bf16[1024,1024]{1,0:T(8,128)(2,1)} %x_ref.9, bf16[1024]{0:T(1024)(128)(2,1)S(1)} %copy-done.29, ...), custom_call_target="tpu_custom_call" | custom-call | flops 4294 | bytes 12 | tf_op jit(solution)/shard_map/attention_forward/pallas_call | solution.py:62
  14.1 6.2 %seed_rows.1 = (bf16[1024,1024]{1,0:T(8,128)(2,1)S(1)}, bf16[16,64,1024]{2,1,0:T(8,128)(2,1)S(1)}, bf16[16,64,1024]{2,1,0:T(8,128)(2,1)}) custom-call(s32[2]{0:T(128)S(1)} %copy-done.36, s32[2]{0:T(128)S(1)} %pad_add_fusion.me_ref, bf16[1024,1024]{1,0:T(8,128)(2,1)} %cot_ref, bf16[1024,1024]{1,0:T(8,128)(2,1)} %x_ref.9, bf16[1024]{0:T(1024)(128)(2,1)S(1)} %copy-done.30), custom_call_target="tpu_custom_call" | custom-call | flops 4 | bytes 6 | tf_op jit(solution)/shard_map/seed_rows/pallas_call | solution.py:62
  20.3 5.7 %middle_rows.1 = (bf16[1024,1024]{1,0:T(8,128)(2,1)}, bf16[1024,1024]{1,0:T(8,128)(2,1)S(1)}, bf16[16,64,1024]{2,1,0:T(8,128)(2,1)S(1)}) custom-call(s32[2]{0:T(128)S(1)} %pad_add_fusion.me_ref, bf16[1024,1024]{1,0:T(8,128)(2,1)S(1)} %copy-done.3, bf16[1024,1024]{1,0:T(8,128)(2,1)} %get-tuple-element.120.own_ref, ...), custom_call_target="tpu_custom_call" | custom-call | flops 8 | bytes 14 | tf_op jit(solution)/shard_map/middle_rows/pallas_call | solution.py:62
  26.0 21.0 %hidden_units.2 = (bf16[1024,2048]{1,0:T(8,128)(2,1)S(1)}, bf16[1024,2048]{1,0:T(8,128)(2,1)S(1)}, bf16[1024,2048]{1,0:T(8,128)(2,1)S(1)}, bf16[8,30,64,128]{3,2,1,0:T(8,128)(2,1)}, bf16[8,30,64,128]{3,2,1,0:T(8,128)(2,1)}) custom-call(bf16[1024,1024]{1,0:T(8,128)(2,1)S(1)} %get-tuple-element.131.refs_0_, ...), custom_call_target="tpu_custom_call" | custom-call | flops 16106 | bytes 20 | tf_op jit(solution)/shard_map/hidden_units/pallas_call | solution.py:62
  47.0 2.5 %collective-permute-start.1 = (bf16[8,30,64,128]{3,2,1,0:T(8,128)(2,1)}, bf16[8,30,64,128]{3,2,1,0:T(8,128)(2,1)S(1)}, u32[]{:S(2)}, u32[]{:S(2)}) collective-permute-start(bf16[8,30,64,128]{3,2,1,0:T(8,128)(2,1)} %get-tuple-element.130), channel_id=1, source_target_pairs={{0,2},{1,5},{2,0},{3,7},{4,6},{5,1},{6,4},{7,3},{8,10},{9,13},{10,... | collective-permute-start | bytes 11796488 | tf_op jit(solution)/shard_map/ppermute | solution.py:736
  49.5 13.5 %hidden_units.3 = (bf16[1024,2048]{1,0:T(8,128)(2,1)S(1)}, bf16[1024,2048]{1,0:T(8,128)(2,1)S(1)}, bf16[1024,2048]{1,0:T(8,128)(2,1)S(1)}, bf16[8,18,64,128]{3,2,1,0:T(8,128)(2,1)}, bf16[8,18,64,128]{3,2,1,0:T(8,128)(2,1)}) custom-call(bf16[1024,1024]{1,0:T(8,128)(2,1)S(1)} %get-tuple-element.131.refs_0_, ...), custom_call_target="tpu_custom_call", output_to_operand_aliasing={{0}: (7, {}), {1}: (8, {}), {2}: (9, {})} | custom-call | flops 9663 | bytes 20 | tf_op jit(solution)/shard_map/hidden_units/pallas_call | solution.py:62
  63.0 5.3 %normed_two_back.2 = (bf16[256,1024]{1,0:T(8,128)(2,1)S(1)}, bf16[256,1024]{1,0:T(8,128)(2,1)S(1)}) custom-call(bf16[1024,2048]{1,0:T(8,128)(2,1)S(1)} %get-tuple-element.146.gg_ref, bf16[1024,2048]{1,0:T(8,128)(2,1)S(1)} %get-tuple-element.144.gu_ref, bf16[1024,2048]{1,0:T(8,128)(2,1)S(1)} %copy-done, bf16[1024,2048]{1,0:T(8,128)(2,1)S(1)} %copy-done.1), custom_call_target="tpu_custom_call" | custom-call | flops 4294 | bytes 14 | tf_op jit(solution)/shard_map/normed_two_back/pallas_call | solution.py:62
  68.6 1.6 collective-permute-start.7
  70.2 5.4 %normed_two_back.3 = (bf16[256,1024]{1,0:T(8,128)(2,1)S(1)}, bf16[256,1024]{1,0:T(8,128)(2,1)S(1)}) custom-call(bf16[1024,2048]{1,0:T(8,128)(2,1)S(1)} %get-tuple-element.146.gg_ref, bf16[1024,2048]{1,0:T(8,128)(2,1)S(1)} %get-tuple-element.144.gu_ref, bf16[1024,2048]{1,0:T(8,128)(2,1)S(1)} %copy-done, bf16[1024,2048]{1,0:T(8,128)(2,1)S(1)} %copy-done.1), custom_call_target="tpu_custom_call" | custom-call | flops 4294 | bytes 14 | tf_op jit(solution)/shard_map/normed_two_back/pallas_call | solution.py:62
  76.3 3.6 %middle_backward.2 = (bf16[16,64,1024]{2,1,0:T(8,128)(2,1)}, bf16[1024,512]{1,0:T(8,128)(2,1)}, bf16[512,1024]{1,0:T(8,128)(2,1)}, f32[1,1024]{1,0:T(1,128)}) custom-call(s32[2]{0:T(128)S(1)} %pad_add_fusion.me_ref, bf16[1024,1024]{1,0:T(8,128)(2,1)S(1)} %copy-done.7, bf16[1024,1024]{1,0:T(8,128)(2,1)S(1)} %get-tuple-element.128.refs_2_.seed_ref, ...), custom_call_target="tpu_custom_call" | custom-call | flops 536 | bytes 9 | tf_op jit(solution)/shard_map/middle_backward/pallas_call | solution.py:62
  80.0 3.7 %middle_backward.3 = (bf16[16,64,1024]{2,1,0:T(8,128)(2,1)}, bf16[1024,512]{1,0:T(8,128)(2,1)}, bf16[512,1024]{1,0:T(8,128)(2,1)}, f32[1,1024]{1,0:T(1,128)}) custom-call(s32[2]{0:T(128)S(1)} %pad_add_fusion.me_ref, bf16[1024,1024]{1,0:T(8,128)(2,1)S(1)} %copy-done.7, ...), custom_call_target="tpu_custom_call", output_to_operand_aliasing={{0}: (9, {}), {1}: (10, {})} | custom-call | flops 536 | bytes 9 | tf_op jit(solution)/shard_map/middle_backward/pallas_call | solution.py:62
  84.3 7.4 %attention_backward.2 = (bf16[1024,1536]{1,0:T(8,128)(2,1)S(1)}, bf16[256,1024]{1,0:T(8,128)(2,1)S(1)}, bf16[256,1024]{1,0:T(8,128)(2,1)S(1)}) custom-call(bf16[1024,512]{1,0:T(8,128)(2,1)S(1)} %copy-done.23, bf16[1024,512]{1,0:T(8,128)(2,1)S(1)} %copy-done.24, bf16[1024,512]{1,0:T(8,128)(2,1)S(1)} %copy-done.25, bf16[1024,1024]{1,0:T(8,128)(2,1)S(1)} %copy-done.20, ...), custom_call_target="tpu_custom_call" | custom-call | flops 1610 | bytes 9 | tf_op jit(solution)/shard_map/attention_backward/pallas_call | solution.py:62
  92.2 1.2 collective-permute-done.1.refs_1_
  93.4 1.5 next_send.12
  94.9 2.1 collective-permute-start.6
  97.0 7.3 %attention_backward.3 = (bf16[1024,1536]{1,0:T(8,128)(2,1)S(1)}, bf16[256,1024]{1,0:T(8,128)(2,1)S(1)}, bf16[256,1024]{1,0:T(8,128)(2,1)S(1)}) custom-call(bf16[1024,512]{1,0:T(8,128)(2,1)S(1)} %copy-done.23, bf16[1024,512]{1,0:T(8,128)(2,1)S(1)} %copy-done.24, bf16[1024,512]{1,0:T(8,128)(2,1)S(1)} %copy-done.25, ...), custom_call_target="tpu_custom_call", output_to_operand_aliasing={{0}: (8, {})} | custom-call | flops 1610 | bytes 9 | tf_op jit(solution)/shard_map/attention_backward/pallas_call | solution.py:62
  104.3 0.6 collective-permute-start.8
  105.0 2.3 %input_grad.2 = (bf16[1024,1024]{1,0:T(8,128)(2,1)}, f32[1,1024]{1,0:T(1,128)}) custom-call(bf16[1024,1024]{1,0:T(8,128)(2,1)S(1)} %copy-done.3, bf16[512,1024]{1,0:T(8,128)(2,1)S(1)} %copy-done.27, bf16[1024]{0:T(1024)(128)(2,1)S(1)} %copy-done.30, bf16[256,1024]{1,0:T(8,128)(2,1)S(1)} %get-tuple-element.175.refs_0_, ...), custom_call_target="tpu_custom_call" | custom-call | flops 5 | bytes 6 | tf_op jit(solution)/shard_map/input_grad/pallas_call | solution.py:62
  107.3 3.6 %query_key_grads.1 = (bf16[8,8,64,128]{3,2,1,0:T(8,128)(2,1)}, bf16[8,8,64,128]{3,2,1,0:T(8,128)(2,1)S(1)}) custom-call(bf16[16,64,1024]{2,1,0:T(8,128)(2,1)S(1)} %copy-done.19, bf16[1024,1536]{1,0:T(8,128)(2,1)S(1)} %get-tuple-element.188.right_ref), custom_call_target="tpu_custom_call" | custom-call | flops 2147 | bytes 6 | tf_op jit(solution)/shard_map/query_key_grads/pallas_call | solution.py:62
  111.0 2.4 %input_grad.3 = (bf16[1024,1024]{1,0:T(8,128)(2,1)}, f32[1,1024]{1,0:T(1,128)}) custom-call(bf16[1024,1024]{1,0:T(8,128)(2,1)S(1)} %copy-done.3, bf16[512,1024]{1,0:T(8,128)(2,1)S(1)} %copy-done.28, bf16[1024]{0:T(1024)(128)(2,1)S(1)} %copy-done.30, bf16[256,1024]{1,0:T(8,128)(2,1)S(1)} %get-tuple-element.182.refs_0_, ...), custom_call_target="tpu_custom_call", output_to_operand_aliasing={{0}: (7, {})} | custom-call | flops 5 | bytes 6 | tf_op jit(solution)/shard_map/input_grad/pallas_call | solution.py:62
  113.4 0.7 copy-done.35
  114.1 4.6 %value_out_grads.1 = (bf16[8,9,64,128]{3,2,1,0:T(8,128)(2,1)}, bf16[8,9,64,128]{3,2,1,0:T(8,128)(2,1)S(1)}) custom-call(bf16[16,64,1024]{2,1,0:T(8,128)(2,1)S(1)} %copy-done.19, bf16[1024,1536]{1,0:T(8,128)(2,1)S(1)} %get-tuple-element.188.right_ref, bf16[16,64,1024]{2,1,0:T(8,128)(2,1)S(1)} %copy-done.22, bf16[1024,512]{1,0:T(8,128)(2,1)S(1)} %copy-done.26, ...), custom_call_target="tpu_custom_call" | custom-call | flops 2147 | bytes 8 | tf_op jit(solution)/shard_map/value_out_grads/pallas_call | solution.py:62
  118.7 1.5 collective-permute-start.17
  120.7 1.5 collective-permute-done.7.refs_1_
  122.5 1.4 collective-permute-start.16
  123.9 1.3 copy-done.9
  125.2 1.5 copy-done.10
  127.1 2.7 %collective-permute-start.22 = (bf16[2,30,64,128]{3,2,1,0:T(8,128)(2,1)S(1)}, bf16[2,30,64,128]{3,2,1,0:T(8,128)(2,1)S(1)}, u32[]{:S(2)}, u32[]{:S(2)}) collective-permute-start(bf16[2,30,64,128]{3,2,1,0:T(8,128)(2,1)S(1)} %next_send.14), channel_id=1, source_target_pairs={{0,16},{1,17},{2,18},{3,19},{4,20},{5,21},{6,22},{7,23},{8,24},{9,... | collective-permute-start | bytes 2949128 | tf_op jit(solution)/shard_map/ppermute | solution.py:736
  130.2 5.8 %hidden_down.1 = (bf16[512,1024]{1,0:T(8,128)(2,1)S(1)}, bf16[512,1024]{1,0:T(8,128)(2,1)S(1)}) custom-call(bf16[1024,2048]{1,0:T(8,128)(2,1)S(1)} %copy-done.14, bf16[2048,1024]{1,0:T(8,128)(2,1)S(1)} %copy-done.5), custom_call_target="tpu_custom_call" | custom-call | flops 4294 | bytes 10 | tf_op jit(solution)/shard_map/hidden_down/pallas_call | solution.py:62
  136.0 10.1 %collective-permute-done.14.refs_1_ = bf16[8,8,64,128]{3,2,1,0:T(8,128)(2,1)S(1)} collective-permute-done((bf16[8,8,64,128]{3,2,1,0:T(8,128)(2,1)S(1)}, bf16[8,8,64,128]{3,2,1,0:T(8,128)(2,1)S(1)}, u32[]{:S(2)}, u32[]{:S(2)}) %collective-permute-start.14) | collective-permute-done | bytes 1048608 | tf_op jit(solution)/shard_map/ppermute | solution.py:736
  146.3 1.6 collective-permute-start.15
  148.1 0.8 collective-permute-start.20
  148.9 16.2 %collective-permute-done.16.refs_2_ = bf16[4,18,64,128]{3,2,1,0:T(8,128)(2,1)S(1)} collective-permute-done((bf16[4,18,64,128]{3,2,1,0:T(8,128)(2,1)S(1)}, bf16[4,18,64,128]{3,2,1,0:T(8,128)(2,1)S(1)}, u32[]{:S(2)}, u32[]{:S(2)}) %collective-permute-start.16) | collective-permute-done | bytes 1179680 | tf_op jit(solution)/shard_map/ppermute | solution.py:736
  165.4 14.4 %collective-permute-done.15.refs_2_ = bf16[4,8,64,128]{3,2,1,0:T(8,128)(2,1)S(1)} collective-permute-done((bf16[4,8,64,128]{3,2,1,0:T(8,128)(2,1)S(1)}, bf16[4,8,64,128]{3,2,1,0:T(8,128)(2,1)S(1)}, u32[]{:S(2)}, u32[]{:S(2)}) %collective-permute-start.15) | collective-permute-done | bytes 524320 | tf_op jit(solution)/shard_map/ppermute | solution.py:736
  180.5 5.3 %collective-permute-start.18 = (bf16[2,8,64,128]{3,2,1,0:T(8,128)(2,1)S(1)}, bf16[2,8,64,128]{3,2,1,0:T(8,128)(2,1)S(1)}, u32[]{:S(2)}, u32[]{:S(2)}) collective-permute-start(bf16[2,8,64,128]{3,2,1,0:T(8,128)(2,1)S(1)} %next_send.18), channel_id=1, source_target_pairs={{0,16},{1,17},{2,18},{3,19},{4,20},{5,21},{6,22},{7,23},{8,24},{9,... | collective-permute-start | bytes 786440 | tf_op jit(solution)/shard_map/ppermute | solution.py:736
  186.0 8.5 %collective-permute-done.21.refs_3_ = bf16[2,9,64,128]{3,2,1,0:T(8,128)(2,1)S(1)} collective-permute-done((bf16[2,9,64,128]{3,2,1,0:T(8,128)(2,1)S(1)}, bf16[2,9,64,128]{3,2,1,0:T(8,128)(2,1)S(1)}, u32[]{:S(2)}, u32[]{:S(2)}) %collective-permute-start.21) | collective-permute-done | bytes 294944 | tf_op jit(solution)/shard_map/ppermute | solution.py:736
  194.8 2.5 %collective-permute-start.26 = (bf16[1,18,64,128]{3,2,1,0:T(8,128)(2,1)S(1)}, bf16[1,18,64,128]{3,2,1,0:T(8,128)(2,1)S(1)}, u32[]{:S(2)}, u32[]{:S(2)}) collective-permute-start(bf16[1,18,64,128]{3,2,1,0:T(8,128)(2,1)S(1)} %next_send.22), channel_id=1, source_target_pairs={{0,16},{1,17},{2,18},{3,19},{4,20},{5,21},{6,22},{7,23},{8,24},{9,... | collective-permute-start | bytes 884744 | tf_op jit(solution)/shard_map/ppermute | solution.py:736
  197.3 1.4 collective-permute-start.23
  198.8 3.6 %collective-permute-done.23.refs_4_ = bf16[1,8,64,128]{3,2,1,0:T(8,128)(2,1)S(1)} collective-permute-done((bf16[1,8,64,128]{3,2,1,0:T(8,128)(2,1)S(1)}, bf16[1,8,64,128]{3,2,1,0:T(8,128)(2,1)S(1)}, u32[]{:S(2)}, u32[]{:S(2)}) %collective-permute-start.23) | collective-permute-done | bytes 131104 | tf_op jit(solution)/shard_map/ppermute | solution.py:736
  202.4 1.0 collective-permute-start.24
  203.4 0.7 head_grads_out.2
  204.1 1.9 block_output.1
  206.0 5.9 %collective-permute-done.26.refs_4_ = bf16[1,18,64,128]{3,2,1,0:T(8,128)(2,1)S(1)} collective-permute-done((bf16[1,18,64,128]{3,2,1,0:T(8,128)(2,1)S(1)}, bf16[1,18,64,128]{3,2,1,0:T(8,128)(2,1)S(1)}, u32[]{:S(2)}, u32[]{:S(2)}) %collective-permute-start.26) | collective-permute-done | bytes 294944 | tf_op jit(solution)/shard_map/ppermute | solution.py:736
  212.0 1.4 hidden_grads_out.2
  213.3 2.3 %collective-permute-done.25.refs_4_ = bf16[1,30,64,128]{3,2,1,0:T(8,128)(2,1)S(1)} collective-permute-done((bf16[1,30,64,128]{3,2,1,0:T(8,128)(2,1)S(1)}, bf16[1,30,64,128]{3,2,1,0:T(8,128)(2,1)S(1)}, u32[]{:S(2)}, u32[]{:S(2)}) %collective-permute-start.25) | collective-permute-done | bytes 491552 | tf_op jit(solution)/shard_map/ppermute | solution.py:736
  215.7 1.1 hidden_grads_out.3
  216.8 0.8 head_grads_out.3
  (114 shorter events, 6.3 us)
Async XLA Ops:
  1.3 12.7 %copy-start.30 = (bf16[1024]{0:T(1024)(128)(2,1)S(1)}, bf16[1024]{0:T(1024)(128)(2,1)}, u32[]{:S(2)}) copy-start(bf16[1024]{0:T(1024)(128)(2,1)} %gain_ref.13) | copy-start | bytes 6148
  1.3 12.7 %copy-start.36 = (s32[2]{0:T(128)S(1)}, s32[2]{0:T(128)}, u32[]{:S(2)}) copy-start(s32[2]{0:T(128)} %lengths_ref.1) | copy-start | bytes 28
  1.3 18.9 %copy-start.3 = (bf16[1024,1024]{1,0:T(8,128)(2,1)S(1)}, bf16[1024,1024]{1,0:T(8,128)(2,1)}, u32[]{:S(2)}) copy-start(bf16[1024,1024]{1,0:T(8,128)(2,1)} %x_ref.9) | copy-start | bytes 6291460
  13.5 6.7 %collective-permute-start = (bf16[1024,1024]{1,0:T(8,128)(2,1)}, bf16[1024,1024]{1,0:T(8,128)(2,1)}, u32[]{:S(2)}, u32[]{:S(2)}) collective-permute-start(bf16[1024,1024]{1,0:T(8,128)(2,1)} %get-tuple-element.120.own_ref), channel_id=1, source_target_pairs={{0,1},{1,0},{2,3},{3,2},{4,5},{5,4},{6,7},{7,6},{8,9},{9,8},{10,11... | collective-permute-start | bytes 6291464 | tf_op jit(solution)/shard_map/ppermute | solution.py:728
  14.0 6.2 %copy-start.31 = (bf16[1024]{0:T(1024)(128)(2,1)S(1)}, bf16[1024]{0:T(1024)(128)(2,1)}, u32[]{:S(2)}) copy-start(bf16[1024]{0:T(1024)(128)(2,1)} %gain_ref.11) | copy-start | bytes 6148
  14.0 11.9 %copy-start.1 = (bf16[1024,2048]{1,0:T(8,128)(2,1)S(1)}, bf16[1024,2048]{1,0:T(8,128)(2,1)}, u32[]{:S(2)}) copy-start(bf16[1024,2048]{1,0:T(8,128)(2,1)} %wu_ref.3) | copy-start | bytes 12582916
  20.3 5.7 %copy-start = (bf16[1024,2048]{1,0:T(8,128)(2,1)S(1)}, bf16[1024,2048]{1,0:T(8,128)(2,1)}, u32[]{:S(2)}) copy-start(bf16[1024,2048]{1,0:T(8,128)(2,1)} %wg_ref.3) | copy-start | bytes 12582916
  47.0 46.4 %collective-permute-start.1 = (bf16[8,30,64,128]{3,2,1,0:T(8,128)(2,1)}, bf16[8,30,64,128]{3,2,1,0:T(8,128)(2,1)S(1)}, u32[]{:S(2)}, u32[]{:S(2)}) collective-permute-start(bf16[8,30,64,128]{3,2,1,0:T(8,128)(2,1)} %get-tuple-element.130), channel_id=1, source_target_pairs={{0,2},{1,5},{2,0},{3,7},{4,6},{5,1},{6,4},{7,3},{8,10},{9,13},{10,... | collective-permute-start | bytes 11796488 | tf_op jit(solution)/shard_map/ppermute | solution.py:736
  63.0 5.3 %copy-start.13 = (bf16[1024,2048]{1,0:T(8,128)(2,1)}, bf16[1024,2048]{1,0:T(8,128)(2,1)S(1)}, u32[]{:S(2)}) copy-start(bf16[1024,2048]{1,0:T(8,128)(2,1)S(1)} %get-tuple-element.194.h_ref) | copy-start | bytes 12582916
  68.3 7.9 %collective-permute-start.4 = (bf16[256,1024]{1,0:T(8,128)(2,1)S(1)}, bf16[256,1024]{1,0:T(8,128)(2,1)S(1)}, u32[]{:S(2)}, u32[]{:S(2)}) collective-permute-start(bf16[256,1024]{1,0:T(8,128)(2,1)S(1)} %get-tuple-element.150.refs_0_), channel_id=1, source_target_pairs={{0,1},{1,0},{2,3},{3,2},{4,5},{5,4},{6,7},{7,6},{8,9},{9,8},{10,11... | collective-permute-start | bytes 1572872 | tf_op jit(solution)/shard_map/ppermute | solution.py:728
  68.6 53.6 %collective-permute-start.7 = (bf16[8,18,64,128]{3,2,1,0:T(8,128)(2,1)}, bf16[8,18,64,128]{3,2,1,0:T(8,128)(2,1)S(1)}, u32[]{:S(2)}, u32[]{:S(2)}) collective-permute-start(bf16[8,18,64,128]{3,2,1,0:T(8,128)(2,1)} %get-tuple-element.142), channel_id=1, source_target_pairs={{0,8},{1,9},{2,10},{3,11},{4,12},{5,13},{6,14},{7,15},{8,0},{9,1},... | collective-permute-start | bytes 7077896 | tf_op jit(solution)/shard_map/ppermute | solution.py:736
  70.2 6.1 %copy-start.7 = (bf16[1024,1024]{1,0:T(8,128)(2,1)S(1)}, bf16[1024,1024]{1,0:T(8,128)(2,1)}, u32[]{:S(2)}) copy-start(bf16[1024,1024]{1,0:T(8,128)(2,1)} %get-tuple-element.124.mid_ref) | copy-start | bytes 6291460
  70.2 6.1 %copy-start.18 = (bf16[512,1024]{1,0:T(8,128)(2,1)S(1)}, bf16[512,1024]{1,0:T(8,128)(2,1)}, u32[]{:S(2)}) copy-start(bf16[512,1024]{1,0:T(8,128)(2,1)} %wo_ref.5) | copy-start | bytes 3145732
  70.2 6.1 %collective-permute-start.5 = (bf16[256,1024]{1,0:T(8,128)(2,1)S(1)}, bf16[256,1024]{1,0:T(8,128)(2,1)S(1)}, u32[]{:S(2)}, u32[]{:S(2)}) collective-permute-start(bf16[256,1024]{1,0:T(8,128)(2,1)S(1)} %get-tuple-element.151.refs_1_), channel_id=1, source_target_pairs={{0,1},{1,0},{2,3},{3,2},{4,5},{5,4},{6,7},{7,6},{8,9},{9,8},{10,11... | collective-permute-start | bytes 1572872 | tf_op jit(solution)/shard_map/ppermute | solution.py:728
  75.6 4.3 %collective-permute-start.2 = (bf16[256,1024]{1,0:T(8,128)(2,1)S(1)}, bf16[256,1024]{1,0:T(8,128)(2,1)S(1)}, u32[]{:S(2)}, u32[]{:S(2)}) collective-permute-start(bf16[256,1024]{1,0:T(8,128)(2,1)S(1)} %get-tuple-element.155.refs_0_), channel_id=1, source_target_pairs={{0,1},{1,0},{2,3},{3,2},{4,5},{5,4},{6,7},{7,6},{8,9},{9,8},{10,11... | collective-permute-start | bytes 1572872 | tf_op jit(solution)/shard_map/ppermute | solution.py:728
  76.2 3.7 %collective-permute-start.3 = (bf16[256,1024]{1,0:T(8,128)(2,1)S(1)}, bf16[256,1024]{1,0:T(8,128)(2,1)S(1)}, u32[]{:S(2)}, u32[]{:S(2)}) collective-permute-start(bf16[256,1024]{1,0:T(8,128)(2,1)S(1)} %get-tuple-element.156.refs_1_), channel_id=1, source_target_pairs={{0,1},{1,0},{2,3},{3,2},{4,5},{5,4},{6,7},{7,6},{8,9},{9,8},{10,11... | collective-permute-start | bytes 1572872 | tf_op jit(solution)/shard_map/ppermute | solution.py:728
  80.0 3.8 %copy-start.15 = (bf16[1024,512]{1,0:T(8,128)(2,1)S(1)}, bf16[1024,512]{1,0:T(8,128)(2,1)}, u32[]{:S(2)}) copy-start(bf16[1024,512]{1,0:T(8,128)(2,1)} %wq_ref.5) | copy-start | bytes 3145732
  80.0 3.8 %copy-start.16 = (bf16[1024,512]{1,0:T(8,128)(2,1)S(1)}, bf16[1024,512]{1,0:T(8,128)(2,1)}, u32[]{:S(2)}) copy-start(bf16[1024,512]{1,0:T(8,128)(2,1)} %wk_ref.5) | copy-start | bytes 3145732
  80.0 3.8 %copy-start.17 = (bf16[1024,512]{1,0:T(8,128)(2,1)S(1)}, bf16[1024,512]{1,0:T(8,128)(2,1)}, u32[]{:S(2)}) copy-start(bf16[1024,512]{1,0:T(8,128)(2,1)} %wv_ref.5) | copy-start | bytes 3145732
  80.0 3.7 %copy-start.20 = (bf16[1024,1024]{1,0:T(8,128)(2,1)S(1)}, bf16[1024,1024]{1,0:T(8,128)(2,1)}, u32[]{:S(2)}) copy-start(bf16[1024,1024]{1,0:T(8,128)(2,1)} %get-tuple-element.140.p_ref) | copy-start | bytes 6291460
  80.0 4.3 %copy-start.25 = (bf16[1024,512]{1,0:T(8,128)(2,1)S(1)}, bf16[1024,512]{1,0:T(8,128)(2,1)}, u32[]{:S(2)}) copy-start(bf16[1024,512]{1,0:T(8,128)(2,1)} %get-tuple-element.139.v_ref) | copy-start | bytes 3145732
  84.3 9.1 %copy-start.2 = (bf16[8,30,64,128]{3,2,1,0:T(8,128)(2,1)S(1)}, bf16[8,30,64,128]{3,2,1,0:T(8,128)(2,1)}, u32[]{:S(2)}) copy-start(bf16[8,30,64,128]{3,2,1,0:T(8,128)(2,1)} %get-tuple-element.136.refs_0_) | copy-start | bytes 11796484
  91.7 13.2 %collective-permute-start.10 = (bf16[256,1024]{1,0:T(8,128)(2,1)S(1)}, bf16[256,1024]{1,0:T(8,128)(2,1)S(1)}, u32[]{:S(2)}, u32[]{:S(2)}) collective-permute-start(bf16[256,1024]{1,0:T(8,128)(2,1)S(1)} %get-tuple-element.175.refs_0_), channel_id=1, source_target_pairs={{0,1},{1,0},{2,3},{3,2},{4,5},{5,4},{6,7},{7,6},{8,9},{9,8},{10,11... | collective-permute-start | bytes 1572872 | tf_op jit(solution)/shard_map/ppermute | solution.py:728
  94.9 29.0 %collective-permute-start.6 = (bf16[4,30,64,128]{3,2,1,0:T(8,128)(2,1)}, bf16[4,30,64,128]{3,2,1,0:T(8,128)(2,1)S(1)}, u32[]{:S(2)}, u32[]{:S(2)}) collective-permute-start(bf16[4,30,64,128]{3,2,1,0:T(8,128)(2,1)} %next_send.12), channel_id=1, source_target_pairs={{0,4},{1,3},{2,6},{3,1},{4,0},{5,7},{6,2},{7,5},{8,12},{9,11},{10,... | collective-permute-start | bytes 5898248 | tf_op jit(solution)/shard_map/ppermute | solution.py:736
  97.0 8.0 %collective-permute-start.11 = (bf16[256,1024]{1,0:T(8,128)(2,1)S(1)}, bf16[256,1024]{1,0:T(8,128)(2,1)S(1)}, u32[]{:S(2)}, u32[]{:S(2)}) collective-permute-start(bf16[256,1024]{1,0:T(8,128)(2,1)S(1)} %get-tuple-element.176.refs_1_), channel_id=1, source_target_pairs={{0,1},{1,0},{2,3},{3,2},{4,5},{5,4},{6,7},{7,6},{8,9},{9,8},{10,11... | collective-permute-start | bytes 1572872 | tf_op jit(solution)/shard_map/ppermute | solution.py:728
  97.0 8.0 %copy-start.27 = (bf16[512,1024]{1,0:T(8,128)(2,1)S(1)}, bf16[512,1024]{1,0:T(8,128)(2,1)}, u32[]{:S(2)}) copy-start(bf16[512,1024]{1,0:T(8,128)(2,1)} %get-tuple-element.173.gm_ref) | copy-start | bytes 3145732
  104.3 6.6 %collective-permute-start.8 = (bf16[256,1024]{1,0:T(8,128)(2,1)S(1)}, bf16[256,1024]{1,0:T(8,128)(2,1)S(1)}, u32[]{:S(2)}, u32[]{:S(2)}) collective-permute-start(bf16[256,1024]{1,0:T(8,128)(2,1)S(1)} %get-tuple-element.182.refs_0_), channel_id=1, source_target_pairs={{0,1},{1,0},{2,3},{3,2},{4,5},{5,4},{6,7},{7,6},{8,9},{9,8},{10,11... | collective-permute-start | bytes 1572872 | tf_op jit(solution)/shard_map/ppermute | solution.py:728
  104.9 6.0 %collective-permute-start.9 = (bf16[256,1024]{1,0:T(8,128)(2,1)S(1)}, bf16[256,1024]{1,0:T(8,128)(2,1)S(1)}, u32[]{:S(2)}, u32[]{:S(2)}) collective-permute-start(bf16[256,1024]{1,0:T(8,128)(2,1)S(1)} %get-tuple-element.183.refs_1_), channel_id=1, source_target_pairs={{0,1},{1,0},{2,3},{3,2},{4,5},{5,4},{6,7},{7,6},{8,9},{9,8},{10,11... | collective-permute-start | bytes 1572872 | tf_op jit(solution)/shard_map/ppermute | solution.py:728
  114.1 8.2 %copy-start.4 = (bf16[8,18,64,128]{3,2,1,0:T(8,128)(2,1)S(1)}, bf16[8,18,64,128]{3,2,1,0:T(8,128)(2,1)}, u32[]{:S(2)}) copy-start(bf16[8,18,64,128]{3,2,1,0:T(8,128)(2,1)} %get-tuple-element.166.refs_0_) | copy-start | bytes 7077892
  118.7 29.2 %collective-permute-start.17 = (bf16[8,9,64,128]{3,2,1,0:T(8,128)(2,1)S(1)}, bf16[8,9,64,128]{3,2,1,0:T(8,128)(2,1)S(1)}, u32[]{:S(2)}, u32[]{:S(2)}) collective-permute-start(bf16[8,9,64,128]{3,2,1,0:T(8,128)(2,1)S(1)} %get-tuple-element.191), channel_id=1, source_target_pairs={{0,2},{1,5},{2,0},{3,7},{4,6},{5,1},{6,4},{7,3},{8,10},{9,13},{10,... | collective-permute-start | bytes 3538952 | tf_op jit(solution)/shard_map/ppermute | solution.py:736
  120.2 26.0 %collective-permute-start.14 = (bf16[8,8,64,128]{3,2,1,0:T(8,128)(2,1)S(1)}, bf16[8,8,64,128]{3,2,1,0:T(8,128)(2,1)S(1)}, u32[]{:S(2)}, u32[]{:S(2)}) collective-permute-start(bf16[8,8,64,128]{3,2,1,0:T(8,128)(2,1)S(1)} %get-tuple-element.181), channel_id=1, source_target_pairs={{0,2},{1,5},{2,0},{3,7},{4,6},{5,1},{6,4},{7,3},{8,10},{9,13},{10,... | collective-permute-start | bytes 3145736 | tf_op jit(solution)/shard_map/ppermute | solution.py:736
  122.5 42.6 %collective-permute-start.16 = (bf16[4,18,64,128]{3,2,1,0:T(8,128)(2,1)S(1)}, bf16[4,18,64,128]{3,2,1,0:T(8,128)(2,1)S(1)}, u32[]{:S(2)}, u32[]{:S(2)}) collective-permute-start(bf16[4,18,64,128]{3,2,1,0:T(8,128)(2,1)S(1)} %next_send.13), channel_id=1, source_target_pairs={{0,2},{1,5},{2,0},{3,7},{4,6},{5,1},{6,4},{7,3},{8,10},{9,13},{10,... | collective-permute-start | bytes 3538952 | tf_op jit(solution)/shard_map/ppermute | solution.py:736
  127.1 53.4 %collective-permute-start.22 = (bf16[2,30,64,128]{3,2,1,0:T(8,128)(2,1)S(1)}, bf16[2,30,64,128]{3,2,1,0:T(8,128)(2,1)S(1)}, u32[]{:S(2)}, u32[]{:S(2)}) collective-permute-start(bf16[2,30,64,128]{3,2,1,0:T(8,128)(2,1)S(1)} %next_send.14), channel_id=1, source_target_pairs={{0,16},{1,17},{2,18},{3,19},{4,20},{5,21},{6,22},{7,23},{8,24},{9,... | collective-permute-start | bytes 2949128 | tf_op jit(solution)/shard_map/ppermute | solution.py:736
  130.2 16.0 %copy-start.12 = (bf16[8,8,64,128]{3,2,1,0:T(8,128)(2,1)S(1)}, bf16[8,8,64,128]{3,2,1,0:T(8,128)(2,1)}, u32[]{:S(2)}) copy-start(bf16[8,8,64,128]{3,2,1,0:T(8,128)(2,1)} %get-tuple-element.197.refs_0_) | copy-start | bytes 3145732
  136.0 11.9 %copy-start.6 = (bf16[8,9,64,128]{3,2,1,0:T(8,128)(2,1)S(1)}, bf16[8,9,64,128]{3,2,1,0:T(8,128)(2,1)}, u32[]{:S(2)}) copy-start(bf16[8,9,64,128]{3,2,1,0:T(8,128)(2,1)} %get-tuple-element.199.refs_0_) | copy-start | bytes 3538948
  146.3 33.4 %collective-permute-start.15 = (bf16[4,8,64,128]{3,2,1,0:T(8,128)(2,1)S(1)}, bf16[4,8,64,128]{3,2,1,0:T(8,128)(2,1)S(1)}, u32[]{:S(2)}, u32[]{:S(2)}) collective-permute-start(bf16[4,8,64,128]{3,2,1,0:T(8,128)(2,1)S(1)} %next_send.15), channel_id=1, source_target_pairs={{0,8},{1,9},{2,10},{3,11},{4,12},{5,13},{6,14},{7,15},{8,0},{9,1},... | collective-permute-start | bytes 1572872 | tf_op jit(solution)/shard_map/ppermute | solution.py:736
  148.1 32.2 %collective-permute-start.20 = (bf16[4,9,64,128]{3,2,1,0:T(8,128)(2,1)S(1)}, bf16[4,9,64,128]{3,2,1,0:T(8,128)(2,1)S(1)}, u32[]{:S(2)}, u32[]{:S(2)}) collective-permute-start(bf16[4,9,64,128]{3,2,1,0:T(8,128)(2,1)S(1)} %next_send.16), channel_id=1, source_target_pairs={{0,4},{1,3},{2,6},{3,1},{4,0},{5,7},{6,2},{7,5},{8,12},{9,11},{10,... | collective-permute-start | bytes 1769480 | tf_op jit(solution)/shard_map/ppermute | solution.py:736
  148.9 55.2 %collective-permute-start.12 = (bf16[512,1024]{1,0:T(8,128)(2,1)S(1)}, bf16[512,1024]{1,0:T(8,128)(2,1)S(1)}, u32[]{:S(2)}, u32[]{:S(2)}) collective-permute-start(bf16[512,1024]{1,0:T(8,128)(2,1)S(1)} %get-tuple-element.210.refs_0_), channel_id=1, source_target_pairs={{0,1},{1,0},{2,3},{3,2},{4,5},{5,4},{6,7},{7,6},{8,9},{9,8},{10,11... | collective-permute-start | bytes 3145736 | tf_op jit(solution)/shard_map/ppermute | solution.py:728
  165.1 39.0 %collective-permute-start.13 = (bf16[512,1024]{1,0:T(8,128)(2,1)S(1)}, bf16[512,1024]{1,0:T(8,128)(2,1)S(1)}, u32[]{:S(2)}, u32[]{:S(2)}) collective-permute-start(bf16[512,1024]{1,0:T(8,128)(2,1)S(1)} %get-tuple-element.211.refs_1_), channel_id=1, source_target_pairs={{0,1},{1,0},{2,3},{3,2},{4,5},{5,4},{6,7},{7,6},{8,9},{9,8},{10,11... | collective-permute-start | bytes 3145736 | tf_op jit(solution)/shard_map/ppermute | solution.py:728
  179.7 14.9 %collective-permute-start.19 = (bf16[2,18,64,128]{3,2,1,0:T(8,128)(2,1)S(1)}, bf16[2,18,64,128]{3,2,1,0:T(8,128)(2,1)S(1)}, u32[]{:S(2)}, u32[]{:S(2)}) collective-permute-start(bf16[2,18,64,128]{3,2,1,0:T(8,128)(2,1)S(1)} %next_send.17), channel_id=1, source_target_pairs={{0,4},{1,3},{2,6},{3,1},{4,0},{5,7},{6,2},{7,5},{8,12},{9,11},{10,... | collective-permute-start | bytes 1769480 | tf_op jit(solution)/shard_map/ppermute | solution.py:736
  180.3 5.5 %copy-start.11 = (bf16[4,30,64,128]{3,2,1,0:T(8,128)(2,1)S(1)}, bf16[4,30,64,128]{3,2,1,0:T(8,128)(2,1)}, u32[]{:S(2)}) copy-start(bf16[4,30,64,128]{3,2,1,0:T(8,128)(2,1)} %copy-done.9) | copy-start | bytes 5898244
  180.5 14.1 %collective-permute-start.21 = (bf16[2,9,64,128]{3,2,1,0:T(8,128)(2,1)S(1)}, bf16[2,9,64,128]{3,2,1,0:T(8,128)(2,1)S(1)}, u32[]{:S(2)}, u32[]{:S(2)}) collective-permute-start(bf16[2,9,64,128]{3,2,1,0:T(8,128)(2,1)S(1)} %next_send.19), channel_id=1, source_target_pairs={{0,8},{1,9},{2,10},{3,11},{4,12},{5,13},{6,14},{7,15},{8,0},{9,1},... | collective-permute-start | bytes 884744 | tf_op jit(solution)/shard_map/ppermute | solution.py:736
  180.5 16.7 %collective-permute-start.18 = (bf16[2,8,64,128]{3,2,1,0:T(8,128)(2,1)S(1)}, bf16[2,8,64,128]{3,2,1,0:T(8,128)(2,1)S(1)}, u32[]{:S(2)}, u32[]{:S(2)}) collective-permute-start(bf16[2,8,64,128]{3,2,1,0:T(8,128)(2,1)S(1)} %next_send.18), channel_id=1, source_target_pairs={{0,16},{1,17},{2,18},{3,19},{4,20},{5,21},{6,22},{7,23},{8,24},{9,... | collective-permute-start | bytes 786440 | tf_op jit(solution)/shard_map/ppermute | solution.py:736
  194.5 21.2 %collective-permute-start.25 = (bf16[1,30,64,128]{3,2,1,0:T(8,128)(2,1)S(1)}, bf16[1,30,64,128]{3,2,1,0:T(8,128)(2,1)S(1)}, u32[]{:S(2)}, u32[]{:S(2)}) collective-permute-start(bf16[1,30,64,128]{3,2,1,0:T(8,128)(2,1)S(1)} %next_send.20), channel_id=1, source_target_pairs={{0,8},{1,9},{2,10},{3,11},{4,12},{5,13},{6,14},{7,15},{8,0},{9,1},... | collective-permute-start | bytes 1474568 | tf_op jit(solution)/shard_map/ppermute | solution.py:736
  194.8 17.2 %collective-permute-start.26 = (bf16[1,18,64,128]{3,2,1,0:T(8,128)(2,1)S(1)}, bf16[1,18,64,128]{3,2,1,0:T(8,128)(2,1)S(1)}, u32[]{:S(2)}, u32[]{:S(2)}) collective-permute-start(bf16[1,18,64,128]{3,2,1,0:T(8,128)(2,1)S(1)} %next_send.22), channel_id=1, source_target_pairs={{0,16},{1,17},{2,18},{3,19},{4,20},{5,21},{6,22},{7,23},{8,24},{9,... | collective-permute-start | bytes 884744 | tf_op jit(solution)/shard_map/ppermute | solution.py:736
  197.3 6.8 %copy-start.8 = (bf16[1024,1024]{1,0:T(8,128)(2,1)S(1)}, bf16[1024,1024]{1,0:T(8,128)(2,1)}, u32[]{:S(2)}) copy-start(bf16[1024,1024]{1,0:T(8,128)(2,1)} %get-tuple-element.124.mid_ref) | copy-start | bytes 6291460
  197.3 5.0 %collective-permute-start.23 = (bf16[1,8,64,128]{3,2,1,0:T(8,128)(2,1)S(1)}, bf16[1,8,64,128]{3,2,1,0:T(8,128)(2,1)S(1)}, u32[]{:S(2)}, u32[]{:S(2)}) collective-permute-start(bf16[1,8,64,128]{3,2,1,0:T(8,128)(2,1)S(1)} %next_send.23), channel_id=1, source_target_pairs={{0,4},{1,3},{2,6},{3,1},{4,0},{5,7},{6,2},{7,5},{8,12},{9,11},{10,... | collective-permute-start | bytes 393224 | tf_op jit(solution)/shard_map/ppermute | solution.py:736
  202.4 14.4 %collective-permute-start.24 = (bf16[1,9,64,128]{3,2,1,0:T(8,128)(2,1)S(1)}, bf16[1,9,64,128]{3,2,1,0:T(8,128)(2,1)S(1)}, u32[]{:S(2)}, u32[]{:S(2)}) collective-permute-start(bf16[1,9,64,128]{3,2,1,0:T(8,128)(2,1)S(1)} %next_send.21), channel_id=1, source_target_pairs={{0,16},{1,17},{2,18},{3,19},{4,20},{5,21},{6,22},{7,23},{8,24},{9,... | collective-permute-start | bytes 442376 | tf_op jit(solution)/shard_map/ppermute | solution.py:736
  (16 other events, 39.7 us)
where the time goes:
time: 218 us
  Pallas kernels  120 us (55%)
  waiting for transfers between devices  63.8 us (29%)
  starting transfers between devices  27.8 us (13%)
  local copies, waits for them, and re-layouts  5.29 us (2%)
    pallas_call x33, Pallas kernels, run(): kernel(*(pltpu.with_memory_space_constraint(arg, pltpu.HBM) if n - scalar...  120 us
    ppermute x16, waiting for transfers between devices, hop_swap(): return lax.ppermute(array, ('dp', 'tensor'), pairs)  63.7 us
    ppermute x16, starting transfers between devices, hop_swap(): return lax.ppermute(array, ('dp', 'tensor'), pairs)  25.3 us
    unnamed x74, local copies, waits for them, and re-layouts  5.29 us
  transfers between devices with their start and end apart: 27, of which 9 were waited for; matrix products, arithmetic and copies ran while one was open for 0% of the time, Pallas kernels for 37%

commit v1 on v0

--- a/solution.py
+++ b/solution.py
@@ -17,6 +17,7 @@
 HALVES = 2
 PARTS = 2
 COST = 1e-6
+SLACK = {}
 
 epsilon = 1e-05
 f32 = jnp.float32
@@ -53,7 +54,7 @@
         input_output_aliases=aliases or {},
         compiler_params=pltpu.CompilerParams(vmem_limit_bytes=vmem * MIB),
         cost_estimate=pl.CostEstimate(
-            flops=int(cost[0] * COST), bytes_accessed=int(cost[1] * COST), transcendentals=0
+            flops=int(cost[0] * COST + SLACK.get(name, 0)), bytes_accessed=0, transcendentals=0
         ),
         name=name,
     )
@@ -86,17 +87,17 @@
 
 
 def exchanged(index, size):
+    low, high = (1, 4) if size >= 16 else (1, 0)
     if size < 4:
         return index
-    return index // 4 * 4 + index % 2 * 2 + index // 2 % 2
+    moved = low | high
+    kept = index & ~(3 * moved)
+    return kept | (index & moved) << 1 | index >> 1 & moved
 
 
 def relative(place_ref, g, size):
     apart = g ^ place_ref[0]
-    if size < 4:
-        return apart
-    other = (apart & ~3) | ((apart & 1) << 1) | ((apart >> 1) & 1)
-    return jnp.where(place_ref[1] == 1, other, apart)
+    return jnp.where(place_ref[1] == 1, exchanged(apart, size), apart)
 
 
 def put_transposed(ref, place_ref, values):
@@ -807,9 +808,9 @@
 
 
 STEPS = (
-    "attn", "seed", "mid", "H0", "H1", "ntA", "ntB", "mbA", "mbB", "abA", "h:0", "abB", "igA",
-    "QK", "igB", "VO", "h:1", "h:0", "down", "h:QK", "h:VO", "h:1", "h:QK", "h:VO", "h:0", "h:VO",
-    "h:1", "h:QK", "e:QK", "bo", "e:1", "e:0", "e:VO",
+    "attn", "seed", "mid", "H0", "H1", "ntA", "ntB", "mbA", "mbB", "abA", "h:0", "abB", "QK",
+    "igA", "h:1", "igB", "VO", "h:0", "h:QK", "h:1", "h:VO", "down", "h:QK", "h:VO", "h:0", "h:VO",
+    "h:1", "bo", "e:0", "h:QK", "e:1", "e:VO", "e:QK",
 )
 
 
@@ -992,9 +993,9 @@
         return [1 << k for k in start if k < n_bits] + [1 << k for k in range(n_bits) if k not in start]
 
     bits_of = {
-        0: order(0, 1, 3, 2),
+        0: order(0, 1, 2, 3),
         1: order(2, 0, 1, 3),
-        "qk": order(0, 2, 3, 1),
+        "qk": order(2, 0, 1, 3),
         "vo": order(0, 1, 2, 3),
     }
 

time: 218 us -> 195 us (0.89)
  waiting for transfers between devices: 63.8 us -> 40 us
  starting transfers between devices: 27.8 us -> 24.7 us
    ppermute x16, waiting for transfers between devices: 63.7 us -> 40 us  [hop_swap(): return lax.ppermute(array, ('dp', 'tensor'), pairs)]
    ppermute x16, starting transfers between devices: 25.3 us -> 20.8 us  [hop_swap(): return lax.ppermute(array, ('dp', 'tensor'), pairs)]
  transfers between devices with their start and end apart: 27 -> 27, of which waited for: 9 -> 11; matrix products, arithmetic and copies ran while one was open for 0% -> 0% of each run, Pallas kernels for 37% -> 42%
where the time goes in v1:
time: 195 us; the launch traced here: 193 us
  Pallas kernels  121 us (62%)
  waiting for transfers between devices  40 us (21%)
  starting transfers between devices  24.7 us (13%)
  local copies, waits for them, and re-layouts  5.75 us (3%)
    pallas_call x33, Pallas kernels, run(): kernel(*(pltpu.with_memory_space_constraint(arg, pltpu.HBM) if n - scalar...  121 us
    ppermute x16, waiting for transfers between devices, hop_swap(): return lax.ppermute(array, ('dp', 'tensor'), pairs)  40 us
    ppermute x16, starting transfers between devices, hop_swap(): return lax.ppermute(array, ('dp', 'tensor'), pairs)  20.8 us
    unnamed x74, local copies, waits for them, and re-layouts  5.75 us
    ppermute x11, starting transfers between devices, swap(): return lax.ppermute(array, axis, [(i, i ^ bit) for i in range(size)])  3.9 us
  transfers between devices with their start and end apart: 27, of which 11 were waited for; matrix products, arithmetic and copies ran while one was open for 0% of the time, Pallas kernels for 42%

profile of v1, /device:TPU:0, one launch (start us, length us, event | category | flops | bytes accessed | tf_op | source)
XLA Modules:
  0.0 193.0 jit_solution(6972852777460655964)
XLA Ops:
  1.3 12.2 %attention_forward.1 = (bf16[1024,512]{1,0:T(8,128)(2,1)}, bf16[1024,512]{1,0:T(8,128)(2,1)}, bf16[1024,512]{1,0:T(8,128)(2,1)}, bf16[1024,512]{1,0:T(8,128)(2,1...) custom-call(bf16[1024,1024]{1,0:T(8,128)(2,1)} %x_ref.9, bf16[1024]{0:T(1024)(128)(2,1)S(1)} %copy-done.29, ...), custom_call_target="tpu_custom_call" | custom-call | flops 4294 | tf_op jit(solution)/shard_map/attention_forward/pallas_call | solution.py:63
  14.1 6.2 %seed_rows.1 = (bf16[1024,1024]{1,0:T(8,128)(2,1)S(1)}, bf16[16,64,1024]{2,1,0:T(8,128)(2,1)S(1)}, bf16[16,64,1024]{2,1,0:T(8,128)(2,1)}) custom-call(s32[2]{0:T(128)S(1)} %copy-done.36, s32[2]{0:T(128)S(1)} %pad_add_fusion.me_ref, bf16[1024,1024]{1,0:T(8,128)(2,1)} %cot_ref, bf16[1024,1024]{1,0:T(8,128)(2,1)} %x_ref.9, bf16[1024]{0:T(1024)(128)(2,1)S(1)} %copy-done.30), custom_call_target="tpu_custom_call" | custom-call | flops 4 | tf_op jit(solution)/shard_map/seed_rows/pallas_call | solution.py:63
  20.3 5.7 %middle_rows.1 = (bf16[1024,1024]{1,0:T(8,128)(2,1)}, bf16[1024,1024]{1,0:T(8,128)(2,1)S(1)}, bf16[16,64,1024]{2,1,0:T(8,128)(2,1)S(1)}) custom-call(s32[2]{0:T(128)S(1)} %pad_add_fusion.me_ref, bf16[1024,1024]{1,0:T(8,128)(2,1)S(1)} %copy-done.3, bf16[1024,1024]{1,0:T(8,128)(2,1)} %get-tuple-element.120.own_ref, ...), custom_call_target="tpu_custom_call" | custom-call | flops 8 | tf_op jit(solution)/shard_map/middle_rows/pallas_call | solution.py:63
  26.0 21.0 %hidden_units.2 = (bf16[1024,2048]{1,0:T(8,128)(2,1)S(1)}, bf16[1024,2048]{1,0:T(8,128)(2,1)S(1)}, bf16[1024,2048]{1,0:T(8,128)(2,1)S(1)}, bf16[8,30,64,128]{3,2,1,0:T(8,128)(2,1)}, bf16[8,30,64,128]{3,2,1,0:T(8,128)(2,1)}) custom-call(bf16[1024,1024]{1,0:T(8,128)(2,1)S(1)} %get-tuple-element.131.refs_0_, ...), custom_call_target="tpu_custom_call" | custom-call | flops 16106 | tf_op jit(solution)/shard_map/hidden_units/pallas_call | solution.py:63
  47.0 2.5 %collective-permute-start.5 = (bf16[8,30,64,128]{3,2,1,0:T(8,128)(2,1)}, bf16[8,30,64,128]{3,2,1,0:T(8,128)(2,1)S(1)}, u32[]{:S(2)}, u32[]{:S(2)}) collective-permute-start(bf16[8,30,64,128]{3,2,1,0:T(8,128)(2,1)} %get-tuple-element.130), channel_id=1, source_target_pairs={{0,2},{1,5},{2,0},{3,7},{4,6},{5,1},{6,4},{7,3},{8,10},{9,13},{10,... | collective-permute-start | bytes 11796488 | tf_op jit(solution)/shard_map/ppermute | solution.py:737
  49.5 13.5 %hidden_units.3 = (bf16[1024,2048]{1,0:T(8,128)(2,1)S(1)}, bf16[1024,2048]{1,0:T(8,128)(2,1)S(1)}, bf16[1024,2048]{1,0:T(8,128)(2,1)S(1)}, bf16[8,18,64,128]{3,2,1,0:T(8,128)(2,1)}, bf16[8,18,64,128]{3,2,1,0:T(8,128)(2,1)}) custom-call(bf16[1024,1024]{1,0:T(8,128)(2,1)S(1)} %get-tuple-element.131.refs_0_, ...), custom_call_target="tpu_custom_call", output_to_operand_aliasing={{0}: (7, {}), {1}: (8, {}), {2}: (9, {})} | custom-call | flops 9663 | tf_op jit(solution)/shard_map/hidden_units/pallas_call | solution.py:63
  63.0 2.0 %copy-done.12 = bf16[1024,2048]{1,0:T(8,128)(2,1)} copy-done((bf16[1024,2048]{1,0:T(8,128)(2,1)}, bf16[1024,2048]{1,0:T(8,128)(2,1)S(1)}, u32[]{:S(2)}) %copy-start.12) | copy-done | bytes 4194328
  65.0 1.6 collective-permute-start.8
  66.6 5.3 %normed_two_back.2 = (bf16[256,1024]{1,0:T(8,128)(2,1)S(1)}, bf16[256,1024]{1,0:T(8,128)(2,1)S(1)}) custom-call(bf16[1024,2048]{1,0:T(8,128)(2,1)S(1)} %get-tuple-element.145.gg_ref, bf16[1024,2048]{1,0:T(8,128)(2,1)S(1)} %get-tuple-element.143.gu_ref, bf16[1024,2048]{1,0:T(8,128)(2,1)S(1)} %copy-done, bf16[1024,2048]{1,0:T(8,128)(2,1)S(1)} %copy-done.1), custom_call_target="tpu_custom_call" | custom-call | flops 4294 | tf_op jit(solution)/shard_map/normed_two_back/pallas_call | solution.py:63
  71.9 1.0 collective-permute-start.3
  73.0 5.4 %normed_two_back.3 = (bf16[256,1024]{1,0:T(8,128)(2,1)S(1)}, bf16[256,1024]{1,0:T(8,128)(2,1)S(1)}) custom-call(bf16[1024,2048]{1,0:T(8,128)(2,1)S(1)} %get-tuple-element.145.gg_ref, bf16[1024,2048]{1,0:T(8,128)(2,1)S(1)} %get-tuple-element.143.gu_ref, bf16[1024,2048]{1,0:T(8,128)(2,1)S(1)} %copy-done, bf16[1024,2048]{1,0:T(8,128)(2,1)S(1)} %copy-done.1), custom_call_target="tpu_custom_call" | custom-call | flops 4294 | tf_op jit(solution)/shard_map/normed_two_back/pallas_call | solution.py:63
  79.0 3.6 %middle_backward.2 = (bf16[16,64,1024]{2,1,0:T(8,128)(2,1)}, bf16[1024,512]{1,0:T(8,128)(2,1)}, bf16[512,1024]{1,0:T(8,128)(2,1)}, f32[1,1024]{1,0:T(1,128)}) custom-call(s32[2]{0:T(128)S(1)} %pad_add_fusion.me_ref, bf16[1024,1024]{1,0:T(8,128)(2,1)S(1)} %copy-done.7, bf16[1024,1024]{1,0:T(8,128)(2,1)S(1)} %get-tuple-element.128.refs_2_.seed_ref, ...), custom_call_target="tpu_custom_call" | custom-call | flops 536 | tf_op jit(solution)/shard_map/middle_backward/pallas_call | solution.py:63
  82.8 3.7 %middle_backward.3 = (bf16[16,64,1024]{2,1,0:T(8,128)(2,1)}, bf16[1024,512]{1,0:T(8,128)(2,1)}, bf16[512,1024]{1,0:T(8,128)(2,1)}, f32[1,1024]{1,0:T(1,128)}) custom-call(s32[2]{0:T(128)S(1)} %pad_add_fusion.me_ref, bf16[1024,1024]{1,0:T(8,128)(2,1)S(1)} %copy-done.7, ...), custom_call_target="tpu_custom_call", output_to_operand_aliasing={{0}: (9, {}), {1}: (10, {})} | custom-call | flops 536 | tf_op jit(solution)/shard_map/middle_backward/pallas_call | solution.py:63
  87.1 7.4 %attention_backward.2 = (bf16[1024,1536]{1,0:T(8,128)(2,1)S(1)}, bf16[256,1024]{1,0:T(8,128)(2,1)S(1)}, bf16[256,1024]{1,0:T(8,128)(2,1)S(1)}) custom-call(bf16[1024,512]{1,0:T(8,128)(2,1)S(1)} %copy-done.23, bf16[1024,512]{1,0:T(8,128)(2,1)S(1)} %copy-done.24, bf16[1024,512]{1,0:T(8,128)(2,1)S(1)} %copy-done.25, bf16[1024,1024]{1,0:T(8,128)(2,1)S(1)} %copy-done.20, ...), custom_call_target="tpu_custom_call" | custom-call | flops 1610 | tf_op jit(solution)/shard_map/attention_backward/pallas_call | solution.py:63
  94.5 1.5 next_send.12
  96.0 1.0 collective-permute-start.14
  97.6 8.1 %attention_backward.3 = (bf16[1024,1536]{1,0:T(8,128)(2,1)S(1)}, bf16[256,1024]{1,0:T(8,128)(2,1)}, bf16[256,1024]{1,0:T(8,128)(2,1)S(1)}) custom-call(bf16[1024,512]{1,0:T(8,128)(2,1)S(1)} %copy-done.23, bf16[1024,512]{1,0:T(8,128)(2,1)S(1)} %copy-done.24, bf16[1024,512]{1,0:T(8,128)(2,1)S(1)} %copy-done.25, ...), custom_call_target="tpu_custom_call", output_to_operand_aliasing={{0}: (8, {})} | custom-call | flops 1610 | tf_op jit(solution)/shard_map/attention_backward/pallas_call | solution.py:63
  106.3 3.5 %query_key_grads.1 = (bf16[8,8,64,128]{3,2,1,0:T(8,128)(2,1)}, bf16[8,8,64,128]{3,2,1,0:T(8,128)(2,1)S(1)}) custom-call(bf16[16,64,1024]{2,1,0:T(8,128)(2,1)S(1)} %copy-done.18, bf16[1024,1536]{1,0:T(8,128)(2,1)S(1)} %get-tuple-element.189.right_ref), custom_call_target="tpu_custom_call" | custom-call | flops 2147 | tf_op jit(solution)/shard_map/query_key_grads/pallas_call | solution.py:63
  109.8 1.6 collective-permute-start.13
  111.4 2.3 %input_grad.2 = (bf16[1024,1024]{1,0:T(8,128)(2,1)}, f32[1,1024]{1,0:T(1,128)}) custom-call(bf16[1024,1024]{1,0:T(8,128)(2,1)S(1)} %copy-done.3, bf16[512,1024]{1,0:T(8,128)(2,1)S(1)} %copy-done.27, bf16[1024]{0:T(1024)(128)(2,1)S(1)} %copy-done.30, bf16[256,1024]{1,0:T(8,128)(2,1)S(1)} %get-tuple-element.177.refs_0_, ...), custom_call_target="tpu_custom_call" | custom-call | flops 5 | tf_op jit(solution)/shard_map/input_grad/pallas_call | solution.py:63
  113.7 5.5 %collective-permute-done.8.refs_1_ = bf16[8,18,64,128]{3,2,1,0:T(8,128)(2,1)S(1)} collective-permute-done((bf16[8,18,64,128]{3,2,1,0:T(8,128)(2,1)}, bf16[8,18,64,128]{3,2,1,0:T(8,128)(2,1)S(1)}, u32[]{:S(2)}, u32[]{:S(2)}) %collective-permute-start.8) | collective-permute-done | bytes 2359328 | tf_op jit(solution)/shard_map/ppermute | solution.py:737
  119.7 0.8 copy-done.28
  120.5 3.6 %input_grad.3 = (bf16[1024,1024]{1,0:T(8,128)(2,1)}, f32[1,1024]{1,0:T(1,128)}) custom-call(bf16[1024,1024]{1,0:T(8,128)(2,1)S(1)} %copy-done.3, bf16[512,1024]{1,0:T(8,128)(2,1)S(1)} %copy-done.28, bf16[1024]{0:T(1024)(128)(2,1)S(1)} %copy-done.30, bf16[256,1024]{1,0:T(8,128)(2,1)} %get-tuple-element.183.refs_0_, ...), custom_call_target="tpu_custom_call", output_to_operand_aliasing={{0}: (7, {})} | custom-call | flops 5 | tf_op jit(solution)/shard_map/input_grad/pallas_call | solution.py:63
  124.2 0.7 copy-done.35
  124.9 4.4 %value_out_grads.1 = (bf16[8,9,64,128]{3,2,1,0:T(8,128)(2,1)}, bf16[8,9,64,128]{3,2,1,0:T(8,128)(2,1)S(1)}) custom-call(bf16[16,64,1024]{2,1,0:T(8,128)(2,1)S(1)} %copy-done.19, bf16[1024,1536]{1,0:T(8,128)(2,1)S(1)} %get-tuple-element.189.right_ref, bf16[16,64,1024]{2,1,0:T(8,128)(2,1)S(1)} %copy-done.22, bf16[1024,512]{1,0:T(8,128)(2,1)S(1)} %copy-done.26, ...), custom_call_target="tpu_custom_call" | custom-call | flops 2147 | tf_op jit(solution)/shard_map/value_out_grads/pallas_call | solution.py:63
  129.3 1.2 collective-permute-start.11
  130.9 0.9 copy-done.9
  131.8 1.4 collective-permute-start.21
  133.1 8.6 %collective-permute-done.13.refs_1_ = bf16[8,8,64,128]{3,2,1,0:T(8,128)(2,1)S(1)} collective-permute-done((bf16[8,8,64,128]{3,2,1,0:T(8,128)(2,1)S(1)}, bf16[8,8,64,128]{3,2,1,0:T(8,128)(2,1)S(1)}, u32[]{:S(2)}, u32[]{:S(2)}) %collective-permute-start.13) | collective-permute-done | bytes 1048608 | tf_op jit(solution)/shard_map/ppermute | solution.py:737
  142.3 6.2 %collective-permute-done.11.refs_1_ = bf16[8,9,64,128]{3,2,1,0:T(8,128)(2,1)S(1)} collective-permute-done((bf16[8,9,64,128]{3,2,1,0:T(8,128)(2,1)S(1)}, bf16[8,9,64,128]{3,2,1,0:T(8,128)(2,1)S(1)}, u32[]{:S(2)}, u32[]{:S(2)}) %collective-permute-start.11) | collective-permute-done | bytes 1179680 | tf_op jit(solution)/shard_map/ppermute | solution.py:737
  148.7 0.8 collective-permute-start.18
  149.5 5.8 %hidden_down.1 = (bf16[512,1024]{1,0:T(8,128)(2,1)S(1)}, bf16[512,1024]{1,0:T(8,128)(2,1)S(1)}) custom-call(bf16[1024,2048]{1,0:T(8,128)(2,1)S(1)} %copy-done.13, bf16[2048,1024]{1,0:T(8,128)(2,1)S(1)} %copy-done.5), custom_call_target="tpu_custom_call" | custom-call | flops 4294 | tf_op jit(solution)/shard_map/hidden_down/pallas_call | solution.py:63
  155.9 1.9 collective-permute-done.19.refs_2_
  158.0 1.4 collective-permute-done.18.refs_2_
  159.6 2.6 %collective-permute-start.20 = (bf16[2,9,64,128]{3,2,1,0:T(8,128)(2,1)S(1)}, bf16[2,9,64,128]{3,2,1,0:T(8,128)(2,1)S(1)}, u32[]{:S(2)}, u32[]{:S(2)}) collective-permute-start(bf16[2,9,64,128]{3,2,1,0:T(8,128)(2,1)S(1)} %next_send.19), channel_id=1, source_target_pairs={{0,8},{1,17},{2,10},{3,19},{4,12},{5,21},{6,14},{7,23},{8,0},{9,25... | collective-permute-start | bytes 884744 | tf_op jit(solution)/shard_map/ppermute | solution.py:737
  162.1 0.7 collective-permute-done.21.refs_3_
  163.1 2.2 %collective-permute-start.23 = (bf16[1,30,64,128]{3,2,1,0:T(8,128)(2,1)S(1)}, bf16[1,30,64,128]{3,2,1,0:T(8,128)(2,1)S(1)}, u32[]{:S(2)}, u32[]{:S(2)}) collective-permute-start(bf16[1,30,64,128]{3,2,1,0:T(8,128)(2,1)S(1)} %next_send.20), channel_id=1, source_target_pairs={{0,16},{1,9},{2,18},{3,11},{4,20},{5,13},{6,22},{7,15},{8,24},{9,1... | collective-permute-start | bytes 1474568 | tf_op jit(solution)/shard_map/ppermute | solution.py:737
  165.2 9.9 %collective-permute-done.20.refs_3_ = bf16[2,9,64,128]{3,2,1,0:T(8,128)(2,1)S(1)} collective-permute-done((bf16[2,9,64,128]{3,2,1,0:T(8,128)(2,1)S(1)}, bf16[2,9,64,128]{3,2,1,0:T(8,128)(2,1)S(1)}, u32[]{:S(2)}, u32[]{:S(2)}) %collective-permute-start.20) | collective-permute-done | bytes 294944 | tf_op jit(solution)/shard_map/ppermute | solution.py:737
  175.5 2.9 %collective-permute-start.25 = (bf16[1,9,64,128]{3,2,1,0:T(8,128)(2,1)S(1)}, bf16[1,9,64,128]{3,2,1,0:T(8,128)(2,1)S(1)}, u32[]{:S(2)}, u32[]{:S(2)}) collective-permute-start(bf16[1,9,64,128]{3,2,1,0:T(8,128)(2,1)S(1)} %next_send.21), channel_id=1, source_target_pairs={{0,16},{1,9},{2,18},{3,11},{4,20},{5,13},{6,22},{7,15},{8,24},{9,1... | collective-permute-start | bytes 442376 | tf_op jit(solution)/shard_map/ppermute | solution.py:737
  178.4 1.9 block_output.1
  180.3 1.1 hidden_grads_out.2
  181.6 2.8 %collective-permute-start.24 = (bf16[1,8,64,128]{3,2,1,0:T(8,128)(2,1)S(1)}, bf16[1,8,64,128]{3,2,1,0:T(8,128)(2,1)S(1)}, u32[]{:S(2)}, u32[]{:S(2)}) collective-permute-start(bf16[1,8,64,128]{3,2,1,0:T(8,128)(2,1)S(1)} %next_send.23), channel_id=1, source_target_pairs={{0,16},{1,9},{2,18},{3,11},{4,20},{5,13},{6,22},{7,15},{8,24},{9,1... | collective-permute-start | bytes 393224 | tf_op jit(solution)/shard_map/ppermute | solution.py:737
  184.4 1.8 collective-permute-done.26.refs_4_
  186.2 1.4 hidden_grads_out.3
  187.6 1.8 collective-permute-done.25.refs_4_
  189.4 0.8 head_grads_out.2
  190.2 2.0 %collective-permute-done.24.refs_4_ = bf16[1,8,64,128]{3,2,1,0:T(8,128)(2,1)S(1)} collective-permute-done((bf16[1,8,64,128]{3,2,1,0:T(8,128)(2,1)S(1)}, bf16[1,8,64,128]{3,2,1,0:T(8,128)(2,1)S(1)}, u32[]{:S(2)}, u32[]{:S(2)}) %collective-permute-start.24) | collective-permute-done | bytes 131104 | tf_op jit(solution)/shard_map/ppermute | solution.py:737
  192.2 0.7 head_grads_out.3
  (114 shorter events, 6.9 us)
Async XLA Ops:
  1.3 12.7 %copy-start.30 = (bf16[1024]{0:T(1024)(128)(2,1)S(1)}, bf16[1024]{0:T(1024)(128)(2,1)}, u32[]{:S(2)}) copy-start(bf16[1024]{0:T(1024)(128)(2,1)} %gain_ref.13) | copy-start | bytes 6148
  1.3 12.7 %copy-start.36 = (s32[2]{0:T(128)S(1)}, s32[2]{0:T(128)}, u32[]{:S(2)}) copy-start(s32[2]{0:T(128)} %lengths_ref.1) | copy-start | bytes 28
  1.3 18.9 %copy-start.3 = (bf16[1024,1024]{1,0:T(8,128)(2,1)S(1)}, bf16[1024,1024]{1,0:T(8,128)(2,1)}, u32[]{:S(2)}) copy-start(bf16[1024,1024]{1,0:T(8,128)(2,1)} %x_ref.9) | copy-start | bytes 6291460
  13.5 6.7 %collective-permute-start = (bf16[1024,1024]{1,0:T(8,128)(2,1)}, bf16[1024,1024]{1,0:T(8,128)(2,1)}, u32[]{:S(2)}, u32[]{:S(2)}) collective-permute-start(bf16[1024,1024]{1,0:T(8,128)(2,1)} %get-tuple-element.120.own_ref), channel_id=1, source_target_pairs={{0,1},{1,0},{2,3},{3,2},{4,5},{5,4},{6,7},{7,6},{8,9},{9,8},{10,11... | collective-permute-start | bytes 6291464 | tf_op jit(solution)/shard_map/ppermute | solution.py:729
  14.0 6.2 %copy-start.31 = (bf16[1024]{0:T(1024)(128)(2,1)S(1)}, bf16[1024]{0:T(1024)(128)(2,1)}, u32[]{:S(2)}) copy-start(bf16[1024]{0:T(1024)(128)(2,1)} %gain_ref.11) | copy-start | bytes 6148
  14.0 11.9 %copy-start.1 = (bf16[1024,2048]{1,0:T(8,128)(2,1)S(1)}, bf16[1024,2048]{1,0:T(8,128)(2,1)}, u32[]{:S(2)}) copy-start(bf16[1024,2048]{1,0:T(8,128)(2,1)} %wu_ref.3) | copy-start | bytes 12582916
  20.3 5.7 %copy-start = (bf16[1024,2048]{1,0:T(8,128)(2,1)S(1)}, bf16[1024,2048]{1,0:T(8,128)(2,1)}, u32[]{:S(2)}) copy-start(bf16[1024,2048]{1,0:T(8,128)(2,1)} %wg_ref.3) | copy-start | bytes 12582916
  47.0 47.4 %collective-permute-start.5 = (bf16[8,30,64,128]{3,2,1,0:T(8,128)(2,1)}, bf16[8,30,64,128]{3,2,1,0:T(8,128)(2,1)S(1)}, u32[]{:S(2)}, u32[]{:S(2)}) collective-permute-start(bf16[8,30,64,128]{3,2,1,0:T(8,128)(2,1)} %get-tuple-element.130), channel_id=1, source_target_pairs={{0,2},{1,5},{2,0},{3,7},{4,6},{5,1},{6,4},{7,3},{8,10},{9,13},{10,... | collective-permute-start | bytes 11796488 | tf_op jit(solution)/shard_map/ppermute | solution.py:737
  65.0 54.3 %collective-permute-start.8 = (bf16[8,18,64,128]{3,2,1,0:T(8,128)(2,1)}, bf16[8,18,64,128]{3,2,1,0:T(8,128)(2,1)S(1)}, u32[]{:S(2)}, u32[]{:S(2)}) collective-permute-start(bf16[8,18,64,128]{3,2,1,0:T(8,128)(2,1)} %get-tuple-element.141), channel_id=1, source_target_pairs={{0,8},{1,17},{2,10},{3,19},{4,12},{5,21},{6,14},{7,23},{8,0},{9,25... | collective-permute-start | bytes 7077896 | tf_op jit(solution)/shard_map/ppermute | solution.py:737
  71.9 7.1 %collective-permute-start.3 = (bf16[256,1024]{1,0:T(8,128)(2,1)S(1)}, bf16[256,1024]{1,0:T(8,128)(2,1)S(1)}, u32[]{:S(2)}, u32[]{:S(2)}) collective-permute-start(bf16[256,1024]{1,0:T(8,128)(2,1)S(1)} %get-tuple-element.149.refs_0_), channel_id=1, source_target_pairs={{0,1},{1,0},{2,3},{3,2},{4,5},{5,4},{6,7},{7,6},{8,9},{9,8},{10,11... | collective-permute-start | bytes 1572872 | tf_op jit(solution)/shard_map/ppermute | solution.py:729
  72.9 6.1 %copy-start.7 = (bf16[1024,1024]{1,0:T(8,128)(2,1)S(1)}, bf16[1024,1024]{1,0:T(8,128)(2,1)}, u32[]{:S(2)}) copy-start(bf16[1024,1024]{1,0:T(8,128)(2,1)} %get-tuple-element.124.mid_ref) | copy-start | bytes 6291460
  72.9 6.1 %copy-start.17 = (bf16[512,1024]{1,0:T(8,128)(2,1)S(1)}, bf16[512,1024]{1,0:T(8,128)(2,1)}, u32[]{:S(2)}) copy-start(bf16[512,1024]{1,0:T(8,128)(2,1)} %wo_ref.5) | copy-start | bytes 3145732
  72.9 6.1 %collective-permute-start.4 = (bf16[256,1024]{1,0:T(8,128)(2,1)S(1)}, bf16[256,1024]{1,0:T(8,128)(2,1)S(1)}, u32[]{:S(2)}, u32[]{:S(2)}) collective-permute-start(bf16[256,1024]{1,0:T(8,128)(2,1)S(1)} %get-tuple-element.150.refs_1_), channel_id=1, source_target_pairs={{0,1},{1,0},{2,3},{3,2},{4,5},{5,4},{6,7},{7,6},{8,9},{9,8},{10,11... | collective-permute-start | bytes 1572872 | tf_op jit(solution)/shard_map/ppermute | solution.py:729
  78.4 4.2 %collective-permute-start.1 = (bf16[256,1024]{1,0:T(8,128)(2,1)S(1)}, bf16[256,1024]{1,0:T(8,128)(2,1)S(1)}, u32[]{:S(2)}, u32[]{:S(2)}) collective-permute-start(bf16[256,1024]{1,0:T(8,128)(2,1)S(1)} %get-tuple-element.154.refs_0_), channel_id=1, source_target_pairs={{0,1},{1,0},{2,3},{3,2},{4,5},{5,4},{6,7},{7,6},{8,9},{9,8},{10,11... | collective-permute-start | bytes 1572872 | tf_op jit(solution)/shard_map/ppermute | solution.py:729
  78.9 3.8 %collective-permute-start.2 = (bf16[256,1024]{1,0:T(8,128)(2,1)S(1)}, bf16[256,1024]{1,0:T(8,128)(2,1)S(1)}, u32[]{:S(2)}, u32[]{:S(2)}) collective-permute-start(bf16[256,1024]{1,0:T(8,128)(2,1)S(1)} %get-tuple-element.155.refs_1_), channel_id=1, source_target_pairs={{0,1},{1,0},{2,3},{3,2},{4,5},{5,4},{6,7},{7,6},{8,9},{9,8},{10,11... | collective-permute-start | bytes 1572872 | tf_op jit(solution)/shard_map/ppermute | solution.py:729
  82.7 3.8 %copy-start.14 = (bf16[1024,512]{1,0:T(8,128)(2,1)S(1)}, bf16[1024,512]{1,0:T(8,128)(2,1)}, u32[]{:S(2)}) copy-start(bf16[1024,512]{1,0:T(8,128)(2,1)} %wq_ref.5) | copy-start | bytes 3145732
  82.7 3.8 %copy-start.15 = (bf16[1024,512]{1,0:T(8,128)(2,1)S(1)}, bf16[1024,512]{1,0:T(8,128)(2,1)}, u32[]{:S(2)}) copy-start(bf16[1024,512]{1,0:T(8,128)(2,1)} %wk_ref.5) | copy-start | bytes 3145732
  82.7 3.8 %copy-start.16 = (bf16[1024,512]{1,0:T(8,128)(2,1)S(1)}, bf16[1024,512]{1,0:T(8,128)(2,1)}, u32[]{:S(2)}) copy-start(bf16[1024,512]{1,0:T(8,128)(2,1)} %wv_ref.5) | copy-start | bytes 3145732
  82.8 4.3 %copy-start.25 = (bf16[1024,512]{1,0:T(8,128)(2,1)S(1)}, bf16[1024,512]{1,0:T(8,128)(2,1)}, u32[]{:S(2)}) copy-start(bf16[1024,512]{1,0:T(8,128)(2,1)} %get-tuple-element.138.v_ref) | copy-start | bytes 3145732
  87.1 7.4 %copy-start.2 = (bf16[8,30,64,128]{3,2,1,0:T(8,128)(2,1)S(1)}, bf16[8,30,64,128]{3,2,1,0:T(8,128)(2,1)}, u32[]{:S(2)}) copy-start(bf16[8,30,64,128]{3,2,1,0:T(8,128)(2,1)} %get-tuple-element.161.refs_0_) | copy-start | bytes 11796484
  96.0 34.5 %collective-permute-start.14 = (bf16[4,30,64,128]{3,2,1,0:T(8,128)(2,1)}, bf16[4,30,64,128]{3,2,1,0:T(8,128)(2,1)S(1)}, u32[]{:S(2)}, u32[]{:S(2)}) collective-permute-start(bf16[4,30,64,128]{3,2,1,0:T(8,128)(2,1)} %next_send.12), channel_id=1, source_target_pairs={{0,4},{1,3},{2,6},{3,1},{4,0},{5,7},{6,2},{7,5},{8,12},{9,11},{10,... | collective-permute-start | bytes 5898248 | tf_op jit(solution)/shard_map/ppermute | solution.py:737
  97.0 9.3 %collective-permute-start.9 = (bf16[256,1024]{1,0:T(8,128)(2,1)S(1)}, bf16[256,1024]{1,0:T(8,128)(2,1)S(1)}, u32[]{:S(2)}, u32[]{:S(2)}) collective-permute-start(bf16[256,1024]{1,0:T(8,128)(2,1)S(1)} %get-tuple-element.177.refs_0_), channel_id=1, source_target_pairs={{0,1},{1,0},{2,3},{3,2},{4,5},{5,4},{6,7},{7,6},{8,9},{9,8},{10,11... | collective-permute-start | bytes 1572872 | tf_op jit(solution)/shard_map/ppermute | solution.py:729
  97.6 12.2 %collective-permute-start.10 = (bf16[256,1024]{1,0:T(8,128)(2,1)S(1)}, bf16[256,1024]{1,0:T(8,128)(2,1)S(1)}, u32[]{:S(2)}, u32[]{:S(2)}) collective-permute-start(bf16[256,1024]{1,0:T(8,128)(2,1)S(1)} %get-tuple-element.178.refs_1_), channel_id=1, source_target_pairs={{0,1},{1,0},{2,3},{3,2},{4,5},{5,4},{6,7},{7,6},{8,9},{9,8},{10,11... | collective-permute-start | bytes 1572872 | tf_op jit(solution)/shard_map/ppermute | solution.py:729
  97.6 8.7 %copy-start.18 = (bf16[16,64,1024]{2,1,0:T(8,128)(2,1)S(1)}, bf16[16,64,1024]{2,1,0:T(8,128)(2,1)}, u32[]{:S(2)}) copy-start(bf16[16,64,1024]{2,1,0:T(8,128)(2,1)} %get-tuple-element.122.turned_ref.value_ref) | copy-start | bytes 6291460
  105.8 13.9 %collective-permute-start.6 = (bf16[256,1024]{1,0:T(8,128)(2,1)}, bf16[256,1024]{1,0:T(8,128)(2,1)S(1)}, u32[]{:S(2)}, u32[]{:S(2)}) collective-permute-start(bf16[256,1024]{1,0:T(8,128)(2,1)} %get-tuple-element.183.refs_0_), channel_id=1, source_target_pairs={{0,1},{1,0},{2,3},{3,2},{4,5},{5,4},{6,7},{7,6},{8,9},{9,8},{10,11... | collective-permute-start | bytes 1572872 | tf_op jit(solution)/shard_map/ppermute | solution.py:729
  106.3 13.4 %collective-permute-start.7 = (bf16[256,1024]{1,0:T(8,128)(2,1)S(1)}, bf16[256,1024]{1,0:T(8,128)(2,1)S(1)}, u32[]{:S(2)}, u32[]{:S(2)}) collective-permute-start(bf16[256,1024]{1,0:T(8,128)(2,1)S(1)} %get-tuple-element.184.refs_1_), channel_id=1, source_target_pairs={{0,1},{1,0},{2,3},{3,2},{4,5},{5,4},{6,7},{7,6},{8,9},{9,8},{10,11... | collective-permute-start | bytes 1572872 | tf_op jit(solution)/shard_map/ppermute | solution.py:729
  106.3 5.1 %copy-start.27 = (bf16[512,1024]{1,0:T(8,128)(2,1)S(1)}, bf16[512,1024]{1,0:T(8,128)(2,1)}, u32[]{:S(2)}) copy-start(bf16[512,1024]{1,0:T(8,128)(2,1)} %get-tuple-element.173.gm_ref) | copy-start | bytes 3145732
  109.8 31.9 %collective-permute-start.13 = (bf16[8,8,64,128]{3,2,1,0:T(8,128)(2,1)S(1)}, bf16[8,8,64,128]{3,2,1,0:T(8,128)(2,1)S(1)}, u32[]{:S(2)}, u32[]{:S(2)}) collective-permute-start(bf16[8,8,64,128]{3,2,1,0:T(8,128)(2,1)S(1)} %get-tuple-element.176), channel_id=1, source_target_pairs={{0,8},{1,17},{2,10},{3,19},{4,12},{5,21},{6,14},{7,23},{8,0},{9,25... | collective-permute-start | bytes 3145736 | tf_op jit(solution)/shard_map/ppermute | solution.py:737
  111.4 7.9 %copy-start.4 = (bf16[8,18,64,128]{3,2,1,0:T(8,128)(2,1)S(1)}, bf16[8,18,64,128]{3,2,1,0:T(8,128)(2,1)}, u32[]{:S(2)}) copy-start(bf16[8,18,64,128]{3,2,1,0:T(8,128)(2,1)} %get-tuple-element.172.refs_0_) | copy-start | bytes 7077892
  119.6 22.4 %collective-permute-start.12 = (bf16[4,18,64,128]{3,2,1,0:T(8,128)(2,1)S(1)}, bf16[4,18,64,128]{3,2,1,0:T(8,128)(2,1)S(1)}, u32[]{:S(2)}, u32[]{:S(2)}) collective-permute-start(bf16[4,18,64,128]{3,2,1,0:T(8,128)(2,1)S(1)} %next_send.13), channel_id=1, source_target_pairs={{0,2},{1,5},{2,0},{3,7},{4,6},{5,1},{6,4},{7,3},{8,10},{9,13},{10,... | collective-permute-start | bytes 3538952 | tf_op jit(solution)/shard_map/ppermute | solution.py:737
  129.3 12.5 %copy-start.11 = (bf16[8,8,64,128]{3,2,1,0:T(8,128)(2,1)S(1)}, bf16[8,8,64,128]{3,2,1,0:T(8,128)(2,1)}, u32[]{:S(2)}) copy-start(bf16[8,8,64,128]{3,2,1,0:T(8,128)(2,1)} %get-tuple-element.194.refs_0_) | copy-start | bytes 3145732
  129.3 19.2 %collective-permute-start.11 = (bf16[8,9,64,128]{3,2,1,0:T(8,128)(2,1)S(1)}, bf16[8,9,64,128]{3,2,1,0:T(8,128)(2,1)S(1)}, u32[]{:S(2)}, u32[]{:S(2)}) collective-permute-start(bf16[8,9,64,128]{3,2,1,0:T(8,128)(2,1)S(1)} %get-tuple-element.193), channel_id=1, source_target_pairs={{0,2},{1,5},{2,0},{3,7},{4,6},{5,1},{6,4},{7,3},{8,10},{9,13},{10,... | collective-permute-start | bytes 3538952 | tf_op jit(solution)/shard_map/ppermute | solution.py:737
  131.8 31.0 %collective-permute-start.21 = (bf16[2,30,64,128]{3,2,1,0:T(8,128)(2,1)S(1)}, bf16[2,30,64,128]{3,2,1,0:T(8,128)(2,1)S(1)}, u32[]{:S(2)}, u32[]{:S(2)}) collective-permute-start(bf16[2,30,64,128]{3,2,1,0:T(8,128)(2,1)S(1)} %next_send.14), channel_id=1, source_target_pairs={{0,8},{1,17},{2,10},{3,19},{4,12},{5,21},{6,14},{7,23},{8,0},{9,25... | collective-permute-start | bytes 2949128 | tf_op jit(solution)/shard_map/ppermute | solution.py:737
  141.8 7.7 %copy-start.13 = (bf16[1024,2048]{1,0:T(8,128)(2,1)S(1)}, bf16[1024,2048]{1,0:T(8,128)(2,1)}, u32[]{:S(2)}) copy-start(bf16[1024,2048]{1,0:T(8,128)(2,1)} %copy-done.12) | copy-start | bytes 12582916
  141.9 6.6 %copy-start.6 = (bf16[8,9,64,128]{3,2,1,0:T(8,128)(2,1)S(1)}, bf16[8,9,64,128]{3,2,1,0:T(8,128)(2,1)}, u32[]{:S(2)}) copy-start(bf16[8,9,64,128]{3,2,1,0:T(8,128)(2,1)} %get-tuple-element.192.refs_0_) | copy-start | bytes 3538948
  141.9 15.8 %collective-permute-start.19 = (bf16[4,8,64,128]{3,2,1,0:T(8,128)(2,1)S(1)}, bf16[4,8,64,128]{3,2,1,0:T(8,128)(2,1)S(1)}, u32[]{:S(2)}, u32[]{:S(2)}) collective-permute-start(bf16[4,8,64,128]{3,2,1,0:T(8,128)(2,1)S(1)} %next_send.15), channel_id=1, source_target_pairs={{0,2},{1,5},{2,0},{3,7},{4,6},{5,1},{6,4},{7,3},{8,10},{9,13},{10,... | collective-permute-start | bytes 1572872 | tf_op jit(solution)/shard_map/ppermute | solution.py:737
  142.0 7.5 %copy-start.5 = (bf16[2048,1024]{1,0:T(8,128)(2,1)S(1)}, bf16[2048,1024]{1,0:T(8,128)(2,1)}, u32[]{:S(2)}) copy-start(bf16[2048,1024]{1,0:T(8,128)(2,1)} %wd_ref.1) | copy-start | bytes 12582916
  148.7 10.7 %collective-permute-start.18 = (bf16[4,9,64,128]{3,2,1,0:T(8,128)(2,1)S(1)}, bf16[4,9,64,128]{3,2,1,0:T(8,128)(2,1)S(1)}, u32[]{:S(2)}, u32[]{:S(2)}) collective-permute-start(bf16[4,9,64,128]{3,2,1,0:T(8,128)(2,1)S(1)} %next_send.17), channel_id=1, source_target_pairs={{0,4},{1,3},{2,6},{3,1},{4,0},{5,7},{6,2},{7,5},{8,12},{9,11},{10,... | collective-permute-start | bytes 1769480 | tf_op jit(solution)/shard_map/ppermute | solution.py:737
  155.3 20.2 %collective-permute-start.15 = (bf16[512,1024]{1,0:T(8,128)(2,1)S(1)}, bf16[512,1024]{1,0:T(8,128)(2,1)S(1)}, u32[]{:S(2)}, u32[]{:S(2)}) collective-permute-start(bf16[512,1024]{1,0:T(8,128)(2,1)S(1)} %get-tuple-element.207.refs_0_), channel_id=1, source_target_pairs={{0,1},{1,0},{2,3},{3,2},{4,5},{5,4},{6,7},{7,6},{8,9},{9,8},{10,11... | collective-permute-start | bytes 3145736 | tf_op jit(solution)/shard_map/ppermute | solution.py:729
  155.4 23.0 %collective-permute-start.16 = (bf16[512,1024]{1,0:T(8,128)(2,1)S(1)}, bf16[512,1024]{1,0:T(8,128)(2,1)S(1)}, u32[]{:S(2)}, u32[]{:S(2)}) collective-permute-start(bf16[512,1024]{1,0:T(8,128)(2,1)S(1)} %get-tuple-element.208.refs_1_), channel_id=1, source_target_pairs={{0,1},{1,0},{2,3},{3,2},{4,5},{5,4},{6,7},{7,6},{8,9},{9,8},{10,11... | collective-permute-start | bytes 3145736 | tf_op jit(solution)/shard_map/ppermute | solution.py:729
  157.7 17.5 %collective-permute-start.17 = (bf16[2,18,64,128]{3,2,1,0:T(8,128)(2,1)S(1)}, bf16[2,18,64,128]{3,2,1,0:T(8,128)(2,1)S(1)}, u32[]{:S(2)}, u32[]{:S(2)}) collective-permute-start(bf16[2,18,64,128]{3,2,1,0:T(8,128)(2,1)S(1)} %next_send.16), channel_id=1, source_target_pairs={{0,4},{1,3},{2,6},{3,1},{4,0},{5,7},{6,2},{7,5},{8,12},{9,11},{10,... | collective-permute-start | bytes 1769480 | tf_op jit(solution)/shard_map/ppermute | solution.py:737
  158.0 4.8 %copy-start.10 = (bf16[4,30,64,128]{3,2,1,0:T(8,128)(2,1)S(1)}, bf16[4,30,64,128]{3,2,1,0:T(8,128)(2,1)}, u32[]{:S(2)}) copy-start(bf16[4,30,64,128]{3,2,1,0:T(8,128)(2,1)} %copy-done.9) | copy-start | bytes 5898244
  159.6 15.6 %collective-permute-start.20 = (bf16[2,9,64,128]{3,2,1,0:T(8,128)(2,1)S(1)}, bf16[2,9,64,128]{3,2,1,0:T(8,128)(2,1)S(1)}, u32[]{:S(2)}, u32[]{:S(2)}) collective-permute-start(bf16[2,9,64,128]{3,2,1,0:T(8,128)(2,1)S(1)} %next_send.19), channel_id=1, source_target_pairs={{0,8},{1,17},{2,10},{3,19},{4,12},{5,21},{6,14},{7,23},{8,0},{9,25... | collective-permute-start | bytes 884744 | tf_op jit(solution)/shard_map/ppermute | solution.py:737
  163.1 17.2 %collective-permute-start.23 = (bf16[1,30,64,128]{3,2,1,0:T(8,128)(2,1)S(1)}, bf16[1,30,64,128]{3,2,1,0:T(8,128)(2,1)S(1)}, u32[]{:S(2)}, u32[]{:S(2)}) collective-permute-start(bf16[1,30,64,128]{3,2,1,0:T(8,128)(2,1)S(1)} %next_send.20), channel_id=1, source_target_pairs={{0,16},{1,9},{2,18},{3,11},{4,20},{5,13},{6,22},{7,15},{8,24},{9,1... | collective-permute-start | bytes 1474568 | tf_op jit(solution)/shard_map/ppermute | solution.py:737
  175.1 6.4 %collective-permute-start.22 = (bf16[2,8,64,128]{3,2,1,0:T(8,128)(2,1)S(1)}, bf16[2,8,64,128]{3,2,1,0:T(8,128)(2,1)S(1)}, u32[]{:S(2)}, u32[]{:S(2)}) collective-permute-start(bf16[2,8,64,128]{3,2,1,0:T(8,128)(2,1)S(1)} %next_send.18), channel_id=1, source_target_pairs={{0,4},{1,3},{2,6},{3,1},{4,0},{5,7},{6,2},{7,5},{8,12},{9,11},{10,... | collective-permute-start | bytes 786440 | tf_op jit(solution)/shard_map/ppermute | solution.py:737
  175.4 10.8 %collective-permute-start.26 = (bf16[1,18,64,128]{3,2,1,0:T(8,128)(2,1)S(1)}, bf16[1,18,64,128]{3,2,1,0:T(8,128)(2,1)S(1)}, u32[]{:S(2)}, u32[]{:S(2)}) collective-permute-start(bf16[1,18,64,128]{3,2,1,0:T(8,128)(2,1)S(1)} %next_send.22), channel_id=1, source_target_pairs={{0,16},{1,9},{2,18},{3,11},{4,20},{5,13},{6,22},{7,15},{8,24},{9,1... | collective-permute-start | bytes 884744 | tf_op jit(solution)/shard_map/ppermute | solution.py:737
  175.5 13.9 %collective-permute-start.25 = (bf16[1,9,64,128]{3,2,1,0:T(8,128)(2,1)S(1)}, bf16[1,9,64,128]{3,2,1,0:T(8,128)(2,1)S(1)}, u32[]{:S(2)}, u32[]{:S(2)}) collective-permute-start(bf16[1,9,64,128]{3,2,1,0:T(8,128)(2,1)S(1)} %next_send.21), channel_id=1, source_target_pairs={{0,16},{1,9},{2,18},{3,11},{4,20},{5,13},{6,22},{7,15},{8,24},{9,1... | collective-permute-start | bytes 442376 | tf_op jit(solution)/shard_map/ppermute | solution.py:737
  181.6 10.6 %collective-permute-start.24 = (bf16[1,8,64,128]{3,2,1,0:T(8,128)(2,1)S(1)}, bf16[1,8,64,128]{3,2,1,0:T(8,128)(2,1)S(1)}, u32[]{:S(2)}, u32[]{:S(2)}) collective-permute-start(bf16[1,8,64,128]{3,2,1,0:T(8,128)(2,1)S(1)} %next_send.23), channel_id=1, source_target_pairs={{0,16},{1,9},{2,18},{3,11},{4,20},{5,13},{6,22},{7,15},{8,24},{9,1... | collective-permute-start | bytes 393224 | tf_op jit(solution)/shard_map/ppermute | solution.py:737
  (16 other events, 45.4 us)

commit v2 on v1

--- a/solution.py
+++ b/solution.py
@@ -303,13 +303,13 @@
         back = nt(s_ref[at], wd_ref[...])
         sig = 1.0 / (1.0 + jnp.exp(-gate))
         silu = gate * sig
-        h_ref[at, here] = (silu * up).astype(bf16)
+        h_ref[at] = (silu * up).astype(bf16)
         gg_ref[at, here] = (back * up * (sig * (1.0 + gate * (1.0 - sig)))).astype(bf16)
         gu_ref[at, here] = (back * silu).astype(bf16)
     columns = block // LANES
     product_pieces(keep_ref, send_ref, 0, nt_ref, gg_ref[:, here], order)
     product_pieces(keep_ref, send_ref, columns, nt_ref, gu_ref[:, here], order)
-    product_pieces(keep_ref, send_ref, 2 * columns, st_ref, h_ref[:, here], order)
+    product_pieces(keep_ref, send_ref, 2 * columns, st_ref, h_ref[...], order)
 
 
 def hidden_chunk(first, steps, block, order, normed, normed_t, seed, seed_t, wg, wu, wd, earlier):
@@ -329,14 +329,19 @@
     if earlier is not None:
         aliases = {7: 0, 8: 1, 9: 2}
         args += list(earlier)
-        ins += [resident()] * 3
+        ins += [pl.BlockSpec(memory_space=pl.ANY)] + [resident()] * 2
     return call(
         functools.partial(hidden_body, order, first, block, earlier is None),
         "hidden_units",
         (steps,),
         ins,
-        [(resident(), (rows, hidden), bf16, pltpu.VMEM)] * 3 + [pieces, (*pieces, ANYWHERE)],
-        vmem=13,
+        [
+            (pl.BlockSpec((rows, block), lambda j: (0, first // block + j)), (rows, hidden), bf16),
+            *[(resident(), (rows, hidden), bf16, pltpu.VMEM)] * 2,
+            pieces,
+            (*pieces, ANYWHERE),
+        ],
+        vmem=14,
         far=(6,),
         aliases=aliases,
         cost=(12 * rows * width * block * steps, 20 * MIB),
@@ -387,9 +392,9 @@
         down_body,
         "hidden_down",
         (width // block,),
-        [resident(), pl.BlockSpec((units, block), lambda j: (0, j))],
+        [whole(rows, units), pl.BlockSpec((units, block), lambda j: (0, j))],
         [out] * PARTS,
-        vmem=20,
+        vmem=24,
         cost=(2 * rows * width * units, 10 * MIB),
     )(hidden, wd)
 
@@ -459,7 +464,7 @@
             ),
             (there(heads), (rows, heads), bf16),
             (rows_of(block, width), (share, width), bf16),
-            (whole(1, width), (1, width), f32),
+            (whole(1, width), (1, width), f32, ANYWHERE),
         ],
         scratch=[pltpu.VMEM((block, width), f32)],
         vmem=24,
@@ -627,7 +632,7 @@
         "input_grad",
         (PARTS,),
         ins,
-        [(there, (rows, width), bf16), (whole(1, width), (1, width), f32)],
+        [(there, (rows, width), bf16), (whole(1, width), (1, width), f32, ANYWHERE)],
         scratch=[pltpu.VMEM((block, width), f32)],
         vmem=24,
         aliases=aliases,

time: 195 us -> 192 us (0.985)
  waiting for transfers between devices: 40 us -> 42.4 us
  local copies, waits for them, and re-layouts: 5.75 us -> 3.49 us
    ppermute x16, waiting for transfers between devices: 40 us -> 42.4 us  [hop_swap(): return lax.ppermute(array, ('dp', 'tensor'), pairs)]
    unnamed x74 -> x68, local copies, waits for them, and re-layouts: 5.75 us -> 3.49 us
  transfers between devices with their start and end apart: 27 -> 27, of which waited for: 11 -> 12; matrix products, arithmetic and copies ran while one was open for 0% -> 0% of each run, Pallas kernels for 42% -> 42%
where the time goes in v2:
time: 192 us
  Pallas kernels  120 us (62%)
  waiting for transfers between devices  42.4 us (22%)
  starting transfers between devices  24.5 us (13%)
  local copies, waits for them, and re-layouts  3.49 us (2%)
    pallas_call x33, Pallas kernels, run(): kernel(*(pltpu.with_memory_space_constraint(arg, pltpu.HBM) if n - scalar...  120 us
    ppermute x16, waiting for transfers between devices, hop_swap(): return lax.ppermute(array, ('dp', 'tensor'), pairs)  42.4 us
    ppermute x16, starting transfers between devices, hop_swap(): return lax.ppermute(array, ('dp', 'tensor'), pairs)  20.7 us
  transfers between devices with their start and end apart: 27, of which 12 were waited for; matrix products, arithmetic and copies ran while one was open for 0% of the time, Pallas kernels for 42%

profile of v2, /device:TPU:0, one launch (start us, length us, event | category | flops | bytes accessed | tf_op | source)
XLA Modules:
  0.0 191.9 jit_solution(7218055839797274764)
XLA Ops:
  1.3 12.2 %attention_forward.1 = (bf16[1024,512]{1,0:T(8,128)(2,1)}, bf16[1024,512]{1,0:T(8,128)(2,1)}, bf16[1024,512]{1,0:T(8,128)(2,1)}, bf16[1024,512]{1,0:T(8,128)(2,1...) custom-call(bf16[1024,1024]{1,0:T(8,128)(2,1)} %x_ref.9, bf16[1024]{0:T(1024)(128)(2,1)S(1)} %copy-done.30, ...), custom_call_target="tpu_custom_call" | custom-call | flops 4294 | tf_op jit(solution)/shard_map/attention_forward/pallas_call | solution.py:63
  14.1 6.2 %seed_rows.1 = (bf16[1024,1024]{1,0:T(8,128)(2,1)S(1)}, bf16[16,64,1024]{2,1,0:T(8,128)(2,1)S(1)}, bf16[16,64,1024]{2,1,0:T(8,128)(2,1)}) custom-call(s32[2]{0:T(128)S(1)} %copy-done.33, s32[2]{0:T(128)S(1)} %pad_add_fusion.me_ref, bf16[1024,1024]{1,0:T(8,128)(2,1)} %cot_ref, bf16[1024,1024]{1,0:T(8,128)(2,1)} %x_ref.9, bf16[1024]{0:T(1024)(128)(2,1)S(1)} %copy-done.31), custom_call_target="tpu_custom_call" | custom-call | flops 4 | tf_op jit(solution)/shard_map/seed_rows/pallas_call | solution.py:63
  20.3 6.5 %middle_rows.1 = (bf16[1024,1024]{1,0:T(8,128)(2,1)}, bf16[1024,1024]{1,0:T(8,128)(2,1)S(1)}, bf16[16,64,1024]{2,1,0:T(8,128)(2,1)S(1)}) custom-call(s32[2]{0:T(128)S(1)} %pad_add_fusion.me_ref, bf16[1024,1024]{1,0:T(8,128)(2,1)S(1)} %copy-done.3, bf16[1024,1024]{1,0:T(8,128)(2,1)} %get-tuple-element.120.own_ref, ...), custom_call_target="tpu_custom_call" | custom-call | flops 8 | tf_op jit(solution)/shard_map/middle_rows/pallas_call | solution.py:63
  26.8 21.0 %hidden_units.2 = (bf16[1024,2048]{1,0:T(8,128)(2,1)}, bf16[1024,2048]{1,0:T(8,128)(2,1)S(1)}, bf16[1024,2048]{1,0:T(8,128)(2,1)S(1)}, bf16[8,30,64,128]{3,2,1,0:T(8,128)(2,1)}, bf16[8,30,64,128]{3,2,1,0:T(8,128)(2,1)}) custom-call(bf16[1024,1024]{1,0:T(8,128)(2,1)S(1)} %get-tuple-element.131.refs_0_, bf16[16,64,1024]{2,1,0:T(8,128)(2,1)S(1)} %get-tuple-element.126.refs_1_, ...), custom_call_target="tpu_custom_call" | custom-call | flops 16106 | tf_op jit(solution)/shard_map/hidden_units/pallas_call | solution.py:63
  47.8 2.5 %collective-permute-start.5 = (bf16[8,30,64,128]{3,2,1,0:T(8,128)(2,1)}, bf16[8,30,64,128]{3,2,1,0:T(8,128)(2,1)S(1)}, u32[]{:S(2)}, u32[]{:S(2)}) collective-permute-start(bf16[8,30,64,128]{3,2,1,0:T(8,128)(2,1)} %get-tuple-element.130), channel_id=1, source_target_pairs={{0,2},{1,5},{2,0},{3,7},{4,6},{5,1},{6,4},{7,3},{8,10},{9,13},{10,... | collective-permute-start | bytes 11796488 | tf_op jit(solution)/shard_map/ppermute | solution.py:742
  50.3 13.6 %hidden_units.3 = (bf16[1024,2048]{1,0:T(8,128)(2,1)}, bf16[1024,2048]{1,0:T(8,128)(2,1)S(1)}, bf16[1024,2048]{1,0:T(8,128)(2,1)S(1)}, bf16[8,18,64,128]{3,2,1,0:T(8,128)(2,1)}, bf16[8,18,64,128]{3,2,1,0:T(8,128)(2,1)}) custom-call(bf16[1024,1024]{1,0:T(8,128)(2,1)S(1)} %get-tuple-element.131.refs_0_, ...), custom_call_target="tpu_custom_call", output_to_operand_aliasing={{0}: (7, {}), {1}: (8, {}), {2}: (9, {})} | custom-call | flops 9663 | tf_op jit(solution)/shard_map/hidden_units/pallas_call | solution.py:63
  63.9 1.6 collective-permute-start.8
  65.5 5.3 %normed_two_back.2 = (bf16[256,1024]{1,0:T(8,128)(2,1)S(1)}, bf16[256,1024]{1,0:T(8,128)(2,1)S(1)}) custom-call(bf16[1024,2048]{1,0:T(8,128)(2,1)S(1)} %get-tuple-element.145.gg_ref, bf16[1024,2048]{1,0:T(8,128)(2,1)S(1)} %get-tuple-element.143.gu_ref, bf16[1024,2048]{1,0:T(8,128)(2,1)S(1)} %copy-done, bf16[1024,2048]{1,0:T(8,128)(2,1)S(1)} %copy-done.1), custom_call_target="tpu_custom_call" | custom-call | flops 4294 | tf_op jit(solution)/shard_map/normed_two_back/pallas_call | solution.py:63
  70.7 1.0 collective-permute-start.3
  71.9 5.4 %normed_two_back.3 = (bf16[256,1024]{1,0:T(8,128)(2,1)S(1)}, bf16[256,1024]{1,0:T(8,128)(2,1)S(1)}) custom-call(bf16[1024,2048]{1,0:T(8,128)(2,1)S(1)} %get-tuple-element.145.gg_ref, bf16[1024,2048]{1,0:T(8,128)(2,1)S(1)} %get-tuple-element.143.gu_ref, bf16[1024,2048]{1,0:T(8,128)(2,1)S(1)} %copy-done, bf16[1024,2048]{1,0:T(8,128)(2,1)S(1)} %copy-done.1), custom_call_target="tpu_custom_call" | custom-call | flops 4294 | tf_op jit(solution)/shard_map/normed_two_back/pallas_call | solution.py:63
  77.9 3.7 %middle_backward.2 = (bf16[16,64,1024]{2,1,0:T(8,128)(2,1)}, bf16[1024,512]{1,0:T(8,128)(2,1)}, bf16[512,1024]{1,0:T(8,128)(2,1)}, f32[1,1024]{1,0:T(1,128)S(1)}) custom-call(s32[2]{0:T(128)S(1)} %pad_add_fusion.me_ref, bf16[1024,1024]{1,0:T(8,128)(2,1)S(1)} %copy-done.9, bf16[1024,1024]{1,0:T(8,128)(2,1)S(1)} %copy-done.7, bf16[1024]{0:T(1024)(128)(2,1)S(1)} %copy-done.32, ...), custom_call_target="tpu_custom_call" | custom-call | flops 536 | tf_op jit(solution)/shard_map/middle_backward/pallas_call | solution.py:63
  81.7 3.7 %middle_backward.3 = (bf16[16,64,1024]{2,1,0:T(8,128)(2,1)}, bf16[1024,512]{1,0:T(8,128)(2,1)}, bf16[512,1024]{1,0:T(8,128)(2,1)}, f32[1,1024]{1,0:T(1,128)S(1)}) custom-call(s32[2]{0:T(128)S(1)} %pad_add_fusion.me_ref, bf16[1024,1024]{1,0:T(8,128)(2,1)S(1)} %copy-done.9, ...), custom_call_target="tpu_custom_call", output_to_operand_aliasing={{0}: (9, {}), {1}: (10, {})} | custom-call | flops 536 | tf_op jit(solution)/shard_map/middle_backward/pallas_call | solution.py:63
  85.9 7.4 %attention_backward.2 = (bf16[1024,1536]{1,0:T(8,128)(2,1)S(1)}, bf16[256,1024]{1,0:T(8,128)(2,1)S(1)}, bf16[256,1024]{1,0:T(8,128)(2,1)S(1)}) custom-call(bf16[1024,512]{1,0:T(8,128)(2,1)S(1)} %copy-done.24, bf16[1024,512]{1,0:T(8,128)(2,1)S(1)} %copy-done.25, bf16[1024,512]{1,0:T(8,128)(2,1)S(1)} %copy-done.26, bf16[1024,1024]{1,0:T(8,128)(2,1)S(1)} %copy-done.21, ...), custom_call_target="tpu_custom_call" | custom-call | flops 1610 | tf_op jit(solution)/shard_map/attention_backward/pallas_call | solution.py:63
  93.3 0.9 collective-permute-done.5.refs_1_
  94.2 1.5 next_send.12
  95.7 2.1 %collective-permute-start.14 = (bf16[4,30,64,128]{3,2,1,0:T(8,128)(2,1)}, bf16[4,30,64,128]{3,2,1,0:T(8,128)(2,1)S(1)}, u32[]{:S(2)}, u32[]{:S(2)}) collective-permute-start(bf16[4,30,64,128]{3,2,1,0:T(8,128)(2,1)} %next_send.12), channel_id=1, source_target_pairs={{0,4},{1,3},{2,6},{3,1},{4,0},{5,7},{6,2},{7,5},{8,12},{9,11},{10,... | collective-permute-start | bytes 5898248 | tf_op jit(solution)/shard_map/ppermute | solution.py:742
  98.3 7.4 %attention_backward.3 = (bf16[1024,1536]{1,0:T(8,128)(2,1)S(1)}, bf16[256,1024]{1,0:T(8,128)(2,1)S(1)}, bf16[256,1024]{1,0:T(8,128)(2,1)S(1)}) custom-call(bf16[1024,512]{1,0:T(8,128)(2,1)S(1)} %copy-done.24, bf16[1024,512]{1,0:T(8,128)(2,1)S(1)} %copy-done.25, bf16[1024,512]{1,0:T(8,128)(2,1)S(1)} %copy-done.26, ...), custom_call_target="tpu_custom_call", output_to_operand_aliasing={{0}: (8, {})} | custom-call | flops 1610 | tf_op jit(solution)/shard_map/attention_backward/pallas_call | solution.py:63
  106.3 3.7 %query_key_grads.1 = (bf16[8,8,64,128]{3,2,1,0:T(8,128)(2,1)}, bf16[8,8,64,128]{3,2,1,0:T(8,128)(2,1)}) custom-call(bf16[16,64,1024]{2,1,0:T(8,128)(2,1)S(1)} %copy-done.19, bf16[1024,1536]{1,0:T(8,128)(2,1)S(1)} %get-tuple-element.189.right_ref), custom_call_target="tpu_custom_call" | custom-call | flops 2147 | tf_op jit(solution)/shard_map/query_key_grads/pallas_call | solution.py:63
  110.0 1.6 collective-permute-start.13
  111.5 2.3 %input_grad.2 = (bf16[1024,1024]{1,0:T(8,128)(2,1)}, f32[1,1024]{1,0:T(1,128)S(1)}) custom-call(bf16[1024,1024]{1,0:T(8,128)(2,1)S(1)} %copy-done.3, bf16[512,1024]{1,0:T(8,128)(2,1)S(1)} %copy-done.28, bf16[1024]{0:T(1024)(128)(2,1)S(1)} %copy-done.31, bf16[256,1024]{1,0:T(8,128)(2,1)S(1)} %get-tuple-element.177.refs_0_, ...), custom_call_target="tpu_custom_call" | custom-call | flops 5 | tf_op jit(solution)/shard_map/input_grad/pallas_call | solution.py:63
  113.9 4.2 %collective-permute-done.8.refs_1_ = bf16[8,18,64,128]{3,2,1,0:T(8,128)(2,1)S(1)} collective-permute-done((bf16[8,18,64,128]{3,2,1,0:T(8,128)(2,1)}, bf16[8,18,64,128]{3,2,1,0:T(8,128)(2,1)S(1)}, u32[]{:S(2)}, u32[]{:S(2)}) %collective-permute-start.8) | collective-permute-done | bytes 2359328 | tf_op jit(solution)/shard_map/ppermute | solution.py:742
  118.5 0.8 copy-done.29
  119.4 2.3 %input_grad.3 = (bf16[1024,1024]{1,0:T(8,128)(2,1)}, f32[1,1024]{1,0:T(1,128)S(1)}) custom-call(bf16[1024,1024]{1,0:T(8,128)(2,1)S(1)} %copy-done.3, bf16[512,1024]{1,0:T(8,128)(2,1)S(1)} %copy-done.29, bf16[1024]{0:T(1024)(128)(2,1)S(1)} %copy-done.31, bf16[256,1024]{1,0:T(8,128)(2,1)S(1)} %get-tuple-element.183.refs_0_, ...), custom_call_target="tpu_custom_call", output_to_operand_aliasing={{0}: (7, {})} | custom-call | flops 5 | tf_op jit(solution)/shard_map/input_grad/pallas_call | solution.py:63
  122.2 4.4 %value_out_grads.1 = (bf16[8,9,64,128]{3,2,1,0:T(8,128)(2,1)}, bf16[8,9,64,128]{3,2,1,0:T(8,128)(2,1)S(1)}) custom-call(bf16[16,64,1024]{2,1,0:T(8,128)(2,1)S(1)} %copy-done.20, bf16[1024,1536]{1,0:T(8,128)(2,1)S(1)} %get-tuple-element.189.right_ref, bf16[16,64,1024]{2,1,0:T(8,128)(2,1)S(1)} %copy-done.23, bf16[1024,512]{1,0:T(8,128)(2,1)S(1)} %copy-done.27, ...), custom_call_target="tpu_custom_call" | custom-call | flops 2147 | tf_op jit(solution)/shard_map/value_out_grads/pallas_call | solution.py:63
  126.6 1.2 collective-permute-start.11
  128.2 0.9 copy-done.11
  129.1 1.4 collective-permute-start.21
  130.5 10.2 %collective-permute-done.13.refs_1_ = bf16[8,8,64,128]{3,2,1,0:T(8,128)(2,1)S(1)} collective-permute-done((bf16[8,8,64,128]{3,2,1,0:T(8,128)(2,1)}, bf16[8,8,64,128]{3,2,1,0:T(8,128)(2,1)S(1)}, u32[]{:S(2)}, u32[]{:S(2)}) %collective-permute-start.13) | collective-permute-done | bytes 1048608 | tf_op jit(solution)/shard_map/ppermute | solution.py:742
  141.1 6.2 %collective-permute-done.11.refs_1_ = bf16[8,9,64,128]{3,2,1,0:T(8,128)(2,1)S(1)} collective-permute-done((bf16[8,9,64,128]{3,2,1,0:T(8,128)(2,1)S(1)}, bf16[8,9,64,128]{3,2,1,0:T(8,128)(2,1)S(1)}, u32[]{:S(2)}, u32[]{:S(2)}) %collective-permute-start.11) | collective-permute-done | bytes 1179680 | tf_op jit(solution)/shard_map/ppermute | solution.py:742
  147.5 0.8 collective-permute-start.18
  148.3 5.8 %hidden_down.1 = (bf16[512,1024]{1,0:T(8,128)(2,1)S(1)}, bf16[512,1024]{1,0:T(8,128)(2,1)S(1)}) custom-call(bf16[1024,2048]{1,0:T(8,128)(2,1)S(1)} %copy-done.14, bf16[2048,1024]{1,0:T(8,128)(2,1)S(1)} %copy-done.5), custom_call_target="tpu_custom_call" | custom-call | flops 4294 | tf_op jit(solution)/shard_map/hidden_down/pallas_call | solution.py:63
  154.7 1.9 collective-permute-done.19.refs_2_
  156.7 1.6 collective-permute-done.18.refs_2_
  158.4 1.7 collective-permute-start.20
  160.1 1.6 collective-permute-done.21.refs_3_
  161.9 1.9 collective-permute-start.23
  163.8 7.5 %collective-permute-done.20.refs_3_ = bf16[2,9,64,128]{3,2,1,0:T(8,128)(2,1)S(1)} collective-permute-done((bf16[2,9,64,128]{3,2,1,0:T(8,128)(2,1)S(1)}, bf16[2,9,64,128]{3,2,1,0:T(8,128)(2,1)S(1)}, u32[]{:S(2)}, u32[]{:S(2)}) %collective-permute-start.20) | collective-permute-done | bytes 294944 | tf_op jit(solution)/shard_map/ppermute | solution.py:742
  171.3 1.5 collective-permute-start.22
  173.1 2.9 %collective-permute-start.25 = (bf16[1,9,64,128]{3,2,1,0:T(8,128)(2,1)S(1)}, bf16[1,9,64,128]{3,2,1,0:T(8,128)(2,1)S(1)}, u32[]{:S(2)}, u32[]{:S(2)}) collective-permute-start(bf16[1,9,64,128]{3,2,1,0:T(8,128)(2,1)S(1)} %next_send.21), channel_id=1, source_target_pairs={{0,16},{1,9},{2,18},{3,11},{4,20},{5,13},{6,22},{7,15},{8,24},{9,1... | collective-permute-start | bytes 442376 | tf_op jit(solution)/shard_map/ppermute | solution.py:742
  176.1 1.9 block_output.1
  177.9 0.9 collective-permute-done.23.refs_4_
  178.9 1.1 hidden_grads_out.2
  180.0 1.5 collective-permute-start.24
  181.5 3.7 %collective-permute-done.26.refs_4_ = bf16[1,18,64,128]{3,2,1,0:T(8,128)(2,1)S(1)} collective-permute-done((bf16[1,18,64,128]{3,2,1,0:T(8,128)(2,1)S(1)}, bf16[1,18,64,128]{3,2,1,0:T(8,128)(2,1)S(1)}, u32[]{:S(2)}, u32[]{:S(2)}) %collective-permute-start.26) | collective-permute-done | bytes 294944 | tf_op jit(solution)/shard_map/ppermute | solution.py:742
  185.2 1.4 hidden_grads_out.3
  186.6 1.8 collective-permute-done.25.refs_4_
  188.3 0.8 head_grads_out.2
  189.1 2.0 %collective-permute-done.24.refs_4_ = bf16[1,8,64,128]{3,2,1,0:T(8,128)(2,1)S(1)} collective-permute-done((bf16[1,8,64,128]{3,2,1,0:T(8,128)(2,1)S(1)}, bf16[1,8,64,128]{3,2,1,0:T(8,128)(2,1)S(1)}, u32[]{:S(2)}, u32[]{:S(2)}) %collective-permute-start.24) | collective-permute-done | bytes 131104 | tf_op jit(solution)/shard_map/ppermute | solution.py:742
  (108 shorter events, 7.7 us)
Async XLA Ops:
  1.3 12.7 %copy-start.31 = (bf16[1024]{0:T(1024)(128)(2,1)S(1)}, bf16[1024]{0:T(1024)(128)(2,1)}, u32[]{:S(2)}) copy-start(bf16[1024]{0:T(1024)(128)(2,1)} %gain_ref.13) | copy-start | bytes 6148
  1.3 12.7 %copy-start.33 = (s32[2]{0:T(128)S(1)}, s32[2]{0:T(128)}, u32[]{:S(2)}) copy-start(s32[2]{0:T(128)} %lengths_ref.1) | copy-start | bytes 28
  1.3 18.9 %copy-start.3 = (bf16[1024,1024]{1,0:T(8,128)(2,1)S(1)}, bf16[1024,1024]{1,0:T(8,128)(2,1)}, u32[]{:S(2)}) copy-start(bf16[1024,1024]{1,0:T(8,128)(2,1)} %x_ref.9) | copy-start | bytes 6291460
  13.5 6.7 %collective-permute-start = (bf16[1024,1024]{1,0:T(8,128)(2,1)}, bf16[1024,1024]{1,0:T(8,128)(2,1)}, u32[]{:S(2)}, u32[]{:S(2)}) collective-permute-start(bf16[1024,1024]{1,0:T(8,128)(2,1)} %get-tuple-element.120.own_ref), channel_id=1, source_target_pairs={{0,1},{1,0},{2,3},{3,2},{4,5},{5,4},{6,7},{7,6},{8,9},{9,8},{10,11... | collective-permute-start | bytes 6291464 | tf_op jit(solution)/shard_map/ppermute | solution.py:734
  14.0 6.2 %copy-start.32 = (bf16[1024]{0:T(1024)(128)(2,1)S(1)}, bf16[1024]{0:T(1024)(128)(2,1)}, u32[]{:S(2)}) copy-start(bf16[1024]{0:T(1024)(128)(2,1)} %gain_ref.11) | copy-start | bytes 6148
  14.0 12.7 %copy-start.1 = (bf16[1024,2048]{1,0:T(8,128)(2,1)S(1)}, bf16[1024,2048]{1,0:T(8,128)(2,1)}, u32[]{:S(2)}) copy-start(bf16[1024,2048]{1,0:T(8,128)(2,1)} %wu_ref.3) | copy-start | bytes 12582916
  20.2 30.1 %copy-start.6 = (bf16[1024,1024]{1,0:T(8,128)(2,1)}, bf16[1024,1024]{1,0:T(8,128)(2,1)S(1)}, u32[]{:S(2)}) copy-start(bf16[1024,1024]{1,0:T(8,128)(2,1)S(1)} %get-tuple-element.128.refs_2_.seed_ref) | copy-start | bytes 6291460
  20.3 6.5 %copy-start = (bf16[1024,2048]{1,0:T(8,128)(2,1)S(1)}, bf16[1024,2048]{1,0:T(8,128)(2,1)}, u32[]{:S(2)}) copy-start(bf16[1024,2048]{1,0:T(8,128)(2,1)} %wg_ref.3) | copy-start | bytes 12582916
  47.8 46.4 %collective-permute-start.5 = (bf16[8,30,64,128]{3,2,1,0:T(8,128)(2,1)}, bf16[8,30,64,128]{3,2,1,0:T(8,128)(2,1)S(1)}, u32[]{:S(2)}, u32[]{:S(2)}) collective-permute-start(bf16[8,30,64,128]{3,2,1,0:T(8,128)(2,1)} %get-tuple-element.130), channel_id=1, source_target_pairs={{0,2},{1,5},{2,0},{3,7},{4,6},{5,1},{6,4},{7,3},{8,10},{9,13},{10,... | collective-permute-start | bytes 11796488 | tf_op jit(solution)/shard_map/ppermute | solution.py:742
  63.9 54.3 %collective-permute-start.8 = (bf16[8,18,64,128]{3,2,1,0:T(8,128)(2,1)}, bf16[8,18,64,128]{3,2,1,0:T(8,128)(2,1)S(1)}, u32[]{:S(2)}, u32[]{:S(2)}) collective-permute-start(bf16[8,18,64,128]{3,2,1,0:T(8,128)(2,1)} %get-tuple-element.141), channel_id=1, source_target_pairs={{0,8},{1,17},{2,10},{3,19},{4,12},{5,21},{6,14},{7,23},{8,0},{9,25... | collective-permute-start | bytes 7077896 | tf_op jit(solution)/shard_map/ppermute | solution.py:742
  70.7 7.1 %collective-permute-start.3 = (bf16[256,1024]{1,0:T(8,128)(2,1)S(1)}, bf16[256,1024]{1,0:T(8,128)(2,1)S(1)}, u32[]{:S(2)}, u32[]{:S(2)}) collective-permute-start(bf16[256,1024]{1,0:T(8,128)(2,1)S(1)} %get-tuple-element.149.refs_0_), channel_id=1, source_target_pairs={{0,1},{1,0},{2,3},{3,2},{4,5},{5,4},{6,7},{7,6},{8,9},{9,8},{10,11... | collective-permute-start | bytes 1572872 | tf_op jit(solution)/shard_map/ppermute | solution.py:734
  71.7 6.1 %copy-start.7 = (bf16[1024,1024]{1,0:T(8,128)(2,1)S(1)}, bf16[1024,1024]{1,0:T(8,128)(2,1)}, u32[]{:S(2)}) copy-start(bf16[1024,1024]{1,0:T(8,128)(2,1)} %copy-done.6) | copy-start | bytes 6291460
  71.8 6.1 %copy-start.9 = (bf16[1024,1024]{1,0:T(8,128)(2,1)S(1)}, bf16[1024,1024]{1,0:T(8,128)(2,1)}, u32[]{:S(2)}) copy-start(bf16[1024,1024]{1,0:T(8,128)(2,1)} %get-tuple-element.124.mid_ref) | copy-start | bytes 6291460
  71.8 6.1 %copy-start.18 = (bf16[512,1024]{1,0:T(8,128)(2,1)S(1)}, bf16[512,1024]{1,0:T(8,128)(2,1)}, u32[]{:S(2)}) copy-start(bf16[512,1024]{1,0:T(8,128)(2,1)} %wo_ref.5) | copy-start | bytes 3145732
  71.8 6.1 %collective-permute-start.4 = (bf16[256,1024]{1,0:T(8,128)(2,1)S(1)}, bf16[256,1024]{1,0:T(8,128)(2,1)S(1)}, u32[]{:S(2)}, u32[]{:S(2)}) collective-permute-start(bf16[256,1024]{1,0:T(8,128)(2,1)S(1)} %get-tuple-element.150.refs_1_), channel_id=1, source_target_pairs={{0,1},{1,0},{2,3},{3,2},{4,5},{5,4},{6,7},{7,6},{8,9},{9,8},{10,11... | collective-permute-start | bytes 1572872 | tf_op jit(solution)/shard_map/ppermute | solution.py:734
  77.3 4.3 %collective-permute-start.1 = (bf16[256,1024]{1,0:T(8,128)(2,1)S(1)}, bf16[256,1024]{1,0:T(8,128)(2,1)S(1)}, u32[]{:S(2)}, u32[]{:S(2)}) collective-permute-start(bf16[256,1024]{1,0:T(8,128)(2,1)S(1)} %get-tuple-element.154.refs_0_), channel_id=1, source_target_pairs={{0,1},{1,0},{2,3},{3,2},{4,5},{5,4},{6,7},{7,6},{8,9},{9,8},{10,11... | collective-permute-start | bytes 1572872 | tf_op jit(solution)/shard_map/ppermute | solution.py:734
  77.8 3.8 %collective-permute-start.2 = (bf16[256,1024]{1,0:T(8,128)(2,1)S(1)}, bf16[256,1024]{1,0:T(8,128)(2,1)S(1)}, u32[]{:S(2)}, u32[]{:S(2)}) collective-permute-start(bf16[256,1024]{1,0:T(8,128)(2,1)S(1)} %get-tuple-element.155.refs_1_), channel_id=1, source_target_pairs={{0,1},{1,0},{2,3},{3,2},{4,5},{5,4},{6,7},{7,6},{8,9},{9,8},{10,11... | collective-permute-start | bytes 1572872 | tf_op jit(solution)/shard_map/ppermute | solution.py:734
  81.6 4.3 %copy-start.26 = (bf16[1024,512]{1,0:T(8,128)(2,1)S(1)}, bf16[1024,512]{1,0:T(8,128)(2,1)}, u32[]{:S(2)}) copy-start(bf16[1024,512]{1,0:T(8,128)(2,1)} %get-tuple-element.138.v_ref) | copy-start | bytes 3145732
  85.9 8.3 %copy-start.2 = (bf16[8,30,64,128]{3,2,1,0:T(8,128)(2,1)S(1)}, bf16[8,30,64,128]{3,2,1,0:T(8,128)(2,1)}, u32[]{:S(2)}) copy-start(bf16[8,30,64,128]{3,2,1,0:T(8,128)(2,1)} %get-tuple-element.161.refs_0_) | copy-start | bytes 11796484
  94.2 4.1 %copy-start.22 = (bf16[1024,1024]{1,0:T(8,128)(2,1)S(1)}, bf16[1024,1024]{1,0:T(8,128)(2,1)}, u32[]{:S(2)}) copy-start(bf16[1024,1024]{1,0:T(8,128)(2,1)} %get-tuple-element.139.p_ref) | copy-start | bytes 6291460
  95.7 32.1 %collective-permute-start.14 = (bf16[4,30,64,128]{3,2,1,0:T(8,128)(2,1)}, bf16[4,30,64,128]{3,2,1,0:T(8,128)(2,1)S(1)}, u32[]{:S(2)}, u32[]{:S(2)}) collective-permute-start(bf16[4,30,64,128]{3,2,1,0:T(8,128)(2,1)} %next_send.12), channel_id=1, source_target_pairs={{0,4},{1,3},{2,6},{3,1},{4,0},{5,7},{6,2},{7,5},{8,12},{9,11},{10,... | collective-permute-start | bytes 5898248 | tf_op jit(solution)/shard_map/ppermute | solution.py:742
  97.8 8.0 %collective-permute-start.9 = (bf16[256,1024]{1,0:T(8,128)(2,1)S(1)}, bf16[256,1024]{1,0:T(8,128)(2,1)S(1)}, u32[]{:S(2)}, u32[]{:S(2)}) collective-permute-start(bf16[256,1024]{1,0:T(8,128)(2,1)S(1)} %get-tuple-element.177.refs_0_), channel_id=1, source_target_pairs={{0,1},{1,0},{2,3},{3,2},{4,5},{5,4},{6,7},{7,6},{8,9},{9,8},{10,11... | collective-permute-start | bytes 1572872 | tf_op jit(solution)/shard_map/ppermute | solution.py:734
  97.8 12.2 %collective-permute-start.10 = (bf16[256,1024]{1,0:T(8,128)(2,1)S(1)}, bf16[256,1024]{1,0:T(8,128)(2,1)S(1)}, u32[]{:S(2)}, u32[]{:S(2)}) collective-permute-start(bf16[256,1024]{1,0:T(8,128)(2,1)S(1)} %get-tuple-element.178.refs_1_), channel_id=1, source_target_pairs={{0,1},{1,0},{2,3},{3,2},{4,5},{5,4},{6,7},{7,6},{8,9},{9,8},{10,11... | collective-permute-start | bytes 1572872 | tf_op jit(solution)/shard_map/ppermute | solution.py:734
  98.3 8.0 %copy-start.19 = (bf16[16,64,1024]{2,1,0:T(8,128)(2,1)S(1)}, bf16[16,64,1024]{2,1,0:T(8,128)(2,1)}, u32[]{:S(2)}) copy-start(bf16[16,64,1024]{2,1,0:T(8,128)(2,1)} %get-tuple-element.122.turned_ref.value_ref) | copy-start | bytes 6291460
  105.7 12.9 %collective-permute-start.6 = (bf16[256,1024]{1,0:T(8,128)(2,1)S(1)}, bf16[256,1024]{1,0:T(8,128)(2,1)S(1)}, u32[]{:S(2)}, u32[]{:S(2)}) collective-permute-start(bf16[256,1024]{1,0:T(8,128)(2,1)S(1)} %get-tuple-element.183.refs_0_), channel_id=1, source_target_pairs={{0,1},{1,0},{2,3},{3,2},{4,5},{5,4},{6,7},{7,6},{8,9},{9,8},{10,11... | collective-permute-start | bytes 1572872 | tf_op jit(solution)/shard_map/ppermute | solution.py:734
  105.8 12.8 %collective-permute-start.7 = (bf16[256,1024]{1,0:T(8,128)(2,1)S(1)}, bf16[256,1024]{1,0:T(8,128)(2,1)S(1)}, u32[]{:S(2)}, u32[]{:S(2)}) collective-permute-start(bf16[256,1024]{1,0:T(8,128)(2,1)S(1)} %get-tuple-element.184.refs_1_), channel_id=1, source_target_pairs={{0,1},{1,0},{2,3},{3,2},{4,5},{5,4},{6,7},{7,6},{8,9},{9,8},{10,11... | collective-permute-start | bytes 1572872 | tf_op jit(solution)/shard_map/ppermute | solution.py:734
  106.2 5.3 %copy-start.28 = (bf16[512,1024]{1,0:T(8,128)(2,1)S(1)}, bf16[512,1024]{1,0:T(8,128)(2,1)}, u32[]{:S(2)}) copy-start(bf16[512,1024]{1,0:T(8,128)(2,1)} %get-tuple-element.173.gm_ref) | copy-start | bytes 3145732
  110.0 30.6 %collective-permute-start.13 = (bf16[8,8,64,128]{3,2,1,0:T(8,128)(2,1)}, bf16[8,8,64,128]{3,2,1,0:T(8,128)(2,1)S(1)}, u32[]{:S(2)}, u32[]{:S(2)}) collective-permute-start(bf16[8,8,64,128]{3,2,1,0:T(8,128)(2,1)} %get-tuple-element.176), channel_id=1, source_target_pairs={{0,8},{1,17},{2,10},{3,19},{4,12},{5,21},{6,14},{7,23},{8,0},{9,25... | collective-permute-start | bytes 3145736 | tf_op jit(solution)/shard_map/ppermute | solution.py:742
  111.5 6.6 %copy-start.4 = (bf16[8,18,64,128]{3,2,1,0:T(8,128)(2,1)S(1)}, bf16[8,18,64,128]{3,2,1,0:T(8,128)(2,1)}, u32[]{:S(2)}) copy-start(bf16[8,18,64,128]{3,2,1,0:T(8,128)(2,1)} %get-tuple-element.172.refs_0_) | copy-start | bytes 7077892
  118.4 22.4 %collective-permute-start.12 = (bf16[4,18,64,128]{3,2,1,0:T(8,128)(2,1)S(1)}, bf16[4,18,64,128]{3,2,1,0:T(8,128)(2,1)S(1)}, u32[]{:S(2)}, u32[]{:S(2)}) collective-permute-start(bf16[4,18,64,128]{3,2,1,0:T(8,128)(2,1)S(1)} %next_send.13), channel_id=1, source_target_pairs={{0,2},{1,5},{2,0},{3,7},{4,6},{5,1},{6,4},{7,3},{8,10},{9,13},{10,... | collective-permute-start | bytes 3538952 | tf_op jit(solution)/shard_map/ppermute | solution.py:742
  126.6 14.0 %copy-start.13 = (bf16[8,8,64,128]{3,2,1,0:T(8,128)(2,1)S(1)}, bf16[8,8,64,128]{3,2,1,0:T(8,128)(2,1)}, u32[]{:S(2)}) copy-start(bf16[8,8,64,128]{3,2,1,0:T(8,128)(2,1)} %get-tuple-element.194.refs_0_) | copy-start | bytes 3145732
  126.6 20.7 %collective-permute-start.11 = (bf16[8,9,64,128]{3,2,1,0:T(8,128)(2,1)S(1)}, bf16[8,9,64,128]{3,2,1,0:T(8,128)(2,1)S(1)}, u32[]{:S(2)}, u32[]{:S(2)}) collective-permute-start(bf16[8,9,64,128]{3,2,1,0:T(8,128)(2,1)S(1)} %get-tuple-element.193), channel_id=1, source_target_pairs={{0,2},{1,5},{2,0},{3,7},{4,6},{5,1},{6,4},{7,3},{8,10},{9,13},{10,... | collective-permute-start | bytes 3538952 | tf_op jit(solution)/shard_map/ppermute | solution.py:742
  129.1 32.6 %collective-permute-start.21 = (bf16[2,30,64,128]{3,2,1,0:T(8,128)(2,1)S(1)}, bf16[2,30,64,128]{3,2,1,0:T(8,128)(2,1)S(1)}, u32[]{:S(2)}, u32[]{:S(2)}) collective-permute-start(bf16[2,30,64,128]{3,2,1,0:T(8,128)(2,1)S(1)} %next_send.14), channel_id=1, source_target_pairs={{0,8},{1,17},{2,10},{3,19},{4,12},{5,21},{6,14},{7,23},{8,0},{9,25... | collective-permute-start | bytes 2949128 | tf_op jit(solution)/shard_map/ppermute | solution.py:742
  140.6 7.7 %copy-start.14 = (bf16[1024,2048]{1,0:T(8,128)(2,1)S(1)}, bf16[1024,2048]{1,0:T(8,128)(2,1)}, u32[]{:S(2)}) copy-start(bf16[1024,2048]{1,0:T(8,128)(2,1)} %get-tuple-element.199.h_ref) | copy-start | bytes 12582916
  140.8 6.6 %copy-start.8 = (bf16[8,9,64,128]{3,2,1,0:T(8,128)(2,1)S(1)}, bf16[8,9,64,128]{3,2,1,0:T(8,128)(2,1)}, u32[]{:S(2)}) copy-start(bf16[8,9,64,128]{3,2,1,0:T(8,128)(2,1)} %get-tuple-element.192.refs_0_) | copy-start | bytes 3538948
  140.8 15.8 %collective-permute-start.19 = (bf16[4,8,64,128]{3,2,1,0:T(8,128)(2,1)S(1)}, bf16[4,8,64,128]{3,2,1,0:T(8,128)(2,1)S(1)}, u32[]{:S(2)}, u32[]{:S(2)}) collective-permute-start(bf16[4,8,64,128]{3,2,1,0:T(8,128)(2,1)S(1)} %next_send.15), channel_id=1, source_target_pairs={{0,2},{1,5},{2,0},{3,7},{4,6},{5,1},{6,4},{7,3},{8,10},{9,13},{10,... | collective-permute-start | bytes 1572872 | tf_op jit(solution)/shard_map/ppermute | solution.py:742
  140.9 7.5 %copy-start.5 = (bf16[2048,1024]{1,0:T(8,128)(2,1)S(1)}, bf16[2048,1024]{1,0:T(8,128)(2,1)}, u32[]{:S(2)}) copy-start(bf16[2048,1024]{1,0:T(8,128)(2,1)} %wd_ref.1) | copy-start | bytes 12582916
  147.5 10.8 %collective-permute-start.18 = (bf16[4,9,64,128]{3,2,1,0:T(8,128)(2,1)S(1)}, bf16[4,9,64,128]{3,2,1,0:T(8,128)(2,1)S(1)}, u32[]{:S(2)}, u32[]{:S(2)}) collective-permute-start(bf16[4,9,64,128]{3,2,1,0:T(8,128)(2,1)S(1)} %next_send.17), channel_id=1, source_target_pairs={{0,4},{1,3},{2,6},{3,1},{4,0},{5,7},{6,2},{7,5},{8,12},{9,11},{10,... | collective-permute-start | bytes 1769480 | tf_op jit(solution)/shard_map/ppermute | solution.py:742
  154.1 19.0 %collective-permute-start.15 = (bf16[512,1024]{1,0:T(8,128)(2,1)S(1)}, bf16[512,1024]{1,0:T(8,128)(2,1)S(1)}, u32[]{:S(2)}, u32[]{:S(2)}) collective-permute-start(bf16[512,1024]{1,0:T(8,128)(2,1)S(1)} %get-tuple-element.207.refs_0_), channel_id=1, source_target_pairs={{0,1},{1,0},{2,3},{3,2},{4,5},{5,4},{6,7},{7,6},{8,9},{9,8},{10,11... | collective-permute-start | bytes 3145736 | tf_op jit(solution)/shard_map/ppermute | solution.py:734
  154.2 21.8 %collective-permute-start.16 = (bf16[512,1024]{1,0:T(8,128)(2,1)S(1)}, bf16[512,1024]{1,0:T(8,128)(2,1)S(1)}, u32[]{:S(2)}, u32[]{:S(2)}) collective-permute-start(bf16[512,1024]{1,0:T(8,128)(2,1)S(1)} %get-tuple-element.208.refs_1_), channel_id=1, source_target_pairs={{0,1},{1,0},{2,3},{3,2},{4,5},{5,4},{6,7},{7,6},{8,9},{9,8},{10,11... | collective-permute-start | bytes 3145736 | tf_op jit(solution)/shard_map/ppermute | solution.py:734
  156.6 16.3 %collective-permute-start.17 = (bf16[2,18,64,128]{3,2,1,0:T(8,128)(2,1)S(1)}, bf16[2,18,64,128]{3,2,1,0:T(8,128)(2,1)S(1)}, u32[]{:S(2)}, u32[]{:S(2)}) collective-permute-start(bf16[2,18,64,128]{3,2,1,0:T(8,128)(2,1)S(1)} %next_send.16), channel_id=1, source_target_pairs={{0,4},{1,3},{2,6},{3,1},{4,0},{5,7},{6,2},{7,5},{8,12},{9,11},{10,... | collective-permute-start | bytes 1769480 | tf_op jit(solution)/shard_map/ppermute | solution.py:742
  156.7 5.0 %copy-start.12 = (bf16[4,30,64,128]{3,2,1,0:T(8,128)(2,1)S(1)}, bf16[4,30,64,128]{3,2,1,0:T(8,128)(2,1)}, u32[]{:S(2)}) copy-start(bf16[4,30,64,128]{3,2,1,0:T(8,128)(2,1)} %copy-done.11) | copy-start | bytes 5898244
  158.4 12.9 %collective-permute-start.20 = (bf16[2,9,64,128]{3,2,1,0:T(8,128)(2,1)S(1)}, bf16[2,9,64,128]{3,2,1,0:T(8,128)(2,1)S(1)}, u32[]{:S(2)}, u32[]{:S(2)}) collective-permute-start(bf16[2,9,64,128]{3,2,1,0:T(8,128)(2,1)S(1)} %next_send.19), channel_id=1, source_target_pairs={{0,8},{1,17},{2,10},{3,19},{4,12},{5,21},{6,14},{7,23},{8,0},{9,25... | collective-permute-start | bytes 884744 | tf_op jit(solution)/shard_map/ppermute | solution.py:742
  161.9 16.9 %collective-permute-start.23 = (bf16[1,30,64,128]{3,2,1,0:T(8,128)(2,1)S(1)}, bf16[1,30,64,128]{3,2,1,0:T(8,128)(2,1)S(1)}, u32[]{:S(2)}, u32[]{:S(2)}) collective-permute-start(bf16[1,30,64,128]{3,2,1,0:T(8,128)(2,1)S(1)} %next_send.20), channel_id=1, source_target_pairs={{0,16},{1,9},{2,18},{3,11},{4,20},{5,13},{6,22},{7,15},{8,24},{9,1... | collective-permute-start | bytes 1474568 | tf_op jit(solution)/shard_map/ppermute | solution.py:742
  171.3 8.6 %collective-permute-start.22 = (bf16[2,8,64,128]{3,2,1,0:T(8,128)(2,1)S(1)}, bf16[2,8,64,128]{3,2,1,0:T(8,128)(2,1)S(1)}, u32[]{:S(2)}, u32[]{:S(2)}) collective-permute-start(bf16[2,8,64,128]{3,2,1,0:T(8,128)(2,1)S(1)} %next_send.18), channel_id=1, source_target_pairs={{0,4},{1,3},{2,6},{3,1},{4,0},{5,7},{6,2},{7,5},{8,12},{9,11},{10,... | collective-permute-start | bytes 786440 | tf_op jit(solution)/shard_map/ppermute | solution.py:742
  173.0 12.1 %collective-permute-start.26 = (bf16[1,18,64,128]{3,2,1,0:T(8,128)(2,1)S(1)}, bf16[1,18,64,128]{3,2,1,0:T(8,128)(2,1)S(1)}, u32[]{:S(2)}, u32[]{:S(2)}) collective-permute-start(bf16[1,18,64,128]{3,2,1,0:T(8,128)(2,1)S(1)} %next_send.22), channel_id=1, source_target_pairs={{0,16},{1,9},{2,18},{3,11},{4,20},{5,13},{6,22},{7,15},{8,24},{9,1... | collective-permute-start | bytes 884744 | tf_op jit(solution)/shard_map/ppermute | solution.py:742
  173.1 15.2 %collective-permute-start.25 = (bf16[1,9,64,128]{3,2,1,0:T(8,128)(2,1)S(1)}, bf16[1,9,64,128]{3,2,1,0:T(8,128)(2,1)S(1)}, u32[]{:S(2)}, u32[]{:S(2)}) collective-permute-start(bf16[1,9,64,128]{3,2,1,0:T(8,128)(2,1)S(1)} %next_send.21), channel_id=1, source_target_pairs={{0,16},{1,9},{2,18},{3,11},{4,20},{5,13},{6,22},{7,15},{8,24},{9,1... | collective-permute-start | bytes 442376 | tf_op jit(solution)/shard_map/ppermute | solution.py:742
  180.0 11.1 %collective-permute-start.24 = (bf16[1,8,64,128]{3,2,1,0:T(8,128)(2,1)S(1)}, bf16[1,8,64,128]{3,2,1,0:T(8,128)(2,1)S(1)}, u32[]{:S(2)}, u32[]{:S(2)}) collective-permute-start(bf16[1,8,64,128]{3,2,1,0:T(8,128)(2,1)S(1)} %next_send.23), channel_id=1, source_target_pairs={{0,16},{1,9},{2,18},{3,11},{4,20},{5,13},{6,22},{7,15},{8,24},{9,1... | collective-permute-start | bytes 393224 | tf_op jit(solution)/shard_map/ppermute | solution.py:742
  (13 other events, 36.8 us)

commit v3 on v2

--- a/solution.py
+++ b/solution.py
@@ -185,7 +185,7 @@
         outs,
         vmem=24,
         cost=(8 * rows * width * heads, 12 * MIB),
-        far=(0, 2, 3, 4, 5),
+        far=(0, 1, 2, 3, 4, 5),
     )(x, gain, wq, wk, wv, wo)
 
 

time: 192 us -> 192 us (level)
  no operation moved by 1% of the time
where the time goes in v3:
time: 192 us; the launch traced here: 191 us
  Pallas kernels  120 us (62%)
  waiting for transfers between devices  41.8 us (22%)
  starting transfers between devices  25.1 us (13%)
  local copies, waits for them, and re-layouts  2.83 us (1%)
    pallas_call x33, Pallas kernels, run(): kernel(*(pltpu.with_memory_space_constraint(arg, pltpu.HBM) if n - scalar...  120 us
    ppermute x16, waiting for transfers between devices, hop_swap(): return lax.ppermute(array, ('dp', 'tensor'), pairs)  41.8 us
    ppermute x16, starting transfers between devices, hop_swap(): return lax.ppermute(array, ('dp', 'tensor'), pairs)  21.2 us
  transfers between devices with their start and end apart: 27, of which 12 were waited for; matrix products, arithmetic and copies ran while one was open for 0% of the time, Pallas kernels for 42%

profile of v3, /device:TPU:0, one launch (start us, length us, event | category | flops | bytes accessed | tf_op | source)
XLA Modules:
  0.0 191.2 jit_solution(18124725717857321939)
XLA Ops:
  0.7 12.3 %attention_forward.1 = (bf16[1024,512]{1,0:T(8,128)(2,1)}, bf16[1024,512]{1,0:T(8,128)(2,1)}, bf16[1024,512]{1,0:T(8,128)(2,1)}, bf16[1024,512]{1,0:T(8,128)(2,1...) custom-call(bf16[1024,1024]{1,0:T(8,128)(2,1)} %x_ref.9, bf16[1024]{0:T(1024)(128)(2,1)} %gain_ref.13, ...), custom_call_target="tpu_custom_call" | custom-call | flops 4294 | tf_op jit(solution)/shard_map/attention_forward/pallas_call | solution.py:63
  13.5 6.2 %seed_rows.1 = (bf16[1024,1024]{1,0:T(8,128)(2,1)S(1)}, bf16[16,64,1024]{2,1,0:T(8,128)(2,1)S(1)}, bf16[16,64,1024]{2,1,0:T(8,128)(2,1)}) custom-call(s32[2]{0:T(128)S(1)} %copy-done.32, s32[2]{0:T(128)S(1)} %pad_add_fusion.me_ref, bf16[1024,1024]{1,0:T(8,128)(2,1)} %cot_ref, bf16[1024,1024]{1,0:T(8,128)(2,1)} %x_ref.9, bf16[1024]{0:T(1024)(128)(2,1)S(1)} %copy-done.30), custom_call_target="tpu_custom_call" | custom-call | flops 4 | tf_op jit(solution)/shard_map/seed_rows/pallas_call | solution.py:63
  19.7 6.5 %middle_rows.1 = (bf16[1024,1024]{1,0:T(8,128)(2,1)}, bf16[1024,1024]{1,0:T(8,128)(2,1)S(1)}, bf16[16,64,1024]{2,1,0:T(8,128)(2,1)S(1)}) custom-call(s32[2]{0:T(128)S(1)} %pad_add_fusion.me_ref, bf16[1024,1024]{1,0:T(8,128)(2,1)S(1)} %copy-done.3, bf16[1024,1024]{1,0:T(8,128)(2,1)} %get-tuple-element.120.own_ref, ...), custom_call_target="tpu_custom_call" | custom-call | flops 8 | tf_op jit(solution)/shard_map/middle_rows/pallas_call | solution.py:63
  26.2 21.0 %hidden_units.2 = (bf16[1024,2048]{1,0:T(8,128)(2,1)}, bf16[1024,2048]{1,0:T(8,128)(2,1)S(1)}, bf16[1024,2048]{1,0:T(8,128)(2,1)S(1)}, bf16[8,30,64,128]{3,2,1,0:T(8,128)(2,1)}, bf16[8,30,64,128]{3,2,1,0:T(8,128)(2,1)}) custom-call(bf16[1024,1024]{1,0:T(8,128)(2,1)S(1)} %get-tuple-element.131.refs_0_, bf16[16,64,1024]{2,1,0:T(8,128)(2,1)S(1)} %get-tuple-element.126.refs_1_, ...), custom_call_target="tpu_custom_call" | custom-call | flops 16106 | tf_op jit(solution)/shard_map/hidden_units/pallas_call | solution.py:63
  47.2 2.5 %collective-permute-start.5 = (bf16[8,30,64,128]{3,2,1,0:T(8,128)(2,1)}, bf16[8,30,64,128]{3,2,1,0:T(8,128)(2,1)S(1)}, u32[]{:S(2)}, u32[]{:S(2)}) collective-permute-start(bf16[8,30,64,128]{3,2,1,0:T(8,128)(2,1)} %get-tuple-element.130), channel_id=1, source_target_pairs={{0,2},{1,5},{2,0},{3,7},{4,6},{5,1},{6,4},{7,3},{8,10},{9,13},{10,... | collective-permute-start | bytes 11796488 | tf_op jit(solution)/shard_map/ppermute | solution.py:742
  49.7 13.5 %hidden_units.3 = (bf16[1024,2048]{1,0:T(8,128)(2,1)}, bf16[1024,2048]{1,0:T(8,128)(2,1)S(1)}, bf16[1024,2048]{1,0:T(8,128)(2,1)S(1)}, bf16[8,18,64,128]{3,2,1,0:T(8,128)(2,1)}, bf16[8,18,64,128]{3,2,1,0:T(8,128)(2,1)}) custom-call(bf16[1024,1024]{1,0:T(8,128)(2,1)S(1)} %get-tuple-element.131.refs_0_, ...), custom_call_target="tpu_custom_call", output_to_operand_aliasing={{0}: (7, {}), {1}: (8, {}), {2}: (9, {})} | custom-call | flops 9663 | tf_op jit(solution)/shard_map/hidden_units/pallas_call | solution.py:63
  63.3 1.6 collective-permute-start.8
  64.8 5.3 %normed_two_back.2 = (bf16[256,1024]{1,0:T(8,128)(2,1)S(1)}, bf16[256,1024]{1,0:T(8,128)(2,1)S(1)}) custom-call(bf16[1024,2048]{1,0:T(8,128)(2,1)S(1)} %get-tuple-element.145.gg_ref, bf16[1024,2048]{1,0:T(8,128)(2,1)S(1)} %get-tuple-element.143.gu_ref, bf16[1024,2048]{1,0:T(8,128)(2,1)S(1)} %copy-done, bf16[1024,2048]{1,0:T(8,128)(2,1)S(1)} %copy-done.1), custom_call_target="tpu_custom_call" | custom-call | flops 4294 | tf_op jit(solution)/shard_map/normed_two_back/pallas_call | solution.py:63
  70.1 1.0 collective-permute-start.3
  71.2 5.4 %normed_two_back.3 = (bf16[256,1024]{1,0:T(8,128)(2,1)S(1)}, bf16[256,1024]{1,0:T(8,128)(2,1)S(1)}) custom-call(bf16[1024,2048]{1,0:T(8,128)(2,1)S(1)} %get-tuple-element.145.gg_ref, bf16[1024,2048]{1,0:T(8,128)(2,1)S(1)} %get-tuple-element.143.gu_ref, bf16[1024,2048]{1,0:T(8,128)(2,1)S(1)} %copy-done, bf16[1024,2048]{1,0:T(8,128)(2,1)S(1)} %copy-done.1), custom_call_target="tpu_custom_call" | custom-call | flops 4294 | tf_op jit(solution)/shard_map/normed_two_back/pallas_call | solution.py:63
  77.3 3.7 %middle_backward.2 = (bf16[16,64,1024]{2,1,0:T(8,128)(2,1)}, bf16[1024,512]{1,0:T(8,128)(2,1)}, bf16[512,1024]{1,0:T(8,128)(2,1)}, f32[1,1024]{1,0:T(1,128)S(1)}) custom-call(s32[2]{0:T(128)S(1)} %pad_add_fusion.me_ref, bf16[1024,1024]{1,0:T(8,128)(2,1)S(1)} %copy-done.9, bf16[1024,1024]{1,0:T(8,128)(2,1)S(1)} %copy-done.7, bf16[1024]{0:T(1024)(128)(2,1)S(1)} %copy-done.31, ...), custom_call_target="tpu_custom_call" | custom-call | flops 536 | tf_op jit(solution)/shard_map/middle_backward/pallas_call | solution.py:63
  81.1 3.7 %middle_backward.3 = (bf16[16,64,1024]{2,1,0:T(8,128)(2,1)}, bf16[1024,512]{1,0:T(8,128)(2,1)}, bf16[512,1024]{1,0:T(8,128)(2,1)}, f32[1,1024]{1,0:T(1,128)S(1)}) custom-call(s32[2]{0:T(128)S(1)} %pad_add_fusion.me_ref, bf16[1024,1024]{1,0:T(8,128)(2,1)S(1)} %copy-done.9, ...), custom_call_target="tpu_custom_call", output_to_operand_aliasing={{0}: (9, {}), {1}: (10, {})} | custom-call | flops 536 | tf_op jit(solution)/shard_map/middle_backward/pallas_call | solution.py:63
  85.3 7.4 %attention_backward.2 = (bf16[1024,1536]{1,0:T(8,128)(2,1)S(1)}, bf16[256,1024]{1,0:T(8,128)(2,1)S(1)}, bf16[256,1024]{1,0:T(8,128)(2,1)S(1)}) custom-call(bf16[1024,512]{1,0:T(8,128)(2,1)S(1)} %copy-done.24, bf16[1024,512]{1,0:T(8,128)(2,1)S(1)} %copy-done.25, bf16[1024,512]{1,0:T(8,128)(2,1)S(1)} %copy-done.26, bf16[1024,1024]{1,0:T(8,128)(2,1)S(1)} %copy-done.21, ...), custom_call_target="tpu_custom_call" | custom-call | flops 1610 | tf_op jit(solution)/shard_map/attention_backward/pallas_call | solution.py:63
  92.7 0.9 collective-permute-done.5.refs_1_
  93.6 1.5 next_send.12
  95.2 2.1 %collective-permute-start.14 = (bf16[4,30,64,128]{3,2,1,0:T(8,128)(2,1)}, bf16[4,30,64,128]{3,2,1,0:T(8,128)(2,1)S(1)}, u32[]{:S(2)}, u32[]{:S(2)}) collective-permute-start(bf16[4,30,64,128]{3,2,1,0:T(8,128)(2,1)} %next_send.12), channel_id=1, source_target_pairs={{0,4},{1,3},{2,6},{3,1},{4,0},{5,7},{6,2},{7,5},{8,12},{9,11},{10,... | collective-permute-start | bytes 5898248 | tf_op jit(solution)/shard_map/ppermute | solution.py:742
  97.7 7.4 %attention_backward.3 = (bf16[1024,1536]{1,0:T(8,128)(2,1)S(1)}, bf16[256,1024]{1,0:T(8,128)(2,1)S(1)}, bf16[256,1024]{1,0:T(8,128)(2,1)S(1)}) custom-call(bf16[1024,512]{1,0:T(8,128)(2,1)S(1)} %copy-done.24, bf16[1024,512]{1,0:T(8,128)(2,1)S(1)} %copy-done.25, bf16[1024,512]{1,0:T(8,128)(2,1)S(1)} %copy-done.26, ...), custom_call_target="tpu_custom_call", output_to_operand_aliasing={{0}: (8, {})} | custom-call | flops 1610 | tf_op jit(solution)/shard_map/attention_backward/pallas_call | solution.py:63
  105.7 3.7 %query_key_grads.1 = (bf16[8,8,64,128]{3,2,1,0:T(8,128)(2,1)}, bf16[8,8,64,128]{3,2,1,0:T(8,128)(2,1)}) custom-call(bf16[16,64,1024]{2,1,0:T(8,128)(2,1)S(1)} %copy-done.19, bf16[1024,1536]{1,0:T(8,128)(2,1)S(1)} %get-tuple-element.189.right_ref), custom_call_target="tpu_custom_call" | custom-call | flops 2147 | tf_op jit(solution)/shard_map/query_key_grads/pallas_call | solution.py:63
  109.4 1.6 collective-permute-start.13
  111.0 2.3 %input_grad.2 = (bf16[1024,1024]{1,0:T(8,128)(2,1)}, f32[1,1024]{1,0:T(1,128)S(1)}) custom-call(bf16[1024,1024]{1,0:T(8,128)(2,1)S(1)} %copy-done.3, bf16[512,1024]{1,0:T(8,128)(2,1)S(1)} %copy-done.28, bf16[1024]{0:T(1024)(128)(2,1)S(1)} %copy-done.30, bf16[256,1024]{1,0:T(8,128)(2,1)S(1)} %get-tuple-element.177.refs_0_, ...), custom_call_target="tpu_custom_call" | custom-call | flops 5 | tf_op jit(solution)/shard_map/input_grad/pallas_call | solution.py:63
  113.3 4.2 %collective-permute-done.8.refs_1_ = bf16[8,18,64,128]{3,2,1,0:T(8,128)(2,1)S(1)} collective-permute-done((bf16[8,18,64,128]{3,2,1,0:T(8,128)(2,1)}, bf16[8,18,64,128]{3,2,1,0:T(8,128)(2,1)S(1)}, u32[]{:S(2)}, u32[]{:S(2)}) %collective-permute-start.8) | collective-permute-done | bytes 2359328 | tf_op jit(solution)/shard_map/ppermute | solution.py:742
  117.9 0.8 copy-done.29
  118.8 2.3 %input_grad.3 = (bf16[1024,1024]{1,0:T(8,128)(2,1)}, f32[1,1024]{1,0:T(1,128)S(1)}) custom-call(bf16[1024,1024]{1,0:T(8,128)(2,1)S(1)} %copy-done.3, bf16[512,1024]{1,0:T(8,128)(2,1)S(1)} %copy-done.29, bf16[1024]{0:T(1024)(128)(2,1)S(1)} %copy-done.30, bf16[256,1024]{1,0:T(8,128)(2,1)S(1)} %get-tuple-element.183.refs_0_, ...), custom_call_target="tpu_custom_call", output_to_operand_aliasing={{0}: (7, {})} | custom-call | flops 5 | tf_op jit(solution)/shard_map/input_grad/pallas_call | solution.py:63
  121.6 4.4 %value_out_grads.1 = (bf16[8,9,64,128]{3,2,1,0:T(8,128)(2,1)}, bf16[8,9,64,128]{3,2,1,0:T(8,128)(2,1)S(1)}) custom-call(bf16[16,64,1024]{2,1,0:T(8,128)(2,1)S(1)} %copy-done.20, bf16[1024,1536]{1,0:T(8,128)(2,1)S(1)} %get-tuple-element.189.right_ref, bf16[16,64,1024]{2,1,0:T(8,128)(2,1)S(1)} %copy-done.23, bf16[1024,512]{1,0:T(8,128)(2,1)S(1)} %copy-done.27, ...), custom_call_target="tpu_custom_call" | custom-call | flops 2147 | tf_op jit(solution)/shard_map/value_out_grads/pallas_call | solution.py:63
  126.0 1.2 collective-permute-start.11
  127.6 0.9 copy-done.11
  128.4 1.4 collective-permute-start.21
  129.8 10.2 %collective-permute-done.13.refs_1_ = bf16[8,8,64,128]{3,2,1,0:T(8,128)(2,1)S(1)} collective-permute-done((bf16[8,8,64,128]{3,2,1,0:T(8,128)(2,1)}, bf16[8,8,64,128]{3,2,1,0:T(8,128)(2,1)S(1)}, u32[]{:S(2)}, u32[]{:S(2)}) %collective-permute-start.13) | collective-permute-done | bytes 1048608 | tf_op jit(solution)/shard_map/ppermute | solution.py:742
  140.5 6.2 %collective-permute-done.11.refs_1_ = bf16[8,9,64,128]{3,2,1,0:T(8,128)(2,1)S(1)} collective-permute-done((bf16[8,9,64,128]{3,2,1,0:T(8,128)(2,1)S(1)}, bf16[8,9,64,128]{3,2,1,0:T(8,128)(2,1)S(1)}, u32[]{:S(2)}, u32[]{:S(2)}) %collective-permute-start.11) | collective-permute-done | bytes 1179680 | tf_op jit(solution)/shard_map/ppermute | solution.py:742
  146.9 0.8 collective-permute-start.18
  147.7 5.8 %hidden_down.1 = (bf16[512,1024]{1,0:T(8,128)(2,1)S(1)}, bf16[512,1024]{1,0:T(8,128)(2,1)S(1)}) custom-call(bf16[1024,2048]{1,0:T(8,128)(2,1)S(1)} %copy-done.14, bf16[2048,1024]{1,0:T(8,128)(2,1)S(1)} %copy-done.5), custom_call_target="tpu_custom_call" | custom-call | flops 4294 | tf_op jit(solution)/shard_map/hidden_down/pallas_call | solution.py:63
  154.1 1.8 collective-permute-done.19.refs_2_
  156.1 1.5 collective-permute-done.18.refs_2_
  157.8 1.7 collective-permute-start.20
  159.5 1.5 collective-permute-done.21.refs_3_
  161.3 1.9 collective-permute-start.23
  163.2 7.5 %collective-permute-done.20.refs_3_ = bf16[2,9,64,128]{3,2,1,0:T(8,128)(2,1)S(1)} collective-permute-done((bf16[2,9,64,128]{3,2,1,0:T(8,128)(2,1)S(1)}, bf16[2,9,64,128]{3,2,1,0:T(8,128)(2,1)S(1)}, u32[]{:S(2)}, u32[]{:S(2)}) %collective-permute-start.20) | collective-permute-done | bytes 294944 | tf_op jit(solution)/shard_map/ppermute | solution.py:742
  170.7 1.8 collective-permute-start.22
  172.9 2.9 %collective-permute-start.25 = (bf16[1,9,64,128]{3,2,1,0:T(8,128)(2,1)S(1)}, bf16[1,9,64,128]{3,2,1,0:T(8,128)(2,1)S(1)}, u32[]{:S(2)}, u32[]{:S(2)}) collective-permute-start(bf16[1,9,64,128]{3,2,1,0:T(8,128)(2,1)S(1)} %next_send.21), channel_id=1, source_target_pairs={{0,16},{1,9},{2,18},{3,11},{4,20},{5,13},{6,22},{7,15},{8,24},{9,1... | collective-permute-start | bytes 442376 | tf_op jit(solution)/shard_map/ppermute | solution.py:742
  175.8 1.9 block_output.1
  178.2 1.1 hidden_grads_out.2
  179.4 1.6 collective-permute-start.24
  181.0 3.5 %collective-permute-done.26.refs_4_ = bf16[1,18,64,128]{3,2,1,0:T(8,128)(2,1)S(1)} collective-permute-done((bf16[1,18,64,128]{3,2,1,0:T(8,128)(2,1)S(1)}, bf16[1,18,64,128]{3,2,1,0:T(8,128)(2,1)S(1)}, u32[]{:S(2)}, u32[]{:S(2)}) %collective-permute-start.26) | collective-permute-done | bytes 294944 | tf_op jit(solution)/shard_map/ppermute | solution.py:742
  184.5 1.4 hidden_grads_out.3
  185.9 1.8 collective-permute-done.25.refs_4_
  187.7 0.8 head_grads_out.2
  188.4 2.0 %collective-permute-done.24.refs_4_ = bf16[1,8,64,128]{3,2,1,0:T(8,128)(2,1)S(1)} collective-permute-done((bf16[1,8,64,128]{3,2,1,0:T(8,128)(2,1)S(1)}, bf16[1,8,64,128]{3,2,1,0:T(8,128)(2,1)S(1)}, u32[]{:S(2)}, u32[]{:S(2)}) %collective-permute-start.24) | collective-permute-done | bytes 131104 | tf_op jit(solution)/shard_map/ppermute | solution.py:742
  190.5 0.7 head_grads_out.3
  (106 shorter events, 6.8 us)
Async XLA Ops:
  0.6 12.8 %copy-start.30 = (bf16[1024]{0:T(1024)(128)(2,1)S(1)}, bf16[1024]{0:T(1024)(128)(2,1)}, u32[]{:S(2)}) copy-start(bf16[1024]{0:T(1024)(128)(2,1)} %gain_ref.13) | copy-start | bytes 6148
  0.7 12.8 %copy-start.32 = (s32[2]{0:T(128)S(1)}, s32[2]{0:T(128)}, u32[]{:S(2)}) copy-start(s32[2]{0:T(128)} %lengths_ref.1) | copy-start | bytes 28
  0.7 19.0 %copy-start.3 = (bf16[1024,1024]{1,0:T(8,128)(2,1)S(1)}, bf16[1024,1024]{1,0:T(8,128)(2,1)}, u32[]{:S(2)}) copy-start(bf16[1024,1024]{1,0:T(8,128)(2,1)} %x_ref.9) | copy-start | bytes 6291460
  12.9 6.7 %collective-permute-start = (bf16[1024,1024]{1,0:T(8,128)(2,1)}, bf16[1024,1024]{1,0:T(8,128)(2,1)}, u32[]{:S(2)}, u32[]{:S(2)}) collective-permute-start(bf16[1024,1024]{1,0:T(8,128)(2,1)} %get-tuple-element.120.own_ref), channel_id=1, source_target_pairs={{0,1},{1,0},{2,3},{3,2},{4,5},{5,4},{6,7},{7,6},{8,9},{9,8},{10,11... | collective-permute-start | bytes 6291464 | tf_op jit(solution)/shard_map/ppermute | solution.py:734
  13.5 6.2 %copy-start.31 = (bf16[1024]{0:T(1024)(128)(2,1)S(1)}, bf16[1024]{0:T(1024)(128)(2,1)}, u32[]{:S(2)}) copy-start(bf16[1024]{0:T(1024)(128)(2,1)} %gain_ref.11) | copy-start | bytes 6148
  13.5 12.7 %copy-start.1 = (bf16[1024,2048]{1,0:T(8,128)(2,1)S(1)}, bf16[1024,2048]{1,0:T(8,128)(2,1)}, u32[]{:S(2)}) copy-start(bf16[1024,2048]{1,0:T(8,128)(2,1)} %wu_ref.3) | copy-start | bytes 12582916
  19.7 30.1 %copy-start.6 = (bf16[1024,1024]{1,0:T(8,128)(2,1)}, bf16[1024,1024]{1,0:T(8,128)(2,1)S(1)}, u32[]{:S(2)}) copy-start(bf16[1024,1024]{1,0:T(8,128)(2,1)S(1)} %get-tuple-element.128.refs_2_.seed_ref) | copy-start | bytes 6291460
  19.7 6.5 %copy-start = (bf16[1024,2048]{1,0:T(8,128)(2,1)S(1)}, bf16[1024,2048]{1,0:T(8,128)(2,1)}, u32[]{:S(2)}) copy-start(bf16[1024,2048]{1,0:T(8,128)(2,1)} %wg_ref.3) | copy-start | bytes 12582916
  47.2 46.4 %collective-permute-start.5 = (bf16[8,30,64,128]{3,2,1,0:T(8,128)(2,1)}, bf16[8,30,64,128]{3,2,1,0:T(8,128)(2,1)S(1)}, u32[]{:S(2)}, u32[]{:S(2)}) collective-permute-start(bf16[8,30,64,128]{3,2,1,0:T(8,128)(2,1)} %get-tuple-element.130), channel_id=1, source_target_pairs={{0,2},{1,5},{2,0},{3,7},{4,6},{5,1},{6,4},{7,3},{8,10},{9,13},{10,... | collective-permute-start | bytes 11796488 | tf_op jit(solution)/shard_map/ppermute | solution.py:742
  63.3 54.3 %collective-permute-start.8 = (bf16[8,18,64,128]{3,2,1,0:T(8,128)(2,1)}, bf16[8,18,64,128]{3,2,1,0:T(8,128)(2,1)S(1)}, u32[]{:S(2)}, u32[]{:S(2)}) collective-permute-start(bf16[8,18,64,128]{3,2,1,0:T(8,128)(2,1)} %get-tuple-element.141), channel_id=1, source_target_pairs={{0,8},{1,17},{2,10},{3,19},{4,12},{5,21},{6,14},{7,23},{8,0},{9,25... | collective-permute-start | bytes 7077896 | tf_op jit(solution)/shard_map/ppermute | solution.py:742
  70.1 7.1 %collective-permute-start.3 = (bf16[256,1024]{1,0:T(8,128)(2,1)S(1)}, bf16[256,1024]{1,0:T(8,128)(2,1)S(1)}, u32[]{:S(2)}, u32[]{:S(2)}) collective-permute-start(bf16[256,1024]{1,0:T(8,128)(2,1)S(1)} %get-tuple-element.149.refs_0_), channel_id=1, source_target_pairs={{0,1},{1,0},{2,3},{3,2},{4,5},{5,4},{6,7},{7,6},{8,9},{9,8},{10,11... | collective-permute-start | bytes 1572872 | tf_op jit(solution)/shard_map/ppermute | solution.py:734
  71.1 6.1 %copy-start.7 = (bf16[1024,1024]{1,0:T(8,128)(2,1)S(1)}, bf16[1024,1024]{1,0:T(8,128)(2,1)}, u32[]{:S(2)}) copy-start(bf16[1024,1024]{1,0:T(8,128)(2,1)} %copy-done.6) | copy-start | bytes 6291460
  71.1 6.1 %copy-start.9 = (bf16[1024,1024]{1,0:T(8,128)(2,1)S(1)}, bf16[1024,1024]{1,0:T(8,128)(2,1)}, u32[]{:S(2)}) copy-start(bf16[1024,1024]{1,0:T(8,128)(2,1)} %get-tuple-element.124.mid_ref) | copy-start | bytes 6291460
  71.1 6.1 %copy-start.18 = (bf16[512,1024]{1,0:T(8,128)(2,1)S(1)}, bf16[512,1024]{1,0:T(8,128)(2,1)}, u32[]{:S(2)}) copy-start(bf16[512,1024]{1,0:T(8,128)(2,1)} %wo_ref.5) | copy-start | bytes 3145732
  71.1 6.1 %collective-permute-start.4 = (bf16[256,1024]{1,0:T(8,128)(2,1)S(1)}, bf16[256,1024]{1,0:T(8,128)(2,1)S(1)}, u32[]{:S(2)}, u32[]{:S(2)}) collective-permute-start(bf16[256,1024]{1,0:T(8,128)(2,1)S(1)} %get-tuple-element.150.refs_1_), channel_id=1, source_target_pairs={{0,1},{1,0},{2,3},{3,2},{4,5},{5,4},{6,7},{7,6},{8,9},{9,8},{10,11... | collective-permute-start | bytes 1572872 | tf_op jit(solution)/shard_map/ppermute | solution.py:734
  76.7 4.3 %collective-permute-start.1 = (bf16[256,1024]{1,0:T(8,128)(2,1)S(1)}, bf16[256,1024]{1,0:T(8,128)(2,1)S(1)}, u32[]{:S(2)}, u32[]{:S(2)}) collective-permute-start(bf16[256,1024]{1,0:T(8,128)(2,1)S(1)} %get-tuple-element.154.refs_0_), channel_id=1, source_target_pairs={{0,1},{1,0},{2,3},{3,2},{4,5},{5,4},{6,7},{7,6},{8,9},{9,8},{10,11... | collective-permute-start | bytes 1572872 | tf_op jit(solution)/shard_map/ppermute | solution.py:734
  77.2 3.8 %collective-permute-start.2 = (bf16[256,1024]{1,0:T(8,128)(2,1)S(1)}, bf16[256,1024]{1,0:T(8,128)(2,1)S(1)}, u32[]{:S(2)}, u32[]{:S(2)}) collective-permute-start(bf16[256,1024]{1,0:T(8,128)(2,1)S(1)} %get-tuple-element.155.refs_1_), channel_id=1, source_target_pairs={{0,1},{1,0},{2,3},{3,2},{4,5},{5,4},{6,7},{7,6},{8,9},{9,8},{10,11... | collective-permute-start | bytes 1572872 | tf_op jit(solution)/shard_map/ppermute | solution.py:734
  81.0 4.3 %copy-start.26 = (bf16[1024,512]{1,0:T(8,128)(2,1)S(1)}, bf16[1024,512]{1,0:T(8,128)(2,1)}, u32[]{:S(2)}) copy-start(bf16[1024,512]{1,0:T(8,128)(2,1)} %get-tuple-element.138.v_ref) | copy-start | bytes 3145732
  85.3 8.3 %copy-start.2 = (bf16[8,30,64,128]{3,2,1,0:T(8,128)(2,1)S(1)}, bf16[8,30,64,128]{3,2,1,0:T(8,128)(2,1)}, u32[]{:S(2)}) copy-start(bf16[8,30,64,128]{3,2,1,0:T(8,128)(2,1)} %get-tuple-element.161.refs_0_) | copy-start | bytes 11796484
  93.6 4.1 %copy-start.22 = (bf16[1024,1024]{1,0:T(8,128)(2,1)S(1)}, bf16[1024,1024]{1,0:T(8,128)(2,1)}, u32[]{:S(2)}) copy-start(bf16[1024,1024]{1,0:T(8,128)(2,1)} %get-tuple-element.139.p_ref) | copy-start | bytes 6291460
  95.2 32.0 %collective-permute-start.14 = (bf16[4,30,64,128]{3,2,1,0:T(8,128)(2,1)}, bf16[4,30,64,128]{3,2,1,0:T(8,128)(2,1)S(1)}, u32[]{:S(2)}, u32[]{:S(2)}) collective-permute-start(bf16[4,30,64,128]{3,2,1,0:T(8,128)(2,1)} %next_send.12), channel_id=1, source_target_pairs={{0,4},{1,3},{2,6},{3,1},{4,0},{5,7},{6,2},{7,5},{8,12},{9,11},{10,... | collective-permute-start | bytes 5898248 | tf_op jit(solution)/shard_map/ppermute | solution.py:742
  97.2 8.0 %collective-permute-start.9 = (bf16[256,1024]{1,0:T(8,128)(2,1)S(1)}, bf16[256,1024]{1,0:T(8,128)(2,1)S(1)}, u32[]{:S(2)}, u32[]{:S(2)}) collective-permute-start(bf16[256,1024]{1,0:T(8,128)(2,1)S(1)} %get-tuple-element.177.refs_0_), channel_id=1, source_target_pairs={{0,1},{1,0},{2,3},{3,2},{4,5},{5,4},{6,7},{7,6},{8,9},{9,8},{10,11... | collective-permute-start | bytes 1572872 | tf_op jit(solution)/shard_map/ppermute | solution.py:734
  97.2 12.2 %collective-permute-start.10 = (bf16[256,1024]{1,0:T(8,128)(2,1)S(1)}, bf16[256,1024]{1,0:T(8,128)(2,1)S(1)}, u32[]{:S(2)}, u32[]{:S(2)}) collective-permute-start(bf16[256,1024]{1,0:T(8,128)(2,1)S(1)} %get-tuple-element.178.refs_1_), channel_id=1, source_target_pairs={{0,1},{1,0},{2,3},{3,2},{4,5},{5,4},{6,7},{7,6},{8,9},{9,8},{10,11... | collective-permute-start | bytes 1572872 | tf_op jit(solution)/shard_map/ppermute | solution.py:734
  97.7 8.0 %copy-start.19 = (bf16[16,64,1024]{2,1,0:T(8,128)(2,1)S(1)}, bf16[16,64,1024]{2,1,0:T(8,128)(2,1)}, u32[]{:S(2)}) copy-start(bf16[16,64,1024]{2,1,0:T(8,128)(2,1)} %get-tuple-element.122.turned_ref.value_ref) | copy-start | bytes 6291460
  105.1 12.8 %collective-permute-start.6 = (bf16[256,1024]{1,0:T(8,128)(2,1)S(1)}, bf16[256,1024]{1,0:T(8,128)(2,1)S(1)}, u32[]{:S(2)}, u32[]{:S(2)}) collective-permute-start(bf16[256,1024]{1,0:T(8,128)(2,1)S(1)} %get-tuple-element.183.refs_0_), channel_id=1, source_target_pairs={{0,1},{1,0},{2,3},{3,2},{4,5},{5,4},{6,7},{7,6},{8,9},{9,8},{10,11... | collective-permute-start | bytes 1572872 | tf_op jit(solution)/shard_map/ppermute | solution.py:734
  105.2 12.7 %collective-permute-start.7 = (bf16[256,1024]{1,0:T(8,128)(2,1)S(1)}, bf16[256,1024]{1,0:T(8,128)(2,1)S(1)}, u32[]{:S(2)}, u32[]{:S(2)}) collective-permute-start(bf16[256,1024]{1,0:T(8,128)(2,1)S(1)} %get-tuple-element.184.refs_1_), channel_id=1, source_target_pairs={{0,1},{1,0},{2,3},{3,2},{4,5},{5,4},{6,7},{7,6},{8,9},{9,8},{10,11... | collective-permute-start | bytes 1572872 | tf_op jit(solution)/shard_map/ppermute | solution.py:734
  105.7 5.3 %copy-start.28 = (bf16[512,1024]{1,0:T(8,128)(2,1)S(1)}, bf16[512,1024]{1,0:T(8,128)(2,1)}, u32[]{:S(2)}) copy-start(bf16[512,1024]{1,0:T(8,128)(2,1)} %get-tuple-element.173.gm_ref) | copy-start | bytes 3145732
  109.4 30.6 %collective-permute-start.13 = (bf16[8,8,64,128]{3,2,1,0:T(8,128)(2,1)}, bf16[8,8,64,128]{3,2,1,0:T(8,128)(2,1)S(1)}, u32[]{:S(2)}, u32[]{:S(2)}) collective-permute-start(bf16[8,8,64,128]{3,2,1,0:T(8,128)(2,1)} %get-tuple-element.176), channel_id=1, source_target_pairs={{0,8},{1,17},{2,10},{3,19},{4,12},{5,21},{6,14},{7,23},{8,0},{9,25... | collective-permute-start | bytes 3145736 | tf_op jit(solution)/shard_map/ppermute | solution.py:742
  111.0 6.6 %copy-start.4 = (bf16[8,18,64,128]{3,2,1,0:T(8,128)(2,1)S(1)}, bf16[8,18,64,128]{3,2,1,0:T(8,128)(2,1)}, u32[]{:S(2)}) copy-start(bf16[8,18,64,128]{3,2,1,0:T(8,128)(2,1)} %get-tuple-element.172.refs_0_) | copy-start | bytes 7077892
  117.8 22.4 %collective-permute-start.12 = (bf16[4,18,64,128]{3,2,1,0:T(8,128)(2,1)S(1)}, bf16[4,18,64,128]{3,2,1,0:T(8,128)(2,1)S(1)}, u32[]{:S(2)}, u32[]{:S(2)}) collective-permute-start(bf16[4,18,64,128]{3,2,1,0:T(8,128)(2,1)S(1)} %next_send.13), channel_id=1, source_target_pairs={{0,2},{1,5},{2,0},{3,7},{4,6},{5,1},{6,4},{7,3},{8,10},{9,13},{10,... | collective-permute-start | bytes 3538952 | tf_op jit(solution)/shard_map/ppermute | solution.py:742
  126.0 14.0 %copy-start.13 = (bf16[8,8,64,128]{3,2,1,0:T(8,128)(2,1)S(1)}, bf16[8,8,64,128]{3,2,1,0:T(8,128)(2,1)}, u32[]{:S(2)}) copy-start(bf16[8,8,64,128]{3,2,1,0:T(8,128)(2,1)} %get-tuple-element.194.refs_0_) | copy-start | bytes 3145732
  126.0 20.7 %collective-permute-start.11 = (bf16[8,9,64,128]{3,2,1,0:T(8,128)(2,1)S(1)}, bf16[8,9,64,128]{3,2,1,0:T(8,128)(2,1)S(1)}, u32[]{:S(2)}, u32[]{:S(2)}) collective-permute-start(bf16[8,9,64,128]{3,2,1,0:T(8,128)(2,1)S(1)} %get-tuple-element.193), channel_id=1, source_target_pairs={{0,2},{1,5},{2,0},{3,7},{4,6},{5,1},{6,4},{7,3},{8,10},{9,13},{10,... | collective-permute-start | bytes 3538952 | tf_op jit(solution)/shard_map/ppermute | solution.py:742
  128.4 32.6 %collective-permute-start.21 = (bf16[2,30,64,128]{3,2,1,0:T(8,128)(2,1)S(1)}, bf16[2,30,64,128]{3,2,1,0:T(8,128)(2,1)S(1)}, u32[]{:S(2)}, u32[]{:S(2)}) collective-permute-start(bf16[2,30,64,128]{3,2,1,0:T(8,128)(2,1)S(1)} %next_send.14), channel_id=1, source_target_pairs={{0,8},{1,17},{2,10},{3,19},{4,12},{5,21},{6,14},{7,23},{8,0},{9,25... | collective-permute-start | bytes 2949128 | tf_op jit(solution)/shard_map/ppermute | solution.py:742
  140.0 7.7 %copy-start.14 = (bf16[1024,2048]{1,0:T(8,128)(2,1)S(1)}, bf16[1024,2048]{1,0:T(8,128)(2,1)}, u32[]{:S(2)}) copy-start(bf16[1024,2048]{1,0:T(8,128)(2,1)} %get-tuple-element.199.h_ref) | copy-start | bytes 12582916
  140.1 6.6 %copy-start.8 = (bf16[8,9,64,128]{3,2,1,0:T(8,128)(2,1)S(1)}, bf16[8,9,64,128]{3,2,1,0:T(8,128)(2,1)}, u32[]{:S(2)}) copy-start(bf16[8,9,64,128]{3,2,1,0:T(8,128)(2,1)} %get-tuple-element.192.refs_0_) | copy-start | bytes 3538948
  140.2 15.8 %collective-permute-start.19 = (bf16[4,8,64,128]{3,2,1,0:T(8,128)(2,1)S(1)}, bf16[4,8,64,128]{3,2,1,0:T(8,128)(2,1)S(1)}, u32[]{:S(2)}, u32[]{:S(2)}) collective-permute-start(bf16[4,8,64,128]{3,2,1,0:T(8,128)(2,1)S(1)} %next_send.15), channel_id=1, source_target_pairs={{0,2},{1,5},{2,0},{3,7},{4,6},{5,1},{6,4},{7,3},{8,10},{9,13},{10,... | collective-permute-start | bytes 1572872 | tf_op jit(solution)/shard_map/ppermute | solution.py:742
  140.2 7.5 %copy-start.5 = (bf16[2048,1024]{1,0:T(8,128)(2,1)S(1)}, bf16[2048,1024]{1,0:T(8,128)(2,1)}, u32[]{:S(2)}) copy-start(bf16[2048,1024]{1,0:T(8,128)(2,1)} %wd_ref.1) | copy-start | bytes 12582916
  146.9 10.8 %collective-permute-start.18 = (bf16[4,9,64,128]{3,2,1,0:T(8,128)(2,1)S(1)}, bf16[4,9,64,128]{3,2,1,0:T(8,128)(2,1)S(1)}, u32[]{:S(2)}, u32[]{:S(2)}) collective-permute-start(bf16[4,9,64,128]{3,2,1,0:T(8,128)(2,1)S(1)} %next_send.17), channel_id=1, source_target_pairs={{0,4},{1,3},{2,6},{3,1},{4,0},{5,7},{6,2},{7,5},{8,12},{9,11},{10,... | collective-permute-start | bytes 1769480 | tf_op jit(solution)/shard_map/ppermute | solution.py:742
  153.6 19.3 %collective-permute-start.15 = (bf16[512,1024]{1,0:T(8,128)(2,1)S(1)}, bf16[512,1024]{1,0:T(8,128)(2,1)S(1)}, u32[]{:S(2)}, u32[]{:S(2)}) collective-permute-start(bf16[512,1024]{1,0:T(8,128)(2,1)S(1)} %get-tuple-element.207.refs_0_), channel_id=1, source_target_pairs={{0,1},{1,0},{2,3},{3,2},{4,5},{5,4},{6,7},{7,6},{8,9},{9,8},{10,11... | collective-permute-start | bytes 3145736 | tf_op jit(solution)/shard_map/ppermute | solution.py:734
  153.6 22.1 %collective-permute-start.16 = (bf16[512,1024]{1,0:T(8,128)(2,1)S(1)}, bf16[512,1024]{1,0:T(8,128)(2,1)S(1)}, u32[]{:S(2)}, u32[]{:S(2)}) collective-permute-start(bf16[512,1024]{1,0:T(8,128)(2,1)S(1)} %get-tuple-element.208.refs_1_), channel_id=1, source_target_pairs={{0,1},{1,0},{2,3},{3,2},{4,5},{5,4},{6,7},{7,6},{8,9},{9,8},{10,11... | collective-permute-start | bytes 3145736 | tf_op jit(solution)/shard_map/ppermute | solution.py:734
  156.0 16.6 %collective-permute-start.17 = (bf16[2,18,64,128]{3,2,1,0:T(8,128)(2,1)S(1)}, bf16[2,18,64,128]{3,2,1,0:T(8,128)(2,1)S(1)}, u32[]{:S(2)}, u32[]{:S(2)}) collective-permute-start(bf16[2,18,64,128]{3,2,1,0:T(8,128)(2,1)S(1)} %next_send.16), channel_id=1, source_target_pairs={{0,4},{1,3},{2,6},{3,1},{4,0},{5,7},{6,2},{7,5},{8,12},{9,11},{10,... | collective-permute-start | bytes 1769480 | tf_op jit(solution)/shard_map/ppermute | solution.py:742
  156.1 5.0 %copy-start.12 = (bf16[4,30,64,128]{3,2,1,0:T(8,128)(2,1)S(1)}, bf16[4,30,64,128]{3,2,1,0:T(8,128)(2,1)}, u32[]{:S(2)}) copy-start(bf16[4,30,64,128]{3,2,1,0:T(8,128)(2,1)} %copy-done.11) | copy-start | bytes 5898244
  157.8 12.9 %collective-permute-start.20 = (bf16[2,9,64,128]{3,2,1,0:T(8,128)(2,1)S(1)}, bf16[2,9,64,128]{3,2,1,0:T(8,128)(2,1)S(1)}, u32[]{:S(2)}, u32[]{:S(2)}) collective-permute-start(bf16[2,9,64,128]{3,2,1,0:T(8,128)(2,1)S(1)} %next_send.19), channel_id=1, source_target_pairs={{0,8},{1,17},{2,10},{3,19},{4,12},{5,21},{6,14},{7,23},{8,0},{9,25... | collective-permute-start | bytes 884744 | tf_op jit(solution)/shard_map/ppermute | solution.py:742
  161.3 16.9 %collective-permute-start.23 = (bf16[1,30,64,128]{3,2,1,0:T(8,128)(2,1)S(1)}, bf16[1,30,64,128]{3,2,1,0:T(8,128)(2,1)S(1)}, u32[]{:S(2)}, u32[]{:S(2)}) collective-permute-start(bf16[1,30,64,128]{3,2,1,0:T(8,128)(2,1)S(1)} %next_send.20), channel_id=1, source_target_pairs={{0,16},{1,9},{2,18},{3,11},{4,20},{5,13},{6,22},{7,15},{8,24},{9,1... | collective-permute-start | bytes 1474568 | tf_op jit(solution)/shard_map/ppermute | solution.py:742
  170.7 8.6 %collective-permute-start.22 = (bf16[2,8,64,128]{3,2,1,0:T(8,128)(2,1)S(1)}, bf16[2,8,64,128]{3,2,1,0:T(8,128)(2,1)S(1)}, u32[]{:S(2)}, u32[]{:S(2)}) collective-permute-start(bf16[2,8,64,128]{3,2,1,0:T(8,128)(2,1)S(1)} %next_send.18), channel_id=1, source_target_pairs={{0,4},{1,3},{2,6},{3,1},{4,0},{5,7},{6,2},{7,5},{8,12},{9,11},{10,... | collective-permute-start | bytes 786440 | tf_op jit(solution)/shard_map/ppermute | solution.py:742
  172.8 11.7 %collective-permute-start.26 = (bf16[1,18,64,128]{3,2,1,0:T(8,128)(2,1)S(1)}, bf16[1,18,64,128]{3,2,1,0:T(8,128)(2,1)S(1)}, u32[]{:S(2)}, u32[]{:S(2)}) collective-permute-start(bf16[1,18,64,128]{3,2,1,0:T(8,128)(2,1)S(1)} %next_send.22), channel_id=1, source_target_pairs={{0,16},{1,9},{2,18},{3,11},{4,20},{5,13},{6,22},{7,15},{8,24},{9,1... | collective-permute-start | bytes 884744 | tf_op jit(solution)/shard_map/ppermute | solution.py:742
  172.9 14.8 %collective-permute-start.25 = (bf16[1,9,64,128]{3,2,1,0:T(8,128)(2,1)S(1)}, bf16[1,9,64,128]{3,2,1,0:T(8,128)(2,1)S(1)}, u32[]{:S(2)}, u32[]{:S(2)}) collective-permute-start(bf16[1,9,64,128]{3,2,1,0:T(8,128)(2,1)S(1)} %next_send.21), channel_id=1, source_target_pairs={{0,16},{1,9},{2,18},{3,11},{4,20},{5,13},{6,22},{7,15},{8,24},{9,1... | collective-permute-start | bytes 442376 | tf_op jit(solution)/shard_map/ppermute | solution.py:742
  179.4 11.1 %collective-permute-start.24 = (bf16[1,8,64,128]{3,2,1,0:T(8,128)(2,1)S(1)}, bf16[1,8,64,128]{3,2,1,0:T(8,128)(2,1)S(1)}, u32[]{:S(2)}, u32[]{:S(2)}) collective-permute-start(bf16[1,8,64,128]{3,2,1,0:T(8,128)(2,1)S(1)} %next_send.23), channel_id=1, source_target_pairs={{0,16},{1,9},{2,18},{3,11},{4,20},{5,13},{6,22},{7,15},{8,24},{9,1... | collective-permute-start | bytes 393224 | tf_op jit(solution)/shard_map/ppermute | solution.py:742
  (12 other events, 36.1 us)
